TPU v7x, 512 devices: a whole 4x4x16 slice. The times are simulated.
512 devices in a mesh: gx: 64 (over z_lo, x, core), yz: 8 (over y, z_hi).
Axes of the slice: x: 4, y: 4, z: 16 (z_hi: 2, z_lo: 8; z = z_hi * 8 + z_lo), core: 2. Of those that a mesh axis runs over, the one named last changes fastest.
Arguments:
- solution: float32 [4, 512, 64, 3, 128], P(None, 'gx', 'yz'), may hold values from -6 to 6
- residual: float32 [4, 512, 64, 3, 128], P(None, 'gx', 'yz'), may hold values from -6 to 6
- direction: float32 [4, 512, 64, 3, 128], P(None, 'gx', 'yz'), may hold values from -6 to 6
- stiffness: float32 [512, 64, 128], P('gx', 'yz'), may hold values from 0.5 to 13.52
- coupling: float32 [512, 64, 128], P('gx', 'yz'), may hold values from 0.5 to 2
- lower_factor: float32 [64, 8, 384, 384], P('gx', 'yz'), may hold values from -0.122474487 to 1
- upper_factor: float32 [64, 8, 384, 384], P('gx', 'yz'), may hold values from -0.122474487 to 2, as said below
- pivot_order: int32 [64, 8, 384], P('gx', 'yz'), may hold values from 0 to 383, each once within a row
- coarse_basis: float32 [4, 512, 64, 128], P(None, 'gx', 'yz'), may hold values from 0.2 to 1
- coarse_inverse: float32 [64, 8, 12, 6144], P('gx', 'yz'), may hold values from -0.00024917498 to 0.009765625
- inner_prior: float32 [4], replicated, may hold values from 6291456 to 25165824
Outputs:
- solution_next: float32 [4, 512, 64, 3, 128], P(None, 'gx', 'yz')
- residual_next: float32 [4, 512, 64, 3, 128], P(None, 'gx', 'yz')
- direction_next: float32 [4, 512, 64, 3, 128], P(None, 'gx', 'yz')
- inner_next: float32 [4], replicated
Inputs may be any that keep to these rules, and one draw needn't show every extreme that they name: `upper_factor`: upper triangular with positive diagonal.
All inputs are finite; a program needn't handle non-finite values.
Results may differ from a plain program's by a relative error of at most 0.000067.
Values sent between devices are 32-bit elements; how exact they have to be, the bound alone decides.
No kernel may reach another device: no remote copies, remote signals or barrier semaphores. Data moves between devices by JAX's collectives and lax.ppermute only.
A program may use at most 64 MiB of HBM per device.

v0:
```python
import jax
import jax.numpy as jnp
from jax import lax
from jax.sharding import PartitionSpec as P

precise = lax.Precision.HIGHEST


def with_halo(cells, sides, width):
    for axis, dim in sides:
        count = lax.axis_size(axis)
        ends = count - 1
        head = lax.slice_in_dim(cells, 0, width, axis=dim)
        tail = lax.slice_in_dim(cells, cells.shape[dim] - width, cells.shape[dim], axis=dim)
        cells = jnp.concatenate(
            [
                lax.ppermute(tail, axis, [(i, (i + 1) % count) for i in range(ends)]),
                cells,
                lax.ppermute(head, axis, [((i + 1) % count, i) for i in range(ends)]),
            ],
            axis=dim,
        )
    return cells


def stencil(padded, scaled):
    zero_plane = jnp.zeros_like(scaled[..., :1])
    upward = jnp.concatenate([scaled[..., 1:], zero_plane], axis=4)
    downward = jnp.concatenate([zero_plane, scaled[..., :-1]], axis=4)
    beside = padded[:, 2:, 1:-1] + padded[:, :-2, 1:-1] + padded[:, 1:-1, 2:] + padded[:, 1:-1, :-2]
    return 6.0 * scaled - beside - upward - downward


def operate(direction, stiffness, coupling):
    scaled = stiffness[None, :, :, None, :] * direction
    padded = with_halo(scaled, (("gx", 1), ("yz", 2)), 1)
    return stiffness[None, :, :, None, :] * stencil(padded, scaled) + coupling[
        None, :, :, None, :
    ] * jnp.sum(direction, axis=3, keepdims=True)


def local_solve(field, lower_factor, upper_factor, pivot_order):
    line_width = lower_factor.shape[-1]
    line_rows = field.reshape(-1, line_width)
    pivots = pivot_order.reshape(line_width)
    inverse_order = jnp.argsort(pivots)
    permuted = jnp.take(line_rows, pivots, axis=1)
    middle = jnp.dot(
        permuted, lower_factor[0, 0].T, precision=precise, preferred_element_type=jnp.float32
    )
    solved = jnp.dot(
        middle, upper_factor[0, 0].T, precision=precise, preferred_element_type=jnp.float32
    )
    return jnp.take(solved, inverse_order, axis=1).reshape(field.shape)


def across(padded, field):
    field_shape = field.shape
    blank_rows = jnp.zeros(field_shape[:1] + (field_shape[1] - 2,) + field_shape[2:], field.dtype)
    across_first = jnp.concatenate([padded[:, :1, 1:-1], blank_rows, padded[:, -1:, 1:-1]], axis=1)
    blank_cols = jnp.zeros(field_shape[:2] + (field_shape[2] - 2,) + field_shape[3:], field.dtype)
    across_second = jnp.concatenate([padded[:, 1:-1, :1], blank_cols, padded[:, 1:-1, -1:]], axis=2)
    return field + 0.5 * (across_first + across_second)


def restrict(coarse_basis, field):
    weighted = jnp.einsum("pxyz,cxykz->ckp", coarse_basis, field, precision=precise)
    return weighted.reshape(field.shape[0], -1)


def prolong(coarse_basis, coarse_values, field_shape):
    shaped = coarse_values.reshape(field_shape[0], field_shape[3], coarse_basis.shape[0])
    return jnp.einsum("pxyz,ckp->cxykz", coarse_basis, shaped, precision=precise)


def per_device(
    solution,
    residual,
    direction,
    stiffness,
    coupling,
    lower_factor,
    upper_factor,
    pivot_order,
    coarse_basis,
    coarse_inverse,
    inner_prior,
):
    case_count = residual.shape[0]
    applied = operate(direction, stiffness, coupling)
    curve_part = jnp.sum(direction * applied, axis=(1, 2, 3, 4))
    curvature = lax.psum(curve_part, ("gx", "yz"))
    step_size = inner_prior / curvature
    step_field = step_size[:, None, None, None, None]
    residual_next = residual - step_field * applied
    primal = restrict(coarse_basis, residual_next)
    primal_all = lax.all_gather(primal[:, None, :], ("gx", "yz"), axis=1, tiled=True).reshape(
        case_count, -1
    )
    coarse_values = jnp.dot(
        primal_all, coarse_inverse[0, 0].T, precision=precise, preferred_element_type=jnp.float32
    )
    correction = prolong(coarse_basis, coarse_values, residual.shape)
    local_part = local_solve(residual_next, lower_factor, upper_factor, pivot_order)
    padded = with_halo(local_part, (("gx", 1), ("yz", 2)), 1)
    smoothed = across(padded, local_part)
    preconditioned = smoothed + correction
    inner_part = jnp.sum(residual_next * preconditioned, axis=(1, 2, 3, 4))
    inner_next = lax.psum(inner_part, ("gx", "yz"))
    growth = (inner_next / inner_prior)[:, None, None, None, None]
    direction_next = preconditioned + growth * direction
    solution_next = solution + step_field * direction
    return (solution_next, residual_next, direction_next, inner_next)


def solution(mesh):
    in_specs = (
        P(None, "gx", "yz", None, None),
        P(None, "gx", "yz", None, None),
        P(None, "gx", "yz", None, None),
        P("gx", "yz", None),
        P("gx", "yz", None),
        P("gx", "yz", None, None),
        P("gx", "yz", None, None),
        P("gx", "yz", None),
        P(None, "gx", "yz", None),
        P("gx", "yz", None, None),
        P(),
    )
    out_specs = (
        P(None, "gx", "yz", None, None),
        P(None, "gx", "yz", None, None),
        P(None, "gx", "yz", None, None),
        P(),
    )
    return jax.shard_map(
        per_device, mesh=mesh, in_specs=in_specs, out_specs=out_specs, check_vma=False
    )
```

profile of v0, /device:TPU:1, one launch (start us, length us, event | category | flops | bytes accessed | tf_op | source)
XLA Modules:
  0.0 2391.1 jit_solution(16158936149588700655)
XLA Ops:
  0.6 0.0 copy-start
  0.6 1.3 copy_multiply_fusion
  2.0 8.7 collective-permute-start
  10.8 0.0 copy-start.10
  10.8 0.0 copy-start.1
  10.8 2.1 collective-permute-start.1
  12.8 0.3 fusion.30
  13.1 0.0 copy-done.10
  13.2 0.0 copy-done.1
  13.2 0.0 copy-start.9
  13.2 0.0 copy-start.6
  13.2 3.8 sort.17
  17.0 0.0 copy-done.9
  17.1 0.1 copy.50
  17.1 0.0 copy-done.6
  17.2 0.7 reduce.1
  17.9 0.1 dot_general.20
  18.0 0.1 pad.6.clone
  18.0 0.0 collective-permute-done
  18.1 0.0 collective-permute-done.1
  18.1 11.2 collective-permute-start.3
  29.3 1.3 collective-permute-start.2
  30.6 3.7 collective-permute-done.3
  34.3 10.0 collective-permute-done.2
  44.3 0.0 copy-done.7
  44.3 0.7 multiply_reduce_fusion.1
  45.0 103.4 %psum.14 = f32[4]{0:T(128)S(1)} all-reduce(f32[4]{0:T(128)S(1)} %get-tuple-element.19), channel_id=1, replica_groups=mesh['gx'=64,'yz'=8] {'gx','yz'}, use_global_device_ids=true, to_apply=%region_2.0 | all-reduce | flops 4 | bytes 32 | tf_op jit(solution)/shard_map/psum | solution.py:92
  148.5 0.0 copy-done.11
  148.5 0.0 copy-done.5
  148.5 0.3 copy_subtract_fusion
  148.8 0.0 copy-start.8
  148.9 0.0 copy-start.2
  148.9 0.8 copy-done.8
  149.7 1.6 convolution_bitcast_fusion.1
  151.3 0.1 broadcast_in_dim_reshape.3
  151.4 0.2 copy.56
  151.6 0.0 copy-done.2
  151.6 1.7 gather_fusion
  153.3 0.0 copy-start.3
  153.3 1.5 fusion.2
  154.8 0.8 fusion
  155.6 1.7 gather_fusion.1
  157.3 0.1 select_bitcast_fusion
  157.4 0.2 copy.58
  157.6 2.6 collective-permute-start.4
  160.2 2047.1 %all_gather.3 = f32[4,512,12]{2,0,1:T(4,128)S(1)} all-gather(f32[4,1,12]{2,0,1:T(4,128)S(1)} %broadcast_in_dim_reshape.3), channel_id=1, replica_groups=mesh['gx'=64,'yz'=8] {'gx','yz'}, dimensions={1}, use_global_device_ids=true | all-gather | bytes 98496 | tf_op jit(solution)/shard_map/all_gather | solution.py:97
  2207.3 0.1 copy.66
  2207.4 0.7 reshape.66
  2208.1 1.9 collective-permute-start.5
  2210.0 0.0 collective-permute-done.4
  2210.1 0.3 constant_dynamic-update-slice_fusion.1
  2210.4 15.4 collective-permute-done.5
  2225.8 1.3 collective-permute-start.7
  2227.1 12.9 collective-permute-start.6
  2240.0 3.3 convolution_bitcast_fusion.2
  2243.2 0.0 collective-permute-done.7
  2243.3 0.0 collective-permute-done.6
  2243.3 0.0 copy-start.4
  2243.3 1.0 multiply_reduce_fusion
  2244.3 144.2 %psum.15 = f32[4]{0:T(128)S(1)} all-reduce(f32[4]{0:T(128)S(1)} %get-tuple-element.33), channel_id=1, replica_groups=mesh['gx'=64,'yz'=8] {'gx','yz'}, use_global_device_ids=true, to_apply=%region_5.7 | all-reduce | flops 4 | bytes 32 | tf_op jit(solution)/shard_map/psum | solution.py:109
  2388.5 0.5 copy-done.12
  2389.0 0.6 multiply_add_fusion
  2389.6 0.8 copy.69
  2390.4 0.8 copy.71
  (31 shorter events, 0.3 us)
Async XLA Ops:
  0.6 152.6 %copy-start = (f32[1,1,384,384]{3,2,1,0:T(8,128)S(1)}, f32[1,1,384,384]{3,2,1,0:T(8,128)}, u32[]{:S(2)}) copy-start(f32[1,1,384,384]{3,2,1,0:T(8,128)} %param.18) | copy-start | bytes 1769476
  2.0 16.1 collective-permute-start
  10.8 2.4 copy-start.10
  10.8 2.4 copy-start.1
  10.8 7.3 collective-permute-start.1
  13.2 3.8 copy-start.9
  13.2 3.9 copy-start.6
  18.1 26.2 %copy-start.7 = (f32[8,8,128]{2,1,0:T(8,128)S(1)}, f32[8,8,128]{2,1,0:T(8,128)}, u32[]{:S(2)}) copy-start(f32[8,8,128]{2,1,0:T(8,128)} %param.16) | copy-start | bytes 98308
  18.1 16.2 collective-permute-start.3
  29.3 15.0 collective-permute-start.2
  44.3 104.2 %copy-start.5 = (f32[4,8,8,3,128]{4,2,3,1,0:T(8,128)S(1)}, f32[4,8,8,3,128]{4,2,3,1,0:T(8,128)}, u32[]{:S(2)}) copy-start(f32[4,8,8,3,128]{4,2,3,1,0:T(8,128)} %param.14) | copy-start | bytes 1179652
  45.0 103.5 %copy-start.11 = (f32[4]{0:T(128)S(1)}, f32[4]{0:T(128)}, u32[]{:S(2)}) copy-start(f32[4]{0:T(128)} %param.23) | copy-start | bytes 52
  148.8 0.9 copy-start.8
  148.9 2.7 copy-start.2
  153.3 1.5 copy-start.3
  157.6 2052.4 %collective-permute-start.4 = (f32[4,1,8,3,128]{4,0,2,1,3:T(4,128)S(1)}, f32[4,1,8,3,128]{4,0,2,1,3:T(4,128)S(1)}, u32[]{:S(2)}, u32[]{:S(2)}) collective-permute-start(f32[4,1,8,3,128]{4,0,2,1,3:T(4,128)S(1)} %copy.96), channel_id=1, source_target_pairs={{0,8},{8,16},{16,24},{24,32},{32,40},{40,48},{48,56},{56,64},{64,7... | collective-permute-start | bytes 147464 | tf_op jit(solution)/shard_map/ppermute | solution.py:17
  2208.1 17.6 collective-permute-start.5
  2225.8 17.5 collective-permute-start.7
  2227.1 16.2 collective-permute-start.6
  2243.3 145.7 %copy-start.4 = (f32[4,8,8,3,128]{4,2,3,1,0:T(8,128)S(1)}, f32[4,8,8,3,128]{4,2,3,1,0:T(8,128)}, u32[]{:S(2)}) copy-start(f32[4,8,8,3,128]{4,2,3,1,0:T(8,128)} %param.13) | copy-start | bytes 1179652
  2388.5 0.5 copy-start.12
where the time goes:
time: 2390 us
  blocking collectives  2290 us (96%)
  starting transfers between devices  42 us (2%)
  waiting for transfers between devices  29.1 us (1%)
    all_gather x1, blocking collectives, per_device(): lax.all_gather(primal[:, None, :], ('gx', 'yz'), axis=1, tiled=True)  2050 us
    psum x1, blocking collectives, per_device(): inner_next = lax.psum(inner_part, ('gx', 'yz'))  144 us
    psum x1, blocking collectives, per_device(): curvature = lax.psum(curve_part, ('gx', 'yz'))  103 us
  transfers between devices with their start and end apart: 8, of which 3 were waited for; matrix products, arithmetic and copies ran while one was open for 0% of the time, Pallas kernels for 0%

commit v1 on v0

v1 whole, which is shorter than its diff:
```python
import jax
import jax.numpy as jnp
from jax import lax
from jax.sharding import Mesh, PartitionSpec as P

precise = lax.Precision.HIGHEST

DEPTH = ("zl", "zh")
PLANE = ("x", "c", "y")
GX_AXES = ("zl", "x", "c")
YZ_AXES = ("y", "zh")
SIZES = {"zl": 8, "x": 4, "c": 2, "y": 4, "zh": 2}
N_DEPTH = 16
N_PLANE = 32


def exchange(block, axes, count):
    spread = jnp.broadcast_to(block[None], (count,) + block.shape)
    return lax.all_to_all(spread, axes, 0, 0, tiled=True)


def gather_rows(row):
    line = exchange(row, DEPTH, N_DEPTH).reshape(N_DEPTH, 128)
    return exchange(line, PLANE, N_PLANE).reshape(N_PLANE * N_DEPTH, 128)


def total_rows(row):
    line = exchange(row, DEPTH, N_DEPTH)
    part = jnp.sum(line, axis=0)
    return jnp.sum(exchange(part, PLANE, N_PLANE), axis=0)


def faces(field):
    found = []
    for axes, dim in ((YZ_AXES, 2), (GX_AXES, 1)):
        count = 1
        for name in axes:
            count *= SIZES[name]
        up = [(i, i + 1) for i in range(count - 1)]
        down = [(i + 1, i) for i in range(count - 1)]
        last = field.shape[dim]
        head = lax.slice_in_dim(field, 0, 1, axis=dim)
        tail = lax.slice_in_dim(field, last - 1, last, axis=dim)
        found.append((lax.ppermute(tail, axes, up), lax.ppermute(head, axes, down)))
    return found[1] + found[0]


def beside(field, below, above, dim):
    size = field.shape[dim]
    lower = jnp.concatenate([below, lax.slice_in_dim(field, 0, size - 1, axis=dim)], axis=dim)
    upper = jnp.concatenate([lax.slice_in_dim(field, 1, size, axis=dim), above], axis=dim)
    return lower + upper


def edges(field, below, above, dim):
    shape = list(field.shape)
    shape[dim] -= 2
    return jnp.concatenate([below, jnp.zeros(shape, field.dtype), above], axis=dim)


def per_device(
    solution,
    residual,
    direction,
    stiffness,
    coupling,
    lower_factor,
    upper_factor,
    pivot_order,
    coarse_basis,
    coarse_inverse,
    inner_prior,
):
    cases = residual.shape[0]
    stiff = stiffness[None, :, :, None, :]
    scaled = stiff * direction
    halo = faces(scaled)

    pivots = pivot_order.reshape(-1)
    width = pivots.shape[0]
    chosen = (pivots[:, None] == jnp.arange(width)[None, :]).astype(jnp.float32)
    product = jnp.dot(upper_factor[0, 0], lower_factor[0, 0], precision=precise)
    inner = jnp.dot(product, chosen, precision=precise)
    operator = lax.dot_general(
        chosen, inner, (((0,), (0,)), ((), ())), precision=precise
    )

    def solve(field):
        rows = field.reshape(-1, width)
        return lax.dot_general(
            rows, operator, (((1,), (1,)), ((), ())), precision=precise
        ).reshape(field.shape)

    def restrict(field):
        return jnp.einsum("pxyz,cxykz->ckp", coarse_basis, field, precision=precise).reshape(-1)

    coarse_rows = (
        coarse_inverse.reshape(12, 8, 4, 2, 4, 2, 12)
        .transpose(2, 3, 4, 1, 5, 6, 0)
        .reshape(512, 144)
    )
    solved_r = solve(residual)
    primal_r = restrict(residual)

    zero = jnp.zeros_like(scaled[..., :1])
    upward = jnp.concatenate([scaled[..., 1:], zero], axis=4)
    downward = jnp.concatenate([zero, scaled[..., :-1]], axis=4)
    around = beside(scaled, halo[0], halo[1], 1) + beside(scaled, halo[2], halo[3], 2)
    applied = stiff * (6.0 * scaled - around - upward - downward) + coupling[
        None, :, :, None, :
    ] * jnp.sum(direction, axis=3, keepdims=True)
    curve_part = jnp.sum(direction * applied, axis=(1, 2, 3, 4))
    solved_w = solve(applied)
    primal_w = restrict(applied)
    outer = faces(jnp.concatenate([solved_r, solved_w], axis=0))

    row = jnp.concatenate([primal_r, primal_w, curve_part, jnp.zeros((28,), jnp.float32)])
    table = gather_rows(row.reshape(1, 128))
    curvature = jnp.sum(table[:, 96:100], axis=0)
    step_size = inner_prior / curvature
    step_field = step_size[:, None, None, None, None]
    step_lanes = jnp.repeat(step_size, 12)

    primal_all = table[:, :48] - step_lanes[None, :] * table[:, 48:96]
    primal_own = (primal_r - step_lanes * primal_w).reshape(cases, 12)
    mixed = lax.dot_general(
        primal_all, coarse_rows, (((0,), (0,)), ((), ())), precision=precise
    ).reshape(cases, 12, 12, 12)
    same = jnp.eye(12, dtype=jnp.float32)[None, :, :, None]
    coarse_values = jnp.sum(mixed * same, axis=(1, 2))

    residual_next = residual - step_field * applied
    solved = solved_r - step_field * solved_w
    near = [face[:cases] - step_field * face[cases:] for face in outer]
    smoothed = solved + 0.5 * (
        edges(solved, near[0], near[1], 1) + edges(solved, near[2], near[3], 2)
    )
    inner_part = jnp.sum(residual_next * smoothed, axis=(1, 2, 3, 4)) + jnp.sum(
        primal_own * coarse_values, axis=1
    )
    inner_row = jnp.concatenate([inner_part, jnp.zeros((124,), jnp.float32)])
    inner_next = total_rows(inner_row.reshape(1, 128))[0, :4]
    growth = (inner_next / inner_prior)[:, None, None, None, None]
    correction = jnp.einsum(
        "pxyz,ckp->cxykz",
        coarse_basis,
        coarse_values.reshape(cases, 3, 4),
        precision=precise,
    )
    direction_next = smoothed + correction + growth * direction
    solution_next = solution + step_field * direction
    return (solution_next, residual_next, direction_next, inner_next)


def solution(mesh):
    fine = Mesh(mesh.devices.reshape(8, 4, 2, 4, 2), ("zl", "x", "c", "y", "zh"))
    field = P(None, GX_AXES, YZ_AXES, None, None)
    block = P(GX_AXES, YZ_AXES, None)
    factor = P(GX_AXES, YZ_AXES, None, None)
    in_specs = (
        field,
        field,
        field,
        block,
        block,
        factor,
        factor,
        block,
        P(None, GX_AXES, YZ_AXES, None),
        factor,
        P(),
    )
    return jax.shard_map(
        per_device,
        mesh=fine,
        in_specs=in_specs,
        out_specs=(field, field, field, P()),
        check_vma=False,
    )
```

time: 2390 us -> 171 us (0.07)
  blocking collectives: 2290 us -> 0 us
  starting transfers between devices: 42 us -> 83.4 us
    all_gather x1 -> x0, blocking collectives: 2050 us -> none  [per_device(): lax.all_gather(primal[:, None, :], ('gx', 'yz'), axis=1, tiled=True)]
    psum x2 -> x0, blocking collectives: 248 us -> none  [the longest x1 144 us: per_device(): inner_next = lax.psum(inner_part, ('gx', 'yz'))]
    all_to_all x0 -> x4, starting transfers between devices: none -> 40.6 us  [exchange(): return lax.all_to_all(spread, axes, 0, 0, tiled=True)]
  transfers between devices with their start and end apart: 8 -> 12, of which waited for: 3 -> 4; matrix products, arithmetic and copies ran while one was open for 0% -> 24% of each run, Pallas kernels for 0% -> 0%
where the time goes in v1:
time: 171 us; the launch traced here: 170 us
  starting transfers between devices  83.4 us (49%)
  waiting for transfers between devices  28.1 us (16%)
  local copies, waits for them, and re-layouts  26.7 us (16%)
  matrix products  17 us (10%)
  other arithmetic  14 us (8%)
    ppermute x8, starting transfers between devices, faces(): found.append((lax.ppermute(tail, axes, up), lax.ppermute(head, axes, down)))  42.9 us
    all_to_all x4, starting transfers between devices, exchange(): return lax.all_to_all(spread, axes, 0, 0, tiled=True)  40.6 us
    all_to_all x4, waiting for transfers between devices, exchange(): return lax.all_to_all(spread, axes, 0, 0, tiled=True)  17.2 us
    reshape x2, local copies, waits for them, and re-layouts, per_device(): coarse_inverse.reshape(12, 8, 4, 2, 4, 2, 12).transpose(2, 3, 4, 1, 5, 6, 0)  13 us
    ppermute x8, waiting for transfers between devices, faces(): found.append((lax.ppermute(tail, axes, up), lax.ppermute(head, axes, down)))  11 us
    dot_general x2, matrix products, restrict(): jnp.einsum('pxyz,cxykz->ckp', coarse_basis, field, precision=precise)  8.68 us
  transfers between devices with their start and end apart: 12, of which 4 were waited for; matrix products, arithmetic and copies ran while one was open for 24% of the time, Pallas kernels for 0%

profile of v1, /device:TPU:1, one launch (start us, length us, event | category | flops | bytes accessed | tf_op | source)
XLA Modules:
  0.0 170.2 jit_solution(6951199194924130676)
XLA Ops:
  0.7 1.1 broadcast_multiply_fusion
  1.8 4.5 %collective-permute-start = (f32[4,1,8,3,128]{4,2,3,1,0:T(8,128)S(1)}, f32[4,1,8,3,128]{4,2,3,1,0:T(8,128)S(1)}, u32[]{:S(2)}, u32[]{:S(2)}) collective-permute-start(f32[4,1,8,3,128]{4,2,3,1,0:T(8,128)S(1)} %get-tuple-element.17), channel_id=1, source_target_pairs={{0,8},{8,16},{16,24},{24,32},{32,40},{40,48},{48,56},{56,64},{64,7... | collective-permute-start | bytes 147464 | tf_op jit(solution)/shard_map/ppermute | solution.py:44
  6.3 5.5 %collective-permute-start.1 = (f32[4,1,8,3,128]{4,2,3,1,0:T(8,128)S(1)}, f32[4,1,8,3,128]{4,2,3,1,0:T(8,128)}, u32[]{:S(2)}, u32[]{:S(2)}) collective-permute-start(f32[4,1,8,3,128]{4,2,3,1,0:T(8,128)S(1)} %get-tuple-element.18), channel_id=1, source_target_pairs={{8,0},{16,8},{24,16},{32,24},{40,32},{48,40},{56,48},{64,56},{72,6... | collective-permute-start | bytes 147464 | tf_op jit(solution)/shard_map/ppermute | solution.py:44
  11.9 12.4 %collective-permute-start.2 = (f32[4,8,1,3,128]{4,2,3,1,0:T(1,128)S(1)}, f32[4,8,1,3,128]{4,2,3,1,0:T(1,128)}, u32[]{:S(2)}, u32[]{:S(2)}) collective-permute-start(f32[4,8,1,3,128]{4,2,3,1,0:T(1,128)S(1)} %get-tuple-element.21), channel_id=1, source_target_pairs={{0,1},{1,2},{2,3},{3,4},{4,5},{5,6},{6,7},{8,9},{9,10},{10,11},{11... | collective-permute-start | bytes 147464 | tf_op jit(solution)/shard_map/ppermute | solution.py:44
  24.4 1.4 collective-permute-start.3
  25.8 0.8 fusion.43
  26.6 1.0 fusion.44
  27.6 0.9 fusion.41
  28.5 1.3 fusion.1
  29.8 0.8 fusion.5
  30.6 0.8 fusion.4
  31.5 0.8 convolution_bitcast_fusion
  32.3 4.3 %convolution_bitcast_fusion.2 = f32[4,3,4]{0,2,1:T(4,128)S(1)} fusion(f32[4,8,8,3,128]{4,2,3,1,0:T(8,128)S(1)} %copy-done.2, f32[4,8,8,128]{3,2,1,0:T(8,128)S(1)} %copy-done.3), kind=kOutput, calls=%fused_computation.4 | convolution fusion | flops 4718592 | bytes 524480 | tf_op jit(solution)/shard_map/pxyz,cxykz->ckp/dot_general | solution.py:95
  36.7 0.1 copy.82
  36.8 0.1 reshape.83
  36.9 1.4 collective-permute-done.3
  38.4 1.9 %multiply_reduce_fusion.1 = (f32[4]{0:T(128)S(1)}, f32[4,8,8,3,128]{4,2,3,1,0:T(8,128)S(1)}) fusion(f32[4,8,8,3,128]{4,2,3,1,0:T(8,128)S(1)} %copy-done.1, f32[4,8,8,128]{3,2,1,0:T(8,128)S(1)} %broadcast_multiply_fusion.1, f32[4,8,8,3,127]{4,2,3,1,0:T(8,128)} %get-tuple-element.26, f32[4,8,8,3,127]{4,2,3,1,0:T(8,128)} %get-tuple-element.25, ...), kind=kLoop, calls=%fused_computation.31 | loop fusion | flops 1572860 | bytes 3303440 | tf_op jit(solution)/shard_map/reduce_sum | solution.py:112
  40.3 4.3 %convolution_bitcast_fusion.1 = f32[4,3,4]{0,2,1:T(4,128)S(1)} fusion(f32[4,8,8,3,128]{4,2,3,1,0:T(8,128)S(1)} %get-tuple-element.10, f32[4,8,8,128]{3,2,1,0:T(8,128)S(1)} %copy-done.3), kind=kOutput, calls=%fused_computation.3 | convolution fusion | flops 4718592 | bytes 524480 | tf_op jit(solution)/shard_map/pxyz,cxykz->ckp/dot_general | solution.py:95
  44.6 0.1 copy.85
  44.7 0.1 reshape.84
  44.9 0.1 pad_maximum_fusion.4
  44.9 0.6 broadcast_in_dim.18
  45.5 11.3 %all-to-all-start = ((f32[16,1,128]{2,1,0:T(1,128)}), f32[16,1,128]{2,1,0:T(1,128)S(1)}, u32[]{:S(2)}, u32[]{:S(2)}) async-start(f32[16,1,128]{2,1,0:T(1,128)} %broadcast_in_dim.18), calls=%async_computation | async-start | bytes 16384 | tf_op jit(solution)/shard_map/all_to_all | solution.py:19
  56.9 0.6 fusion.36
  57.5 1.7 reduce.4
  59.2 5.6 %reshape.88 = f32[12,8,4,2,4,2,12]{6,5,4,3,2,1,0:T(2,128)} reshape(f32[12,6144]{1,0:T(8,128)S(1)} %reduce.4) | data formatting | bytes 589824 | tf_op jit(solution)/shard_map/reshape | solution.py:98
  64.7 7.4 %copy.88 = f32[12,8,4,2,4,2,12]{0,6,5,1,4,3,2:T(8,128)} copy(f32[12,8,4,2,4,2,12]{6,5,4,3,2,1,0:T(2,128)} %reshape.88) | data formatting | bytes 589824 | tf_op jit(solution)/shard_map/reshape | solution.py:98
  72.1 3.4 %reshape.89 = f32[512,144]{1,0:T(8,128)S(1)} reshape(f32[4,2,4,8,2,12,12]{6,5,4,3,2,1,0:T(8,128)} %bitcast.67) | data formatting | bytes 589824 | tf_op jit(solution)/shard_map/reshape | solution.py:100
  75.5 0.9 copy.89
  76.4 1.7 %reshape.98 = f32[12,12,512,1]{2,1,0,3:T(8,128)} reshape(f32[144,512]{1,0:T(8,128)} %copy.89) | data formatting | bytes 589824 | tf_op jit(solution)/shard_map/dot_general | solution.py:126
  78.1 0.2 copy.86
  78.3 0.6 pad.7.clone
  78.9 0.7 broadcast_in_dim.20
  79.6 8.4 %all-to-all-start.1 = ((f32[32,16,128]{2,1,0:T(8,128)}), f32[32,16,128]{2,1,0:T(8,128)S(1)}, u32[]{:S(2)}, u32[]{:S(2)}) async-start(f32[32,16,128]{2,1,0:T(8,128)} %broadcast_in_dim.20), calls=%async_computation.1 | async-start | bytes 524288 | tf_op jit(solution)/shard_map/all_to_all | solution.py:19
  88.1 0.9 fusion.14
  89.0 0.7 pad_maximum_fusion.3
  89.7 3.5 %collective-permute-start.4 = (f32[8,1,8,3,128]{4,2,3,1,0:T(8,128)}, f32[8,1,8,3,128]{4,2,3,1,0:T(8,128)S(1)}, u32[]{:S(2)}, u32[]{:S(2)}) collective-permute-start(f32[8,1,8,3,128]{4,2,3,1,0:T(8,128)} %get-tuple-element.11), channel_id=1, source_target_pairs={{0,8},{8,16},{16,24},{24,32},{32,40},{40,48},{48,56},{56,64},{64,7... | collective-permute-start | bytes 294920 | tf_op jit(solution)/shard_map/ppermute | solution.py:44
  93.2 1.9 %collective-permute-start.5 = (f32[8,1,8,3,128]{4,2,3,1,0:T(8,128)}, f32[8,1,8,3,128]{4,2,3,1,0:T(8,128)}, u32[]{:S(2)}, u32[]{:S(2)}) collective-permute-start(f32[8,1,8,3,128]{4,2,3,1,0:T(8,128)} %get-tuple-element.12), channel_id=1, source_target_pairs={{8,0},{16,8},{24,16},{32,24},{40,32},{48,40},{56,48},{64,56},{72,6... | collective-permute-start | bytes 294920 | tf_op jit(solution)/shard_map/ppermute | solution.py:44
  95.1 0.8 pad_maximum_fusion.1
  95.9 12.2 %collective-permute-start.6 = (f32[8,8,1,3,128]{4,2,3,1,0:T(1,128)}, f32[8,8,1,3,128]{4,2,3,1,0:T(1,128)S(1)}, u32[]{:S(2)}, u32[]{:S(2)}) collective-permute-start(f32[8,8,1,3,128]{4,2,3,1,0:T(1,128)} %get-tuple-element.13), channel_id=1, source_target_pairs={{0,1},{1,2},{2,3},{3,4},{4,5},{5,6},{6,7},{8,9},{9,10},{10,11},{11... | collective-permute-start | bytes 294920 | tf_op jit(solution)/shard_map/ppermute | solution.py:44
  108.2 1.3 collective-permute-start.7
  109.5 0.1 slice_reduce_fusion
  109.6 0.7 div.6
  110.4 0.1 mul.148
  110.5 0.1 fusion.22
  110.6 0.1 copy.87
  110.7 2.9 %fusion = f32[4,12]{1,0:T(4,128)S(1)} fusion(f32[12,12,512,1]{2,1,0,3:T(8,128)} %reshape.98, f32[12,12]{0,1:T(8,128)} %fusion.36, f32[4,12,512,1]{2,1,0,3:T(8,128)S(1)} %reshape.97), kind=kOutput, calls=%fused_computation.2 | convolution fusion | flops 42481104 | bytes 393984 | tf_op jit(solution)/shard_map/dot_general | solution.py:126
  113.6 0.1 reshape.90
  113.7 0.1 copy.92
  113.8 0.6 copy-done.6
  114.5 0.9 fusion.34
  115.5 9.5 %collective-permute-done.7 = f32[8,8,1,3,128]{4,2,3,1,0:T(1,128)S(1)} collective-permute-done((f32[8,8,1,3,128]{4,2,3,1,0:T(1,128)}, f32[8,8,1,3,128]{4,2,3,1,0:T(1,128)S(1)}, u32[]{:S(2)}, u32[]{:S(2)}) %collective-permute-start.7) | collective-permute-done | bytes 98336 | tf_op jit(solution)/shard_map/ppermute | solution.py:44
  125.0 0.2 fusion.32
  125.2 1.7 %multiply_reduce_fusion = (f32[4]{0:T(128)S(1)}, f32[4,8,8,3,128]{4,2,3,1,0:T(8,128)S(1)}, f32[4,8,8,3,128]{4,2,3,1,0:T(8,128)}) fusion(f32[4,8,1,3,128]{4,2,3,1,0:T(1,128)S(1)} %get-tuple-element.32, f32[8]{0:T(128)} %pad.7.clone, f32[4,8,1,3,128]{4,2,3,1,0:T(1,128)S(1)} %get-tuple-element.31, f32[4,1,8,3,128]{4,2,3,1,0:T(8,128)S(1)} %get-tuple-element.30, ...), kind=kLoop, calls=%fused_computation.28 | loop fusion | flops 1277948 | bytes 2555968 | tf_op jit(solution)/shard_map/reduce_sum | solution.py:138
  126.9 0.6 broadcast_in_dim.50
  127.5 13.2 %all-to-all-start.2 = ((f32[16,1,128]{2,1,0:T(1,128)}), f32[16,1,128]{2,1,0:T(1,128)S(1)}, u32[]{:S(2)}, u32[]{:S(2)}) async-start(f32[16,1,128]{2,1,0:T(1,128)} %broadcast_in_dim.50), calls=%async_computation.2 | async-start | bytes 16384 | tf_op jit(solution)/shard_map/all_to_all | solution.py:19
  140.8 0.1 reshape.99
  140.9 11.1 %all-to-all-done.2 = f32[16,1,128]{2,1,0:T(1,128)S(1)} async-done(((f32[16,1,128]{2,1,0:T(1,128)}), f32[16,1,128]{2,1,0:T(1,128)S(1)}, u32[]{:S(2)}, u32[]{:S(2)}) %all-to-all-start.2) | async-done | bytes 8224 | tf_op jit(solution)/shard_map/all_to_all | solution.py:19
  152.0 0.6 broadcast_in_dim.51
  152.6 7.5 %all-to-all-start.3 = ((f32[32,1,128]{2,1,0:T(1,128)}), f32[32,1,128]{2,1,0:T(1,128)S(1)}, u32[]{:S(2)}, u32[]{:S(2)}) async-start(f32[32,1,128]{2,1,0:T(1,128)} %broadcast_in_dim.51), calls=%async_computation.3 | async-start | bytes 32768 | tf_op jit(solution)/shard_map/all_to_all | solution.py:19
  160.2 0.8 fusion.24
  161.0 6.0 %all-to-all-done.3 = f32[32,1,128]{2,1,0:T(1,128)S(1)} async-done(((f32[32,1,128]{2,1,0:T(1,128)}), f32[32,1,128]{2,1,0:T(1,128)S(1)}, u32[]{:S(2)}, u32[]{:S(2)}) %all-to-all-start.3) | async-done | bytes 16416 | tf_op jit(solution)/shard_map/all_to_all | solution.py:19
  167.1 1.2 fusion.37
  168.2 2.0 %fusion.16 = (f32[4,8,8,3,128]{4,2,3,1,0:T(8,128)}, f32[4,8,8,3,128]{4,2,3,1,0:T(8,128)}) fusion(f32[4,8,8,3,128]{4,2,3,1,0:T(8,128)S(1)} %get-tuple-element.7, f32[4,3,8,8,128]{4,1,3,2,0:T(4,128)S(1)} %fusion.24, f32[4,8,8,3,128]{4,2,3,1,0:T(8,128)S(1)} %copy-done.1, f32[4]{0:T(128)S(1)} %get-tuple-element.4, f32[4,8,8,3,128]{4,2,3,1,0:T(8,128)} %param.11, ...), kind=kLoop, calls=%fused_computation.25 | loop fusion | flops 491520 | bytes 2359328 | tf_op jit(solution)/shard_map/add | solution.py:150
  (40 shorter events, 0.3 us)
Async XLA Ops:
  0.6 27.9 %copy-start = (f32[1,1,384,384]{3,2,1,0:T(8,128)S(1)}, f32[1,1,384,384]{3,2,1,0:T(8,128)}, u32[]{:S(2)}) copy-start(f32[1,1,384,384]{3,2,1,0:T(8,128)} %param.16) | copy-start | bytes 1769476
  0.6 27.9 %copy-start.9 = (s32[1,1,384]{2,1,0:T(1,128)S(1)}, s32[1,1,384]{2,1,0:T(1,128)}, u32[]{:S(2)}) copy-start(s32[1,1,384]{2,1,0:T(1,128)} %param.18) | copy-start | bytes 4612
  0.7 27.9 %copy-start.4 = (f32[1,1,384,384]{3,2,1,0:T(8,128)S(1)}, f32[1,1,384,384]{3,2,1,0:T(8,128)}, u32[]{:S(2)}) copy-start(f32[1,1,384,384]{3,2,1,0:T(8,128)} %param.17) | copy-start | bytes 1769476
  1.8 35.1 %collective-permute-start = (f32[4,1,8,3,128]{4,2,3,1,0:T(8,128)S(1)}, f32[4,1,8,3,128]{4,2,3,1,0:T(8,128)S(1)}, u32[]{:S(2)}, u32[]{:S(2)}) collective-permute-start(f32[4,1,8,3,128]{4,2,3,1,0:T(8,128)S(1)} %get-tuple-element.17), channel_id=1, source_target_pairs={{0,8},{8,16},{16,24},{24,32},{32,40},{40,48},{48,56},{56,64},{64,7... | collective-permute-start | bytes 147464 | tf_op jit(solution)/shard_map/ppermute | solution.py:44
  6.3 30.6 %collective-permute-start.1 = (f32[4,1,8,3,128]{4,2,3,1,0:T(8,128)S(1)}, f32[4,1,8,3,128]{4,2,3,1,0:T(8,128)}, u32[]{:S(2)}, u32[]{:S(2)}) collective-permute-start(f32[4,1,8,3,128]{4,2,3,1,0:T(8,128)S(1)} %get-tuple-element.18), channel_id=1, source_target_pairs={{8,0},{16,8},{24,16},{32,24},{40,32},{48,40},{56,48},{64,56},{72,6... | collective-permute-start | bytes 147464 | tf_op jit(solution)/shard_map/ppermute | solution.py:44
  11.9 25.0 %collective-permute-start.2 = (f32[4,8,1,3,128]{4,2,3,1,0:T(1,128)S(1)}, f32[4,8,1,3,128]{4,2,3,1,0:T(1,128)}, u32[]{:S(2)}, u32[]{:S(2)}) collective-permute-start(f32[4,8,1,3,128]{4,2,3,1,0:T(1,128)S(1)} %get-tuple-element.21), channel_id=1, source_target_pairs={{0,1},{1,2},{2,3},{3,4},{4,5},{5,6},{6,7},{8,9},{9,10},{10,11},{11... | collective-permute-start | bytes 147464 | tf_op jit(solution)/shard_map/ppermute | solution.py:44
  24.4 7.1 %copy-start.8 = (f32[8,8,128]{2,1,0:T(8,128)S(1)}, f32[8,8,128]{2,1,0:T(8,128)}, u32[]{:S(2)}) copy-start(f32[8,8,128]{2,1,0:T(8,128)} %param.15) | copy-start | bytes 98308
  24.4 7.1 %copy-start.2 = (f32[4,8,8,3,128]{4,2,3,1,0:T(8,128)S(1)}, f32[4,8,8,3,128]{4,2,3,1,0:T(8,128)}, u32[]{:S(2)}) copy-start(f32[4,8,8,3,128]{4,2,3,1,0:T(8,128)} %param.12) | copy-start | bytes 1179652
  24.4 14.0 %collective-permute-start.3 = (f32[4,8,1,3,128]{4,2,3,1,0:T(1,128)S(1)}, f32[4,8,1,3,128]{4,2,3,1,0:T(1,128)}, u32[]{:S(2)}, u32[]{:S(2)}) collective-permute-start(f32[4,8,1,3,128]{4,2,3,1,0:T(1,128)S(1)} %get-tuple-element.22), channel_id=1, source_target_pairs={{1,0},{2,1},{3,2},{4,3},{5,4},{6,5},{7,6},{9,8},{10,9},{11,10},{12... | collective-permute-start | bytes 147464 | tf_op jit(solution)/shard_map/ppermute | solution.py:44
  26.6 5.7 %copy-start.3 = (f32[4,8,8,128]{3,2,1,0:T(8,128)S(1)}, f32[4,8,8,128]{3,2,1,0:T(8,128)}, u32[]{:S(2)}) copy-start(f32[4,8,8,128]{3,2,1,0:T(8,128)} %param.19) | copy-start | bytes 393220
  27.6 10.7 %copy-start.1 = (f32[4,8,8,3,128]{4,2,3,1,0:T(8,128)S(1)}, f32[4,8,8,3,128]{4,2,3,1,0:T(8,128)}, u32[]{:S(2)}) copy-start(f32[4,8,8,3,128]{4,2,3,1,0:T(8,128)} %param.13) | copy-start | bytes 1179652
  27.6 10.7 %copy-start.5 = (f32[8,8,128]{2,1,0:T(8,128)S(1)}, f32[8,8,128]{2,1,0:T(8,128)}, u32[]{:S(2)}) copy-start(f32[8,8,128]{2,1,0:T(8,128)} %param.14) | copy-start | bytes 98308
  36.9 1.4 copy-start.7
  45.5 33.4 %all-to-all-start = ((f32[16,1,128]{2,1,0:T(1,128)}), f32[16,1,128]{2,1,0:T(1,128)S(1)}, u32[]{:S(2)}, u32[]{:S(2)}) async-start(f32[16,1,128]{2,1,0:T(1,128)} %broadcast_in_dim.18), calls=%async_computation | async-start | bytes 16384 | tf_op jit(solution)/shard_map/all_to_all | solution.py:19
  79.6 29.9 %all-to-all-start.1 = ((f32[32,16,128]{2,1,0:T(8,128)}), f32[32,16,128]{2,1,0:T(8,128)S(1)}, u32[]{:S(2)}, u32[]{:S(2)}) async-start(f32[32,16,128]{2,1,0:T(8,128)} %broadcast_in_dim.20), calls=%async_computation.1 | async-start | bytes 524288 | tf_op jit(solution)/shard_map/all_to_all | solution.py:19
  89.7 24.2 %collective-permute-start.4 = (f32[8,1,8,3,128]{4,2,3,1,0:T(8,128)}, f32[8,1,8,3,128]{4,2,3,1,0:T(8,128)S(1)}, u32[]{:S(2)}, u32[]{:S(2)}) collective-permute-start(f32[8,1,8,3,128]{4,2,3,1,0:T(8,128)} %get-tuple-element.11), channel_id=1, source_target_pairs={{0,8},{8,16},{16,24},{24,32},{32,40},{40,48},{48,56},{56,64},{64,7... | collective-permute-start | bytes 294920 | tf_op jit(solution)/shard_map/ppermute | solution.py:44
  93.2 21.3 %collective-permute-start.5 = (f32[8,1,8,3,128]{4,2,3,1,0:T(8,128)}, f32[8,1,8,3,128]{4,2,3,1,0:T(8,128)}, u32[]{:S(2)}, u32[]{:S(2)}) collective-permute-start(f32[8,1,8,3,128]{4,2,3,1,0:T(8,128)} %get-tuple-element.12), channel_id=1, source_target_pairs={{8,0},{16,8},{24,16},{32,24},{40,32},{48,40},{56,48},{64,56},{72,6... | collective-permute-start | bytes 294920 | tf_op jit(solution)/shard_map/ppermute | solution.py:44
  95.9 19.5 %collective-permute-start.6 = (f32[8,8,1,3,128]{4,2,3,1,0:T(1,128)}, f32[8,8,1,3,128]{4,2,3,1,0:T(1,128)S(1)}, u32[]{:S(2)}, u32[]{:S(2)}) collective-permute-start(f32[8,8,1,3,128]{4,2,3,1,0:T(1,128)} %get-tuple-element.13), channel_id=1, source_target_pairs={{0,1},{1,2},{2,3},{3,4},{4,5},{5,6},{6,7},{8,9},{9,10},{10,11},{11... | collective-permute-start | bytes 294920 | tf_op jit(solution)/shard_map/ppermute | solution.py:44
  108.2 16.8 %collective-permute-start.7 = (f32[8,8,1,3,128]{4,2,3,1,0:T(1,128)}, f32[8,8,1,3,128]{4,2,3,1,0:T(1,128)S(1)}, u32[]{:S(2)}, u32[]{:S(2)}) collective-permute-start(f32[8,8,1,3,128]{4,2,3,1,0:T(1,128)} %get-tuple-element.14), channel_id=1, source_target_pairs={{1,0},{2,1},{3,2},{4,3},{5,4},{6,5},{7,6},{9,8},{10,9},{11,10},{12... | collective-permute-start | bytes 294920 | tf_op jit(solution)/shard_map/ppermute | solution.py:44
  113.8 0.6 copy-start.6
  127.5 24.5 %all-to-all-start.2 = ((f32[16,1,128]{2,1,0:T(1,128)}), f32[16,1,128]{2,1,0:T(1,128)S(1)}, u32[]{:S(2)}, u32[]{:S(2)}) async-start(f32[16,1,128]{2,1,0:T(1,128)} %broadcast_in_dim.50), calls=%async_computation.2 | async-start | bytes 16384 | tf_op jit(solution)/shard_map/all_to_all | solution.py:19
  152.6 14.4 %all-to-all-start.3 = ((f32[32,1,128]{2,1,0:T(1,128)}), f32[32,1,128]{2,1,0:T(1,128)S(1)}, u32[]{:S(2)}, u32[]{:S(2)}) async-start(f32[32,1,128]{2,1,0:T(1,128)} %broadcast_in_dim.51), calls=%async_computation.3 | async-start | bytes 32768 | tf_op jit(solution)/shard_map/all_to_all | solution.py:19

commit v2 on v1

v2 whole, which is shorter than its diff:
```python
import jax
import jax.numpy as jnp
from jax import lax
from jax.experimental import pallas as pl
from jax.experimental.pallas import tpu as pltpu
from jax.sharding import Mesh, PartitionSpec as P


DEPTH = ("zh", "zl")
PLANE = ("x", "c", "y")
GX_AXES = ("zl", "x", "c")
YZ_AXES = ("y", "zh")
N_DEPTH = 16
N_PLANE = 32
N_GX = 64
N_YZ = 8

CASES, NX, COMP, NY, NZ = 4, 8, 3, 8, 128
NP = 4
PRIMAL = COMP * NP
LINE = COMP * NZ
TILES = CASES * NX * COMP
FIELD = (CASES, NX, COMP, NY, NZ)
f32 = jnp.float32
bf16 = jnp.bfloat16
NT = (((1,), (1,)), ((), ()))
NN = (((1,), (0,)), ((), ()))


def mxu(a, b, dims):
    return lax.dot_general(a, b, dims, preferred_element_type=f32)


def halves(a):
    high = a.astype(bf16)
    return high, (a - high.astype(f32)).astype(bf16)


def thirds(a):
    high = a.astype(bf16)
    rest = a - high.astype(f32)
    mid = rest.astype(bf16)
    return high, mid, (rest - mid.astype(f32)).astype(bf16)


def product(a, b, dims):
    a0, a1, a2 = thirds(a)
    b0, b1, b2 = thirds(b)
    small = mxu(a0, b2, dims) + mxu(a2, b0, dims) + mxu(a1, b1, dims)
    return (small + (mxu(a0, b1, dims) + mxu(a1, b0, dims))) + mxu(a0, b0, dims)


def picked(chosen, b, dims):
    b0, b1, b2 = thirds(b)
    return (mxu(chosen, b2, dims) + mxu(chosen, b1, dims)) + mxu(chosen, b0, dims)


def lane_sums(a):
    ones = jnp.ones((a.shape[1], 128), bf16)
    a0, a1, a2 = thirds(a)
    return (mxu(a2, ones, NN) + mxu(a1, ones, NN)) + mxu(a0, ones, NN)


def lane_row(a):
    rows = a.shape[0]
    if rows < 128:
        a = jnp.concatenate([a, jnp.zeros((128 - rows, 128), f32)], axis=0)
    ones = jnp.ones((8, 128), bf16)
    a0, a1, a2 = thirds(a)
    return ((mxu(ones, a2, NT) + mxu(ones, a1, NT)) + mxu(ones, a0, NT))[0:1]


def restricted(basis, field):
    rows = []
    for c in range(CASES):
        for k in range(COMP):
            for p in range(NP):
                total = basis[p, 0] * field[c, 0, k]
                for x in range(1, NX):
                    total = total + basis[p, x] * field[c, x, k]
                rows.append(jnp.sum(total, axis=0, keepdims=True))
    return jnp.concatenate(rows, axis=0)


def local_solve(field, operator_ref, out_ref):
    total = None
    for k in range(COMP):
        rows = field[:, :, k].reshape(CASES * NX * NY, NZ)
        part = product(rows, operator_ref[k * NZ : (k + 1) * NZ, :], NN)
        total = part if total is None else total + part
    for k in range(COMP):
        out_ref[:, :, k] = total[:, k * NZ : (k + 1) * NZ].reshape(CASES, NX, NY, NZ)


def side_rows(ref, out_ref, y, base):
    for c in range(CASES):
        for x in range(NX):
            for k in range(COMP):
                row = base + (c * NX + x) * COMP + k
                out_ref[row : row + 1, :] = ref[c, x, k, y : y + 1, :]


def faces_kernel(direction, stiffness, low_x, high_x, low_y, high_y):
    for x, out in ((0, low_x), (NX - 1, high_x)):
        out[...] = direction[:, x] * stiffness[x][None, None]
    for y, out in ((0, low_y), (NY - 1, high_y)):
        for c in range(CASES):
            for x in range(NX):
                for k in range(COMP):
                    row = (c * NX + x) * COMP + k
                    out[row : row + 1, :] = (
                        direction[c, x, k, y : y + 1, :] * stiffness[x, y : y + 1, :]
                    )


def prepare_kernel(residual, lower, upper, pivots, basis, operator, solved, primal):
    order = pivots[...]
    at = lax.broadcasted_iota(jnp.int32, (LINE, LINE), 0)
    chosen = jnp.where(at == order, 1.0, 0.0).astype(bf16)
    both = product(upper[...], lower[...], NN)
    rows = picked(chosen, both, NN)
    operator[...] = picked(chosen, rows, NT)
    local_solve(residual, operator, solved)
    primal[...] = lane_sums(restricted(basis, residual))


def by_depth_kernel(inverse, by_depth):
    for r in range(PRIMAL):
        for half in range(2):
            for part in range(3):
                at = r * 48 + half * 3 + part
                by_depth[r, half, :, part * 128 : (part + 1) * 128] = inverse[
                    pl.ds(at, 8, stride=6), :
                ]


def applied_kernel(
    direction, stiffness, coupling, below_x, above_x, below_y, above_y,
    basis, operator, solved_r, primal_r,
    applied, solved, primal, row, low_x, high_x, low_y, high_y,
):
    y_at = lax.broadcasted_iota(jnp.int32, (NY, NZ), 0)
    z_at = lax.broadcasted_iota(jnp.int32, (NY, NZ), 1)
    first_y, last_y = y_at == 0, y_at == NY - 1
    first_z, last_z = z_at == 0, z_at == NZ - 1
    curves = []
    for c in range(CASES):
        curve = None
        for x in range(NX):
            stiff = stiffness[x]
            total = direction[c, x, 0] + direction[c, x, 1] + direction[c, x, 2]
            spread = coupling[x] * total
            for k in range(COMP):
                here = direction[c, x, k]
                mine = stiff * here
                left = below_x[c, k] if x == 0 else stiffness[x - 1] * direction[c, x - 1, k]
                right = above_x[c, k] if x == NX - 1 else stiffness[x + 1] * direction[c, x + 1, k]
                at = (c * NX + x) * COMP + k
                down = jnp.where(
                    first_y,
                    jnp.broadcast_to(below_y[at : at + 1, :], (NY, NZ)),
                    pltpu.roll(mine, 1, 0),
                )
                up = jnp.where(
                    last_y,
                    jnp.broadcast_to(above_y[at : at + 1, :], (NY, NZ)),
                    pltpu.roll(mine, NY - 1, 0),
                )
                before = jnp.where(first_z, 0.0, pltpu.roll(mine, 1, 1))
                after = jnp.where(last_z, 0.0, pltpu.roll(mine, NZ - 1, 1))
                around = (left + right) + (down + up) + (before + after)
                out = stiff * (6.0 * mine - around) + spread
                applied[c, x, k] = out
                part = here * out
                curve = part if curve is None else curve + part
        curves.append(jnp.sum(curve, axis=0, keepdims=True))
    local_solve(applied, operator, solved)
    sums = restricted(basis, applied)
    whole = lane_sums(sums)
    primal[...] = whole
    stacked = jnp.concatenate([sums] + curves, axis=0)
    mine_row = lane_row(stacked)
    lane = lax.broadcasted_iota(jnp.int32, (48, 128), 1)
    sub = lax.broadcasted_iota(jnp.int32, (48, 128), 0)
    first = jnp.sum(jnp.where(lane == sub, primal_r[...], 0.0), axis=0, keepdims=True)
    row[...] = first + pltpu.roll(mine_row, 48, 1)
    for source, base in ((solved_r, 0), (solved, CASES)):
        low_x[base : base + CASES] = source[:, 0]
        high_x[base : base + CASES] = source[:, NX - 1]
        side_rows(source, low_y, 0, base * NX * COMP)
        side_rows(source, high_y, NY - 1, base * NX * COMP)


def steps_of(table, prior):
    total = jnp.sum(table[...], axis=0, keepdims=True)
    lane = lax.broadcasted_iota(jnp.int32, (1, 128), 1)
    steps = []
    for c in range(CASES):
        curvature = jnp.sum(jnp.where(lane == 96 + c, total, 0.0), axis=1, keepdims=True)
        steps.append(jnp.broadcast_to(prior[c] / curvature, (1, 128)))
    return steps


def smoothed_at(c, x, k, step, solved_r, solved_w, below_x, above_x, below_y, above_y, y_at):
    here = solved_r[c, x, k] - step * solved_w[c, x, k]
    at = (c * NX + x) * COMP + k
    under = below_y[at : at + 1, :] - step * below_y[TILES + at : TILES + at + 1, :]
    over = above_y[at : at + 1, :] - step * above_y[TILES + at : TILES + at + 1, :]
    beside = jnp.where(y_at == 0, jnp.broadcast_to(under, (NY, NZ)), 0.0)
    beside = beside + jnp.where(y_at == NY - 1, jnp.broadcast_to(over, (NY, NZ)), 0.0)
    if x == 0:
        beside = beside + (below_x[c, k] - step * below_x[CASES + c, k])
    if x == NX - 1:
        beside = beside + (above_x[c, k] - step * above_x[CASES + c, k])
    return here + 0.5 * beside


def coarse_kernel(
    prior, table, inverse, primal_r, primal_w, residual, applied, solved_r, solved_w,
    below_x, above_x, below_y, above_y,
    row, steps_out, coarse,
):
    steps = steps_of(table, prior)
    for c in range(CASES):
        steps_out[c : c + 1, :] = steps[c]
    lane = lax.broadcasted_iota(jnp.int32, (1, 128), 1)
    weight = jnp.zeros((1, 128), f32)
    for c in range(CASES):
        weight = jnp.where(lane // PRIMAL == c, steps[c], weight)
    everything = table[...]
    primal = everything - weight * pltpu.roll(everything, 80, 1)
    high, low = halves(primal)
    pair = jnp.concatenate([high, low], axis=1)
    source = lax.broadcasted_iota(jnp.int32, (256, LINE), 0) % 128
    target = lax.broadcasted_iota(jnp.int32, (256, LINE), 1)
    slot = lax.broadcasted_iota(jnp.int32, (8, LINE), 1) // PRIMAL
    rows = []
    for c in range(CASES):
        spread = jnp.where(source == c * PRIMAL + target % PRIMAL, 1.0, 0.0).astype(bf16)
        wide = mxu(pair, spread, NN)
        gathered = []
        for half in range(2):
            total = None
            for group in range(16):
                for z_high in range(2):
                    at = ((half * 16 + group) * 2 + z_high) * 8
                    part = jnp.where(slot == group * 2 + z_high, wide[at : at + 8], 0.0)
                    total = part if total is None else total + part
            gathered.append(total)
        for r in range(PRIMAL):
            total = None
            for half in range(2):
                part = gathered[half] * inverse[r, half]
                total = part if total is None else total + part
            folded = total[:, 0:128] + total[:, 128:256] + total[:, 256:384]
            rows.append(jnp.sum(folded, axis=0, keepdims=True))
    coarse_values = lane_sums(jnp.concatenate(rows, axis=0))
    coarse[...] = coarse_values

    y_at = lax.broadcasted_iota(jnp.int32, (NY, NZ), 0)
    sums = []
    for c in range(CASES):
        step = steps[c]
        total = None
        for x in range(NX):
            for k in range(COMP):
                smooth = smoothed_at(
                    c, x, k, step, solved_r, solved_w, below_x, above_x, below_y, above_y, y_at
                )
                part = (residual[c, x, k] - step * applied[c, x, k]) * smooth
                total = part if total is None else total + part
        own = primal_r[c * PRIMAL : (c + 1) * PRIMAL] - step * primal_w[c * PRIMAL : (c + 1) * PRIMAL]
        both = jnp.sum(own * coarse_values[c * PRIMAL : (c + 1) * PRIMAL], axis=0, keepdims=True)
        sums.append(
            jnp.sum(total, axis=0, keepdims=True) + jnp.where(lane == 0, both, 0.0)
        )
    row[...] = lane_row(jnp.concatenate(sums, axis=0))


def update_kernel(
    steps, coarse, basis, solution, residual, direction, applied, solved_r, solved_w,
    below_x, above_x, below_y, above_y,
    solution_next, residual_next, preconditioned,
):
    y_at = lax.broadcasted_iota(jnp.int32, (NY, NZ), 0)
    for c in range(CASES):
        step = steps[c : c + 1, :]
        for x in range(NX):
            for k in range(COMP):
                residual_next[c, x, k] = residual[c, x, k] - step * applied[c, x, k]
                solution_next[c, x, k] = solution[c, x, k] + step * direction[c, x, k]
                out = smoothed_at(
                    c, x, k, step, solved_r, solved_w, below_x, above_x, below_y, above_y, y_at
                )
                for p in range(NP):
                    at = c * PRIMAL + k * NP + p
                    out = out + basis[p, x] * coarse[at : at + 1, :]
                preconditioned[c, x, k] = out


def final_kernel(prior, parts, preconditioned, direction, direction_next, inner):
    total = jnp.sum(parts[...], axis=0, keepdims=True)
    inner[...] = total
    lane = lax.broadcasted_iota(jnp.int32, (1, 128), 1)
    for c in range(CASES):
        mine = jnp.sum(jnp.where(lane == c, total, 0.0), axis=1, keepdims=True)
        growth = jnp.broadcast_to(mine / prior[c], (1, NZ))
        for x in range(NX):
            for k in range(COMP):
                direction_next[c, x, k] = (
                    preconditioned[c, x, k] + growth * direction[c, x, k]
                )


VMEM = pl.BlockSpec(memory_space=pltpu.VMEM)
SMEM = pl.BlockSpec(memory_space=pltpu.SMEM)


def local_call(body, outs, scalars, *args):
    return pl.pallas_call(
        body,
        out_shape=[jax.ShapeDtypeStruct(shape, f32) for shape in outs],
        in_specs=[SMEM] * scalars + [VMEM] * (len(args) - scalars),
        out_specs=[VMEM] * len(outs),
        compiler_params=pltpu.CompilerParams(vmem_limit_bytes=40 << 20),
    )(*args)


def exchange(block, axes, count):
    spread = jnp.broadcast_to(block[None], (count,) + block.shape)
    return lax.all_to_all(spread, axes, 0, 0, tiled=True)


def neighbours(low, high, axes, count):
    up = [(i, i + 1) for i in range(count - 1)]
    down = [(i + 1, i) for i in range(count - 1)]
    return lax.ppermute(high, axes, up), lax.ppermute(low, axes, down)


def body(
    solution, residual, direction, stiffness, coupling, lower_factor, upper_factor,
    pivot_order, coarse_basis, coarse_inverse, inner_prior,
):
    solution, residual, direction = (
        a.transpose(0, 1, 3, 2, 4) for a in (solution, residual, direction)
    )
    end_x = (CASES, COMP, NY, NZ)
    end_y = (TILES, NZ)
    low_x, high_x, low_y, high_y = local_call(
        faces_kernel, [end_x, end_x, end_y, end_y], 0, direction, stiffness
    )
    below_y, above_y = neighbours(low_y, high_y, YZ_AXES, N_YZ)
    below_x, above_x = neighbours(low_x, high_x, GX_AXES, N_GX)

    operator, solved_r, primal_r = local_call(
        prepare_kernel, [(LINE, LINE), FIELD, (48, 128)], 0,
        residual, lower_factor[0, 0], upper_factor[0, 0], pivot_order[0], coarse_basis,
    )

    twice_x = (2 * CASES, COMP, NY, NZ)
    twice_y = (2 * TILES, NZ)
    applied, solved_w, primal_w, row, low_x, high_x, low_y, high_y = local_call(
        applied_kernel,
        [FIELD, FIELD, (48, 128), (1, 128), twice_x, twice_x, twice_y, twice_y], 0,
        direction, stiffness, coupling, below_x, above_x, below_y, above_y,
        coarse_basis, operator, solved_r, primal_r,
    )

    line = exchange(row, DEPTH, N_DEPTH)
    below_y, above_y = neighbours(low_y, high_y, YZ_AXES, N_YZ)
    below_x, above_x = neighbours(low_x, high_x, GX_AXES, N_GX)
    (inverse,) = local_call(
        by_depth_kernel, [(PRIMAL, 2, 8, LINE)], 0,
        coarse_inverse.reshape(PRIMAL * 48, 128),
    )
    table = exchange(line.reshape(N_DEPTH, 128), PLANE, N_PLANE)
    table = table.reshape(N_PLANE * N_DEPTH, 128)

    inner_row, steps, coarse = local_call(
        coarse_kernel, [(1, 128), (CASES, 128), (48, 128)], 1,
        inner_prior, table, inverse, primal_r, primal_w, residual, applied, solved_r, solved_w,
        below_x, above_x, below_y, above_y,
    )
    line = exchange(inner_row, DEPTH, N_DEPTH)
    solution_next, residual_next, preconditioned = local_call(
        update_kernel, [FIELD, FIELD, FIELD], 0,
        steps, coarse, coarse_basis, solution, residual, direction, applied,
        solved_r, solved_w, below_x, above_x, below_y, above_y,
    )
    parts = exchange(jnp.sum(line, axis=0), PLANE, N_PLANE)
    direction_next, inner = local_call(
        final_kernel, [FIELD, (1, 128)], 1,
        inner_prior, parts.reshape(N_PLANE, 128), preconditioned, direction,
    )
    solution_next, residual_next, direction_next = (
        a.transpose(0, 1, 3, 2, 4) for a in (solution_next, residual_next, direction_next)
    )
    return (solution_next, residual_next, direction_next, inner[0, :CASES])


def solution(mesh):
    fine = Mesh(mesh.devices.reshape(8, 4, 2, 4, 2), ("zl", "x", "c", "y", "zh"))
    field = P(None, GX_AXES, YZ_AXES, None, None)
    block = P(GX_AXES, YZ_AXES, None)
    factor = P(GX_AXES, YZ_AXES, None, None)
    in_specs = (
        field, field, field, block, block, factor, factor, block,
        P(None, GX_AXES, YZ_AXES, None), factor, P(),
    )
    return jax.shard_map(
        body,
        mesh=fine,
        in_specs=in_specs,
        out_specs=(field, field, field, P()),
        check_vma=False,
    )
```

time: 171 us -> 146 us (0.85)
  blocking collectives: 0 us -> 42.9 us
  starting transfers between devices: 83.4 us -> 50.7 us
  matrix products: 17 us -> 0 us
  local copies, waits for them, and re-layouts: 26.7 us -> 9.72 us
  other arithmetic: 14 us -> 0.02 us
  Pallas kernels: 0 us -> 11.7 us
    all_to_all x0 -> x2, blocking collectives: none -> 42.9 us  [exchange(): return lax.all_to_all(spread, axes, 0, 0, tiled=True)]
    all_to_all x4 -> x2, starting transfers between devices: 40.6 us -> 18.4 us  [exchange(): return lax.all_to_all(spread, axes, 0, 0, tiled=True)]
    dot_general x9 -> x0, matrix products: 17 us -> none  [the longest x2 8.68 us: restrict(): jnp.einsum('pxyz,cxykz->ckp', coarse_basis, field, precision=precise)]
    reshape x8 -> x0, local copies, waits for them, and re-layouts: 16.8 us -> none  [the longest x2 13 us: per_device(): coarse_inverse.reshape(12, 8, 4, 2, 4, 2, 12).transpose(2, 3, 4, 1, 5, 6, 0)]
    ppermute x8, waiting for transfers between devices: 11 us -> 24 us  [neighbours(): return (lax.ppermute(high, axes, up), lax.ppermute(low, axes, down))]
    all_to_all x4 -> x2, waiting for transfers between devices: 17.2 us -> 5.06 us  [exchange(): return lax.all_to_all(spread, axes, 0, 0, tiled=True)]
    pallas_call x0 -> x7, Pallas kernels: none -> 11.7 us  [local_call(): pl.pallas_call(body, out_shape=[jax.ShapeDtypeStruct(shape, f32) for shap...]
    ppermute x8, starting transfers between devices: 42.9 us -> 32.3 us  [neighbours(): return (lax.ppermute(high, axes, up), lax.ppermute(low, axes, down))]
  transfers between devices with their start and end apart: 12 -> 10, of which waited for: 4 -> 4; matrix products, arithmetic and copies ran while one was open for 24% -> 0% of each run, Pallas kernels for 0% -> 4%
where the time goes in v2:
time: 146 us; the launch traced here: 145 us
  starting transfers between devices  50.7 us (35%)
  blocking collectives  42.9 us (29%)
  waiting for transfers between devices  29.1 us (20%)
  Pallas kernels  11.7 us (8%)
  local copies, waits for them, and re-layouts  9.72 us (7%)
    all_to_all x2, blocking collectives, exchange(): return lax.all_to_all(spread, axes, 0, 0, tiled=True)  42.9 us
    ppermute x8, starting transfers between devices, neighbours(): return (lax.ppermute(high, axes, up), lax.ppermute(low, axes, down))  32.3 us
    ppermute x8, waiting for transfers between devices, neighbours(): return (lax.ppermute(high, axes, up), lax.ppermute(low, axes, down))  24 us
    all_to_all x2, starting transfers between devices, exchange(): return lax.all_to_all(spread, axes, 0, 0, tiled=True)  18.4 us
    pallas_call x7, Pallas kernels, local_call(): pl.pallas_call(body, out_shape=[jax.ShapeDtypeStruct(shape, f32) for shap...  11.7 us
    unnamed x32, local copies, waits for them, and re-layouts  7.87 us
    all_to_all x2, waiting for transfers between devices, exchange(): return lax.all_to_all(spread, axes, 0, 0, tiled=True)  5.06 us
  transfers between devices with their start and end apart: 10, of which 4 were waited for; matrix products, arithmetic and copies ran while one was open for 0% of the time, Pallas kernels for 4%

profile of v2, /device:TPU:1, one launch (start us, length us, event | category | flops | bytes accessed | tf_op | source)
XLA Modules:
  0.0 144.9 jit_solution(120797493988259611)
XLA Ops:
  0.6 0.0 copy-start
  0.6 1.0 copy-done
  1.6 0.0 copy-start.11
  1.6 0.8 copy-done.11
  2.4 0.0 copy-start.2
  2.4 0.1 shard_map.138
  2.5 4.6 %collective-permute-start = (f32[4,3,8,128]{3,2,1,0:T(8,128)S(1)}, f32[4,3,8,128]{3,2,1,0:T(8,128)S(1)}, u32[]{:S(2)}, u32[]{:S(2)}) collective-permute-start(f32[4,3,8,128]{3,2,1,0:T(8,128)S(1)} %get-tuple-element.27), channel_id=1, source_target_pairs={{0,8},{8,16},{16,24},{24,32},{32,40},{40,48},{48,56},{56,64},{64,7... | collective-permute-start | bytes 147464 | tf_op jit(solution)/shard_map/ppermute | solution.py:337
  7.1 5.5 %collective-permute-start.1 = (f32[4,3,8,128]{3,2,1,0:T(8,128)S(1)}, f32[4,3,8,128]{3,2,1,0:T(8,128)S(1)}, u32[]{:S(2)}, u32[]{:S(2)}) collective-permute-start(f32[4,3,8,128]{3,2,1,0:T(8,128)S(1)} %get-tuple-element.28), channel_id=1, source_target_pairs={{8,0},{16,8},{24,16},{32,24},{40,32},{48,40},{56,48},{64,56},{72,6... | collective-permute-start | bytes 147464 | tf_op jit(solution)/shard_map/ppermute | solution.py:337
  12.7 11.8 %collective-permute-start.2 = (f32[96,128]{1,0:T(8,128)S(1)}, f32[96,128]{1,0:T(8,128)S(1)}, u32[]{:S(2)}, u32[]{:S(2)}) collective-permute-start(f32[96,128]{1,0:T(8,128)S(1)} %get-tuple-element.29), channel_id=1, source_target_pairs={{0,1},{1,2},{2,3},{3,4},{4,5},{5,6},{6,7},{8,9},{9,10},{10,11},{11... | collective-permute-start | bytes 147464 | tf_op jit(solution)/shard_map/ppermute | solution.py:337
  24.5 1.3 collective-permute-start.3
  25.8 0.0 copy-start.15
  25.8 0.0 copy-done.2
  25.8 0.7 copy-done.15
  26.5 0.0 copy-start.3
  26.5 0.9 copy-done.3
  27.4 0.0 copy-start.5
  27.4 1.1 copy-done.5
  28.4 0.0 copy-start.6
  28.4 1.1 copy-done.6
  29.5 0.0 copy-start.1
  29.5 0.0 copy-start.4
  29.5 0.0 copy-start.12
  29.5 0.0 copy-start.13
  29.5 5.2 %shard_map.139 = (f32[384,384]{1,0:T(8,128)S(1)}, f32[4,8,3,8,128]{4,3,2,1,0:T(8,128)S(1)}, f32[48,128]{1,0:T(8,128)S(1)}) custom-call(f32[4,8,3,8,128]{4,3,2,1,0:T(8,128)S(1)} %bitcast.22, f32[384,384]{1,0:T(8,128)S(1)} %bitcast.26, f32[384,384]{1,0:T(8,128)S(1)} %bitcast.27, s32[1,384]{1,0:T(1,128)S(1)} %bitcast.31, f32[4,8,8,128]{3,2,1,0:T(8,128)S(1)} %copy-done.3), custom_call_target="tpu_custom_call" | custom-call | tf_op jit(solution)/shard_map/pallas_call | solution.py:320
  34.7 0.0 collective-permute-done.below_x
  34.7 0.0 collective-permute-done.1.above_x
  34.8 0.0 collective-permute-done.2.below_y
  34.8 3.8 %collective-permute-done.3.above_y = f32[96,128]{1,0:T(8,128)S(1)} collective-permute-done((f32[96,128]{1,0:T(8,128)S(1)}, f32[96,128]{1,0:T(8,128)S(1)}, u32[]{:S(2)}, u32[]{:S(2)}) %collective-permute-start.3) | collective-permute-done | bytes 49184 | tf_op jit(solution)/shard_map/ppermute | solution.py:337
  38.6 0.0 copy-done.1
  38.6 0.0 copy-done.4
  38.6 0.0 copy-done.12
  38.6 0.0 copy-done.13
  38.6 2.1 %shard_map.140 = (f32[4,8,3,8,128]{4,3,2,1,0:T(8,128)S(1)}, f32[4,8,3,8,128]{4,3,2,1,0:T(8,128)S(1)}, f32[48,128]{1,0:T(8,128)S(1)}, f32[1,128]{1,0:T(1,128)S(1)...) custom-call(f32[4,8,3,8,128]{4,3,2,1,0:T(8,128)S(1)} %bitcast.19, ...), custom_call_target="tpu_custom_call" | custom-call | tf_op jit(solution)/shard_map/pallas_call | solution.py:320
  40.7 19.5 %all_to_all.20 = f32[16,1,128]{2,1,0:T(1,128)S(1)} all-to-all(f32[16,1,128]{2,1,0:T(1,128)S(1)} %broadcast_in_dim.30), channel_id=1, replica_groups=mesh['zl'=8,'x'=4,'c'=2,'y'=4,'zh'=2] {'zh','zl'}, dimensions={0} | all-to-all | bytes 16384 | tf_op jit(solution)/shard_map/all_to_all | solution.py:331
  60.2 0.7 broadcast_in_dim.32
  60.9 0.0 copy-start.10
  60.9 9.8 %all-to-all-start.1 = ((f32[32,16,128]{2,1,0:T(8,128)}), f32[32,16,128]{2,1,0:T(8,128)S(1)}, u32[]{:S(2)}, u32[]{:S(2)}) async-start(f32[32,16,128]{2,1,0:T(8,128)} %broadcast_in_dim.32), calls=%async_computation.1 | async-start | bytes 524288 | tf_op jit(solution)/shard_map/all_to_all | solution.py:331
  70.8 3.5 %collective-permute-start.4 = (f32[8,3,8,128]{3,2,1,0:T(8,128)}, f32[8,3,8,128]{3,2,1,0:T(8,128)S(1)}, u32[]{:S(2)}, u32[]{:S(2)}) collective-permute-start(f32[8,3,8,128]{3,2,1,0:T(8,128)} %get-tuple-element.38), channel_id=1, source_target_pairs={{0,8},{8,16},{16,24},{24,32},{32,40},{40,48},{48,56},{56,64},{64,7... | collective-permute-start | bytes 294920 | tf_op jit(solution)/shard_map/ppermute | solution.py:337
  74.3 1.9 %collective-permute-start.5 = (f32[8,3,8,128]{3,2,1,0:T(8,128)}, f32[8,3,8,128]{3,2,1,0:T(8,128)S(1)}, u32[]{:S(2)}, u32[]{:S(2)}) collective-permute-start(f32[8,3,8,128]{3,2,1,0:T(8,128)} %get-tuple-element.39), channel_id=1, source_target_pairs={{8,0},{16,8},{24,16},{32,24},{40,32},{48,40},{56,48},{64,56},{72,6... | collective-permute-start | bytes 294920 | tf_op jit(solution)/shard_map/ppermute | solution.py:337
  76.3 2.2 %collective-permute-start.6 = (f32[192,128]{1,0:T(8,128)}, f32[192,128]{1,0:T(8,128)S(1)}, u32[]{:S(2)}, u32[]{:S(2)}) collective-permute-start(f32[192,128]{1,0:T(8,128)} %get-tuple-element.40), channel_id=1, source_target_pairs={{0,1},{1,2},{2,3},{3,4},{4,5},{5,6},{6,7},{8,9},{9,10},{10,11},{11... | collective-permute-start | bytes 294920 | tf_op jit(solution)/shard_map/ppermute | solution.py:337
  78.5 1.3 collective-permute-start.7
  79.8 0.0 copy-done.10
  79.9 0.0 collective-permute-done.4.below_x
  79.9 0.6 collective-permute-done.5.above_x
  80.5 0.0 collective-permute-done.6.below_y
  80.5 19.6 %collective-permute-done.7.above_y = f32[192,128]{1,0:T(8,128)S(1)} collective-permute-done((f32[192,128]{1,0:T(8,128)S(1)}, f32[192,128]{1,0:T(8,128)S(1)}, u32[]{:S(2)}, u32[]{:S(2)}) %collective-permute-start.7) | collective-permute-done | bytes 98336 | tf_op jit(solution)/shard_map/ppermute | solution.py:337
  100.1 0.0 all-to-all-done.1
  100.1 0.0 copy-start.14
  100.1 0.7 copy-done.14
  100.7 0.0 copy-start.7
  100.7 1.8 %shard_map.142 = (f32[1,128]{1,0:T(1,128)S(1)}, f32[4,128]{1,0:T(4,128)S(1)}, f32[48,128]{1,0:T(8,128)S(1)}) custom-call(f32[4]{0:T(128)S(1)} %copy-done.14, f32[512,128]{1,0:T(8,128)S(1)} %bitcast.25, f32[12,2,8,384]{3,2,1,0:T(8,128)S(1)} %shard_map.141.inverse, f32[48,128]{1,0:T(8,128)S(1)} %get-tuple-element.33.primal_r, ...), custom_call_target="tpu_custom_call" | custom-call | tf_op jit(solution)/shard_map/pallas_call | solution.py:320
  102.5 23.4 %all_to_all.21 = f32[16,1,128]{2,1,0:T(1,128)S(1)} all-to-all(f32[16,1,128]{2,1,0:T(1,128)S(1)} %broadcast_in_dim.34), channel_id=1, replica_groups=mesh['zl'=8,'x'=4,'c'=2,'y'=4,'zh'=2] {'zh','zl'}, dimensions={0} | all-to-all | bytes 16384 | tf_op jit(solution)/shard_map/all_to_all | solution.py:331
  125.9 0.6 broadcast_in_dim.35
  126.5 8.5 %all-to-all-start.3 = ((f32[32,1,128]{2,1,0:T(1,128)}), f32[32,1,128]{2,1,0:T(1,128)S(1)}, u32[]{:S(2)}, u32[]{:S(2)}) async-start(f32[32,1,128]{2,1,0:T(1,128)} %broadcast_in_dim.35), calls=%async_computation.3 | async-start | bytes 32768 | tf_op jit(solution)/shard_map/all_to_all | solution.py:331
  135.1 0.0 copy-done.7
  135.1 1.1 shard_map.143
  136.2 0.0 copy-start.8
  136.2 0.7 copy-done.8
  136.9 5.1 %all-to-all-done.3 = f32[32,1,128]{2,1,0:T(1,128)S(1)} async-done(((f32[32,1,128]{2,1,0:T(1,128)}), f32[32,1,128]{2,1,0:T(1,128)S(1)}, u32[]{:S(2)}, u32[]{:S(2)}) %all-to-all-start.3) | async-done | bytes 16416 | tf_op jit(solution)/shard_map/all_to_all | solution.py:331
  142.0 0.0 copy-start.9
  142.0 1.0 copy-done.9
  143.0 1.4 shard_map.144
  144.4 0.5 slice_bitcast_fusion
  (4 shorter events, 0.1 us)
Async XLA Ops:
  0.6 1.0 copy-start
  1.6 0.8 copy-start.11
  2.4 23.4 %copy-start.2 = (f32[4,8,8,3,128]{4,2,3,1,0:T(8,128)S(1)}, f32[4,8,8,3,128]{4,2,3,1,0:T(8,128)}, u32[]{:S(2)}) copy-start(f32[4,8,8,3,128]{4,2,3,1,0:T(8,128)} %param.12) | copy-start | bytes 1179652
  2.5 32.3 %collective-permute-start = (f32[4,3,8,128]{3,2,1,0:T(8,128)S(1)}, f32[4,3,8,128]{3,2,1,0:T(8,128)S(1)}, u32[]{:S(2)}, u32[]{:S(2)}) collective-permute-start(f32[4,3,8,128]{3,2,1,0:T(8,128)S(1)} %get-tuple-element.27), channel_id=1, source_target_pairs={{0,8},{8,16},{16,24},{24,32},{32,40},{40,48},{48,56},{56,64},{64,7... | collective-permute-start | bytes 147464 | tf_op jit(solution)/shard_map/ppermute | solution.py:337
  7.1 27.6 %collective-permute-start.1 = (f32[4,3,8,128]{3,2,1,0:T(8,128)S(1)}, f32[4,3,8,128]{3,2,1,0:T(8,128)S(1)}, u32[]{:S(2)}, u32[]{:S(2)}) collective-permute-start(f32[4,3,8,128]{3,2,1,0:T(8,128)S(1)} %get-tuple-element.28), channel_id=1, source_target_pairs={{8,0},{16,8},{24,16},{32,24},{40,32},{48,40},{56,48},{64,56},{72,6... | collective-permute-start | bytes 147464 | tf_op jit(solution)/shard_map/ppermute | solution.py:337
  12.7 22.1 %collective-permute-start.2 = (f32[96,128]{1,0:T(8,128)S(1)}, f32[96,128]{1,0:T(8,128)S(1)}, u32[]{:S(2)}, u32[]{:S(2)}) collective-permute-start(f32[96,128]{1,0:T(8,128)S(1)} %get-tuple-element.29), channel_id=1, source_target_pairs={{0,1},{1,2},{2,3},{3,4},{4,5},{5,6},{6,7},{8,9},{9,10},{10,11},{11... | collective-permute-start | bytes 147464 | tf_op jit(solution)/shard_map/ppermute | solution.py:337
  24.5 14.1 %collective-permute-start.3 = (f32[96,128]{1,0:T(8,128)S(1)}, f32[96,128]{1,0:T(8,128)S(1)}, u32[]{:S(2)}, u32[]{:S(2)}) collective-permute-start(f32[96,128]{1,0:T(8,128)S(1)} %get-tuple-element.30), channel_id=1, source_target_pairs={{1,0},{2,1},{3,2},{4,3},{5,4},{6,5},{7,6},{9,8},{10,9},{11,10},{12... | collective-permute-start | bytes 147464 | tf_op jit(solution)/shard_map/ppermute | solution.py:337
  25.8 0.7 copy-start.15
  26.5 0.9 copy-start.3
  27.4 1.1 copy-start.5
  28.4 1.1 copy-start.6
  29.5 9.1 %copy-start.1 = (f32[4,8,8,3,128]{4,2,3,1,0:T(8,128)S(1)}, f32[4,8,8,3,128]{4,2,3,1,0:T(8,128)}, u32[]{:S(2)}) copy-start(f32[4,8,8,3,128]{4,2,3,1,0:T(8,128)} %param.13) | copy-start | bytes 1179652
  29.5 9.1 %copy-start.4 = (f32[4,8,8,128]{3,2,1,0:T(8,128)S(1)}, f32[4,8,8,128]{3,2,1,0:T(8,128)}, u32[]{:S(2)}) copy-start(f32[4,8,8,128]{3,2,1,0:T(8,128)} %basis.5) | copy-start | bytes 393220
  29.5 9.1 %copy-start.12 = (f32[8,8,128]{2,1,0:T(8,128)S(1)}, f32[8,8,128]{2,1,0:T(8,128)}, u32[]{:S(2)}) copy-start(f32[8,8,128]{2,1,0:T(8,128)} %stiffness.3) | copy-start | bytes 98308
  29.5 9.1 %copy-start.13 = (f32[8,8,128]{2,1,0:T(8,128)S(1)}, f32[8,8,128]{2,1,0:T(8,128)}, u32[]{:S(2)}) copy-start(f32[8,8,128]{2,1,0:T(8,128)} %coupling.1) | copy-start | bytes 98308
  60.9 18.9 %copy-start.10 = (f32[1,1,12,6144]{3,1,2,0:T(1,128)S(1)}, f32[1,1,12,6144]{3,1,2,0:T(1,128)}, u32[]{:S(2)}) copy-start(f32[1,1,12,6144]{3,1,2,0:T(1,128)} %param.20) | copy-start | bytes 884740
  60.9 39.1 %all-to-all-start.1 = ((f32[32,16,128]{2,1,0:T(8,128)}), f32[32,16,128]{2,1,0:T(8,128)S(1)}, u32[]{:S(2)}, u32[]{:S(2)}) async-start(f32[32,16,128]{2,1,0:T(8,128)} %broadcast_in_dim.32), calls=%async_computation.1 | async-start | bytes 524288 | tf_op jit(solution)/shard_map/all_to_all | solution.py:331
  70.8 9.1 %collective-permute-start.4 = (f32[8,3,8,128]{3,2,1,0:T(8,128)}, f32[8,3,8,128]{3,2,1,0:T(8,128)S(1)}, u32[]{:S(2)}, u32[]{:S(2)}) collective-permute-start(f32[8,3,8,128]{3,2,1,0:T(8,128)} %get-tuple-element.38), channel_id=1, source_target_pairs={{0,8},{8,16},{16,24},{24,32},{32,40},{40,48},{48,56},{56,64},{64,7... | collective-permute-start | bytes 294920 | tf_op jit(solution)/shard_map/ppermute | solution.py:337
  74.3 6.1 %collective-permute-start.5 = (f32[8,3,8,128]{3,2,1,0:T(8,128)}, f32[8,3,8,128]{3,2,1,0:T(8,128)S(1)}, u32[]{:S(2)}, u32[]{:S(2)}) collective-permute-start(f32[8,3,8,128]{3,2,1,0:T(8,128)} %get-tuple-element.39), channel_id=1, source_target_pairs={{8,0},{16,8},{24,16},{32,24},{40,32},{48,40},{56,48},{64,56},{72,6... | collective-permute-start | bytes 294920 | tf_op jit(solution)/shard_map/ppermute | solution.py:337
  76.3 4.2 %collective-permute-start.6 = (f32[192,128]{1,0:T(8,128)}, f32[192,128]{1,0:T(8,128)S(1)}, u32[]{:S(2)}, u32[]{:S(2)}) collective-permute-start(f32[192,128]{1,0:T(8,128)} %get-tuple-element.40), channel_id=1, source_target_pairs={{0,1},{1,2},{2,3},{3,4},{4,5},{5,6},{6,7},{8,9},{9,10},{10,11},{11... | collective-permute-start | bytes 294920 | tf_op jit(solution)/shard_map/ppermute | solution.py:337
  78.5 21.5 %collective-permute-start.7 = (f32[192,128]{1,0:T(8,128)S(1)}, f32[192,128]{1,0:T(8,128)S(1)}, u32[]{:S(2)}, u32[]{:S(2)}) collective-permute-start(f32[192,128]{1,0:T(8,128)S(1)} %get-tuple-element.41), channel_id=1, source_target_pairs={{1,0},{2,1},{3,2},{4,3},{5,4},{6,5},{7,6},{9,8},{10,9},{11,10},{12... | collective-permute-start | bytes 294920 | tf_op jit(solution)/shard_map/ppermute | solution.py:337
  100.1 0.7 copy-start.14
  100.7 34.3 %copy-start.7 = (f32[4,8,8,3,128]{4,2,3,1,0:T(8,128)S(1)}, f32[4,8,8,3,128]{4,2,3,1,0:T(8,128)}, u32[]{:S(2)}) copy-start(f32[4,8,8,3,128]{4,2,3,1,0:T(8,128)} %param.11) | copy-start | bytes 1179652
  126.5 15.5 %all-to-all-start.3 = ((f32[32,1,128]{2,1,0:T(1,128)}), f32[32,1,128]{2,1,0:T(1,128)S(1)}, u32[]{:S(2)}, u32[]{:S(2)}) async-start(f32[32,1,128]{2,1,0:T(1,128)} %broadcast_in_dim.35), calls=%async_computation.3 | async-start | bytes 32768 | tf_op jit(solution)/shard_map/all_to_all | solution.py:331
  136.2 0.7 copy-start.8
  142.0 1.0 copy-start.9

commit v3 on v2

--- a/solution.py
+++ b/solution.py
@@ -50,9 +50,15 @@
     return (small + (mxu(a0, b1, dims) + mxu(a1, b0, dims))) + mxu(a0, b0, dims)
 
 
+def product_of_halves(a, b, dims):
+    a0, a1 = halves(a)
+    b0, b1 = halves(b)
+    return (mxu(a0, b1, dims) + mxu(a1, b0, dims)) + mxu(a0, b0, dims)
+
+
 def picked(chosen, b, dims):
-    b0, b1, b2 = thirds(b)
-    return (mxu(chosen, b2, dims) + mxu(chosen, b1, dims)) + mxu(chosen, b0, dims)
+    high, low = halves(b)
+    return mxu(chosen, low, dims) + mxu(chosen, high, dims)
 
 
 def lane_sums(a):
@@ -100,7 +106,17 @@
                 out_ref[row : row + 1, :] = ref[c, x, k, y : y + 1, :]
 
 
-def faces_kernel(direction, stiffness, low_x, high_x, low_y, high_y):
+def faces_kernel(
+    direction_hbm, stiffness_hbm, low_x, high_x, low_y, high_y, direction, stiffness, sems
+):
+    copies = [
+        pltpu.make_async_copy(direction_hbm, direction, sems.at[0]),
+        pltpu.make_async_copy(stiffness_hbm, stiffness, sems.at[1]),
+    ]
+    for copy in copies:
+        copy.start()
+    for copy in copies:
+        copy.wait()
     for x, out in ((0, low_x), (NX - 1, high_x)):
         out[...] = direction[:, x] * stiffness[x][None, None]
     for y, out in ((0, low_y), (NY - 1, high_y)):
@@ -113,14 +129,30 @@
                     )
 
 
-def prepare_kernel(residual, lower, upper, pivots, basis, operator, solved, primal):
-    order = pivots[...]
+def prepare_kernel(
+    prior, residual, lower_hbm, upper_hbm, pivots_hbm, basis_hbm,
+    operator, solved, primal, prior_rows,
+    lower, upper, pivots, basis, sems,
+):
+    pairs = ((upper_hbm, upper), (lower_hbm, lower), (pivots_hbm, pivots), (basis_hbm, basis))
+    copies = [
+        pltpu.make_async_copy(source, target, sems.at[i])
+        for i, (source, target) in enumerate(pairs)
+    ]
+    for copy in copies:
+        copy.start()
+    for c in range(CASES):
+        prior_rows[c : c + 1, :] = jnp.full((1, 128), prior[c], f32)
+    copies[0].wait()
+    copies[1].wait()
+    both = product_of_halves(upper[...], lower[...], NN)
+    copies[2].wait()
     at = lax.broadcasted_iota(jnp.int32, (LINE, LINE), 0)
-    chosen = jnp.where(at == order, 1.0, 0.0).astype(bf16)
-    both = product(upper[...], lower[...], NN)
+    chosen = jnp.where(at == pivots[...], 1.0, 0.0).astype(bf16)
     rows = picked(chosen, both, NN)
     operator[...] = picked(chosen, rows, NT)
     local_solve(residual, operator, solved)
+    copies[3].wait()
     primal[...] = lane_sums(restricted(basis, residual))
 
 
@@ -183,7 +215,7 @@
     lane = lax.broadcasted_iota(jnp.int32, (48, 128), 1)
     sub = lax.broadcasted_iota(jnp.int32, (48, 128), 0)
     first = jnp.sum(jnp.where(lane == sub, primal_r[...], 0.0), axis=0, keepdims=True)
-    row[...] = first + pltpu.roll(mine_row, 48, 1)
+    row[...] = jnp.broadcast_to((first + pltpu.roll(mine_row, 48, 1))[None], (N_DEPTH, 1, 128))
     for source, base in ((solved_r, 0), (solved, CASES)):
         low_x[base : base + CASES] = source[:, 0]
         high_x[base : base + CASES] = source[:, NX - 1]
@@ -197,7 +229,7 @@
     steps = []
     for c in range(CASES):
         curvature = jnp.sum(jnp.where(lane == 96 + c, total, 0.0), axis=1, keepdims=True)
-        steps.append(jnp.broadcast_to(prior[c] / curvature, (1, 128)))
+        steps.append(prior[c : c + 1, :] / jnp.broadcast_to(curvature, (1, 128)))
     return steps
 
 
@@ -274,21 +306,30 @@
         sums.append(
             jnp.sum(total, axis=0, keepdims=True) + jnp.where(lane == 0, both, 0.0)
         )
-    row[...] = lane_row(jnp.concatenate(sums, axis=0))
-
-
-def update_kernel(
-    steps, coarse, basis, solution, residual, direction, applied, solved_r, solved_w,
-    below_x, above_x, below_y, above_y,
-    solution_next, residual_next, preconditioned,
-):
-    y_at = lax.broadcasted_iota(jnp.int32, (NY, NZ), 0)
+    row[...] = jnp.broadcast_to(
+        lane_row(jnp.concatenate(sums, axis=0))[None], (N_DEPTH, 1, 128)
+    )
+
+
+def advance_kernel(
+    steps, solution, residual, direction, applied, solution_next, residual_next
+):
     for c in range(CASES):
         step = steps[c : c + 1, :]
         for x in range(NX):
             for k in range(COMP):
                 residual_next[c, x, k] = residual[c, x, k] - step * applied[c, x, k]
                 solution_next[c, x, k] = solution[c, x, k] + step * direction[c, x, k]
+
+
+def precondition_kernel(
+    steps, coarse, basis, solved_r, solved_w, below_x, above_x, below_y, above_y, preconditioned
+):
+    y_at = lax.broadcasted_iota(jnp.int32, (NY, NZ), 0)
+    for c in range(CASES):
+        step = steps[c : c + 1, :]
+        for x in range(NX):
+            for k in range(COMP):
                 out = smoothed_at(
                     c, x, k, step, solved_r, solved_w, below_x, above_x, below_y, above_y, y_at
                 )
@@ -300,11 +341,11 @@
 
 def final_kernel(prior, parts, preconditioned, direction, direction_next, inner):
     total = jnp.sum(parts[...], axis=0, keepdims=True)
-    inner[...] = total
+    inner[...] = total[0, :CASES]
     lane = lax.broadcasted_iota(jnp.int32, (1, 128), 1)
     for c in range(CASES):
         mine = jnp.sum(jnp.where(lane == c, total, 0.0), axis=1, keepdims=True)
-        growth = jnp.broadcast_to(mine / prior[c], (1, NZ))
+        growth = jnp.broadcast_to(mine, (1, NZ)) / prior[c : c + 1, :]
         for x in range(NX):
             for k in range(COMP):
                 direction_next[c, x, k] = (
@@ -314,21 +355,32 @@
 
 VMEM = pl.BlockSpec(memory_space=pltpu.VMEM)
 SMEM = pl.BlockSpec(memory_space=pltpu.SMEM)
-
-
-def local_call(body, outs, scalars, *args):
+HBM = pl.BlockSpec(memory_space=pltpu.HBM)
+
+
+def local_call(body, outs, spaces, *args, scratch=()):
+    specs = [{"s": SMEM, "v": VMEM, "h": HBM}[space] for space in spaces]
+    specs += [VMEM] * (len(args) - len(specs))
+    args = tuple(
+        pltpu.with_memory_space_constraint(arg, pltpu.HBM) if spec is HBM else arg
+        for arg, spec in zip(args, specs)
+    )
     return pl.pallas_call(
         body,
         out_shape=[jax.ShapeDtypeStruct(shape, f32) for shape in outs],
-        in_specs=[SMEM] * scalars + [VMEM] * (len(args) - scalars),
+        in_specs=specs,
         out_specs=[VMEM] * len(outs),
-        compiler_params=pltpu.CompilerParams(vmem_limit_bytes=40 << 20),
+        scratch_shapes=list(scratch),
+        compiler_params=pltpu.CompilerParams(vmem_limit_bytes=20 << 20),
     )(*args)
 
 
-def exchange(block, axes, count):
-    spread = jnp.broadcast_to(block[None], (count,) + block.shape)
-    return lax.all_to_all(spread, axes, 0, 0, tiled=True)
+def spread(block, count):
+    return jnp.broadcast_to(block[None], (count,) + block.shape)
+
+
+def exchange(rows, axes):
+    return lax.all_to_all(rows, axes, 0, 0, tiled=True)
 
 
 def neighbours(low, high, axes, count):
@@ -347,55 +399,69 @@
     end_x = (CASES, COMP, NY, NZ)
     end_y = (TILES, NZ)
     low_x, high_x, low_y, high_y = local_call(
-        faces_kernel, [end_x, end_x, end_y, end_y], 0, direction, stiffness
+        faces_kernel, [end_x, end_x, end_y, end_y], "hh", direction, stiffness,
+        scratch=[
+            pltpu.VMEM(FIELD, f32), pltpu.VMEM((NX, NY, NZ), f32), pltpu.SemaphoreType.DMA((2,)),
+        ],
     )
     below_y, above_y = neighbours(low_y, high_y, YZ_AXES, N_YZ)
     below_x, above_x = neighbours(low_x, high_x, GX_AXES, N_GX)
 
-    operator, solved_r, primal_r = local_call(
-        prepare_kernel, [(LINE, LINE), FIELD, (48, 128)], 0,
-        residual, lower_factor[0, 0], upper_factor[0, 0], pivot_order[0], coarse_basis,
+    operator, solved_r, primal_r, prior_rows = local_call(
+        prepare_kernel, [(LINE, LINE), FIELD, (48, 128), (CASES, 128)], "svhhhh",
+        inner_prior, residual, lower_factor[0, 0], upper_factor[0, 0], pivot_order[0],
+        coarse_basis,
+        scratch=[
+            pltpu.VMEM((LINE, LINE), f32), pltpu.VMEM((LINE, LINE), f32),
+            pltpu.VMEM((1, LINE), jnp.int32), pltpu.VMEM((NP, NX, NY, NZ), f32),
+            pltpu.SemaphoreType.DMA((4,)),
+        ],
     )
 
     twice_x = (2 * CASES, COMP, NY, NZ)
     twice_y = (2 * TILES, NZ)
-    applied, solved_w, primal_w, row, low_x, high_x, low_y, high_y = local_call(
+    rows_z = (N_DEPTH, 1, 128)
+    applied, solved_w, primal_w, rows, low_x, high_x, low_y, high_y = local_call(
         applied_kernel,
-        [FIELD, FIELD, (48, 128), (1, 128), twice_x, twice_x, twice_y, twice_y], 0,
+        [FIELD, FIELD, (48, 128), rows_z, twice_x, twice_x, twice_y, twice_y], "",
         direction, stiffness, coupling, below_x, above_x, below_y, above_y,
         coarse_basis, operator, solved_r, primal_r,
     )
 
-    line = exchange(row, DEPTH, N_DEPTH)
+    line = exchange(rows, DEPTH)
     below_y, above_y = neighbours(low_y, high_y, YZ_AXES, N_YZ)
     below_x, above_x = neighbours(low_x, high_x, GX_AXES, N_GX)
     (inverse,) = local_call(
-        by_depth_kernel, [(PRIMAL, 2, 8, LINE)], 0,
+        by_depth_kernel, [(PRIMAL, 2, 8, LINE)], "",
         coarse_inverse.reshape(PRIMAL * 48, 128),
     )
-    table = exchange(line.reshape(N_DEPTH, 128), PLANE, N_PLANE)
+    table = exchange(spread(line.reshape(N_DEPTH, 128), N_PLANE), PLANE)
     table = table.reshape(N_PLANE * N_DEPTH, 128)
 
-    inner_row, steps, coarse = local_call(
-        coarse_kernel, [(1, 128), (CASES, 128), (48, 128)], 1,
-        inner_prior, table, inverse, primal_r, primal_w, residual, applied, solved_r, solved_w,
-        below_x, above_x, below_y, above_y,
-    )
-    line = exchange(inner_row, DEPTH, N_DEPTH)
-    solution_next, residual_next, preconditioned = local_call(
-        update_kernel, [FIELD, FIELD, FIELD], 0,
-        steps, coarse, coarse_basis, solution, residual, direction, applied,
-        solved_r, solved_w, below_x, above_x, below_y, above_y,
-    )
-    parts = exchange(jnp.sum(line, axis=0), PLANE, N_PLANE)
+    halo = (below_x, above_x, below_y, above_y)
+    rows, steps, coarse = local_call(
+        coarse_kernel, [rows_z, (CASES, 128), (48, 128)], "",
+        prior_rows, table, inverse, primal_r, primal_w, residual, applied, solved_r, solved_w,
+        *halo,
+    )
+    line = exchange(rows, DEPTH)
+    solution_next, residual_next = local_call(
+        advance_kernel, [FIELD, FIELD], "",
+        steps, solution, residual, direction, applied,
+    )
+    parts = exchange(spread(jnp.sum(line, axis=0), N_PLANE), PLANE)
+    (preconditioned,) = local_call(
+        precondition_kernel, [FIELD], "",
+        steps, coarse, coarse_basis, solved_r, solved_w, *halo,
+    )
     direction_next, inner = local_call(
-        final_kernel, [FIELD, (1, 128)], 1,
-        inner_prior, parts.reshape(N_PLANE, 128), preconditioned, direction,
+        final_kernel, [FIELD, (CASES,)], "",
+        prior_rows, parts.reshape(N_PLANE, 128), preconditioned, direction,
     )
     solution_next, residual_next, direction_next = (
         a.transpose(0, 1, 3, 2, 4) for a in (solution_next, residual_next, direction_next)
     )
-    return (solution_next, residual_next, direction_next, inner[0, :CASES])
+    return (solution_next, residual_next, direction_next, inner)
 
 
 def solution(mesh):

time: 146 us -> 139 us (0.952)
  local copies, waits for them, and re-layouts: 9.72 us -> 2 us
  waiting for transfers between devices: 29.1 us -> 32.3 us
  blocking collectives: 42.9 us -> 40.2 us
    unnamed x32 -> x16, local copies, waits for them, and re-layouts: 7.87 us -> 0.67 us
    all_to_all x2, blocking collectives: 42.9 us -> 40.2 us  [exchange(): return lax.all_to_all(rows, axes, 0, 0, tiled=True)]
    ppermute x8, waiting for transfers between devices: 24 us -> 26.7 us  [neighbours(): return (lax.ppermute(high, axes, up), lax.ppermute(low, axes, down))]
    pallas_call x7 -> x8, Pallas kernels: 11.7 us -> 12.2 us  [local_call(): pl.pallas_call(body, out_shape=[jax.ShapeDtypeStruct(shape, f32) for shap...]
  transfers between devices with their start and end apart: 10 -> 10, of which waited for: 4 -> 4; matrix products, arithmetic and copies ran while one was open for 0% -> 0% of each run, Pallas kernels for 4% -> 5%
where the time goes in v3:
time: 139 us
  starting transfers between devices  51.4 us (37%)
  blocking collectives  40.2 us (29%)
  waiting for transfers between devices  32.3 us (23%)
  Pallas kernels  12.2 us (9%)
  local copies, waits for them, and re-layouts  2 us (1%)
    all_to_all x2, blocking collectives, exchange(): return lax.all_to_all(rows, axes, 0, 0, tiled=True)  40.2 us
    ppermute x8, starting transfers between devices, neighbours(): return (lax.ppermute(high, axes, up), lax.ppermute(low, axes, down))  32.2 us
    ppermute x8, waiting for transfers between devices, neighbours(): return (lax.ppermute(high, axes, up), lax.ppermute(low, axes, down))  26.7 us
    all_to_all x2, starting transfers between devices, exchange(): return lax.all_to_all(rows, axes, 0, 0, tiled=True)  19.2 us
    pallas_call x8, Pallas kernels, local_call(): pl.pallas_call(body, out_shape=[jax.ShapeDtypeStruct(shape, f32) for shap...  12.2 us
    all_to_all x2, waiting for transfers between devices, exchange(): return lax.all_to_all(rows, axes, 0, 0, tiled=True)  5.62 us
  transfers between devices with their start and end apart: 10, of which 4 were waited for; matrix products, arithmetic and copies ran while one was open for 0% of the time, Pallas kernels for 5%

profile of v3, /device:TPU:1, one launch (start us, length us, event | category | flops | bytes accessed | tf_op | source)
XLA Modules:
  0.0 138.9 jit_solution(9881146787575394173)
XLA Ops:
  0.6 0.0 copy-start.1
  0.6 1.1 shard_map.139
  1.8 4.5 %collective-permute-start = (f32[4,3,8,128]{3,2,1,0:T(8,128)S(1)}, f32[4,3,8,128]{3,2,1,0:T(8,128)S(1)}, u32[]{:S(2)}, u32[]{:S(2)}) collective-permute-start(f32[4,3,8,128]{3,2,1,0:T(8,128)S(1)} %get-tuple-element.28), channel_id=1, source_target_pairs={{0,8},{8,16},{16,24},{24,32},{32,40},{40,48},{48,56},{56,64},{64,7... | collective-permute-start | bytes 147464 | tf_op jit(solution)/shard_map/ppermute | solution.py:389
  6.3 5.5 %collective-permute-start.1 = (f32[4,3,8,128]{3,2,1,0:T(8,128)S(1)}, f32[4,3,8,128]{3,2,1,0:T(8,128)S(1)}, u32[]{:S(2)}, u32[]{:S(2)}) collective-permute-start(f32[4,3,8,128]{3,2,1,0:T(8,128)S(1)} %get-tuple-element.29), channel_id=1, source_target_pairs={{8,0},{16,8},{24,16},{32,24},{40,32},{48,40},{56,48},{64,56},{72,6... | collective-permute-start | bytes 147464 | tf_op jit(solution)/shard_map/ppermute | solution.py:389
  11.8 11.8 %collective-permute-start.2 = (f32[96,128]{1,0:T(8,128)S(1)}, f32[96,128]{1,0:T(8,128)S(1)}, u32[]{:S(2)}, u32[]{:S(2)}) collective-permute-start(f32[96,128]{1,0:T(8,128)S(1)} %get-tuple-element.30), channel_id=1, source_target_pairs={{0,1},{1,2},{2,3},{3,4},{4,5},{5,6},{6,7},{8,9},{9,10},{10,11},{11... | collective-permute-start | bytes 147464 | tf_op jit(solution)/shard_map/ppermute | solution.py:389
  23.7 1.3 collective-permute-start.3
  25.0 0.0 copy-start.7
  25.0 0.0 copy-done.1
  25.0 0.6 copy-done.7
  25.6 0.0 copy-start
  25.6 0.0 copy-start.2
  25.6 0.0 copy-start.5
  25.6 0.0 copy-start.6
  25.6 5.5 %shard_map.138 = (f32[384,384]{1,0:T(8,128)S(1)}, f32[4,8,3,8,128]{4,3,2,1,0:T(8,128)S(1)}, f32[48,128]{1,0:T(8,128)S(1)}, f32[4,128]{1,0:T(4,128)S(1)}) custom-call(f32[4]{0:T(128)S(1)} %copy-done.7, f32[4,8,3,8,128]{4,3,2,1,0:T(8,128)S(1)} %bitcast.17, f32[384,384]{1,0:T(8,128)} %bitcast.24, f32[384,384]{1,0:T(8,128)} %bitcast.25, s32[1,384]{1,0:T(1,128)} %bitcast.27, ...), custom_call_target="tpu_custom_call" | custom-call | tf_op jit(solution)/shard_map/pallas_call | solution.py:368
  31.2 0.0 collective-permute-done.below_x
  31.2 0.0 collective-permute-done.1.above_x
  31.2 0.0 collective-permute-done.2.below_y
  31.2 6.5 %collective-permute-done.3.above_y = f32[96,128]{1,0:T(8,128)S(1)} collective-permute-done((f32[96,128]{1,0:T(8,128)S(1)}, f32[96,128]{1,0:T(8,128)S(1)}, u32[]{:S(2)}, u32[]{:S(2)}) %collective-permute-start.3) | collective-permute-done | bytes 49184 | tf_op jit(solution)/shard_map/ppermute | solution.py:389
  37.8 0.0 copy-done
  37.8 0.0 copy-done.2
  37.8 0.0 copy-done.5
  37.8 0.0 copy-done.6
  37.8 2.1 %shard_map.140 = (f32[4,8,3,8,128]{4,3,2,1,0:T(8,128)S(1)}, f32[4,8,3,8,128]{4,3,2,1,0:T(8,128)S(1)}, f32[48,128]{1,0:T(8,128)S(1)}, f32[16,1,128]{2,1,0:T(1,128...) custom-call(f32[4,8,3,8,128]{4,3,2,1,0:T(8,128)S(1)} %bitcast.14, ...), custom_call_target="tpu_custom_call" | custom-call | tf_op jit(solution)/shard_map/pallas_call | solution.py:368
  39.9 16.8 %all_to_all.20 = f32[16,1,128]{2,1,0:T(1,128)S(1)} all-to-all(f32[16,1,128]{2,1,0:T(1,128)S(1)} %get-tuple-element.35), channel_id=1, replica_groups=mesh['zl'=8,'x'=4,'c'=2,'y'=4,'zh'=2] {'zh','zl'}, dimensions={0} | all-to-all | bytes 16384 | tf_op jit(solution)/shard_map/all_to_all | solution.py:383
  56.7 0.7 broadcast_in_dim.14
  57.4 0.0 copy-start.4
  57.4 10.6 %all-to-all-start.1 = ((f32[32,16,128]{2,1,0:T(8,128)}), f32[32,16,128]{2,1,0:T(8,128)S(1)}, u32[]{:S(2)}, u32[]{:S(2)}) async-start(f32[32,16,128]{2,1,0:T(8,128)} %broadcast_in_dim.14), calls=%async_computation.1 | async-start | bytes 524288 | tf_op jit(solution)/shard_map/all_to_all | solution.py:383
  68.0 3.5 %collective-permute-start.4 = (f32[8,3,8,128]{3,2,1,0:T(8,128)}, f32[8,3,8,128]{3,2,1,0:T(8,128)S(1)}, u32[]{:S(2)}, u32[]{:S(2)}) collective-permute-start(f32[8,3,8,128]{3,2,1,0:T(8,128)} %get-tuple-element.39), channel_id=1, source_target_pairs={{0,8},{8,16},{16,24},{24,32},{32,40},{40,48},{48,56},{56,64},{64,7... | collective-permute-start | bytes 294920 | tf_op jit(solution)/shard_map/ppermute | solution.py:389
  71.5 1.9 %collective-permute-start.5 = (f32[8,3,8,128]{3,2,1,0:T(8,128)}, f32[8,3,8,128]{3,2,1,0:T(8,128)S(1)}, u32[]{:S(2)}, u32[]{:S(2)}) collective-permute-start(f32[8,3,8,128]{3,2,1,0:T(8,128)} %get-tuple-element.40), channel_id=1, source_target_pairs={{8,0},{16,8},{24,16},{32,24},{40,32},{48,40},{56,48},{64,56},{72,6... | collective-permute-start | bytes 294920 | tf_op jit(solution)/shard_map/ppermute | solution.py:389
  73.4 2.3 %collective-permute-start.6 = (f32[192,128]{1,0:T(8,128)}, f32[192,128]{1,0:T(8,128)S(1)}, u32[]{:S(2)}, u32[]{:S(2)}) collective-permute-start(f32[192,128]{1,0:T(8,128)} %get-tuple-element.41), channel_id=1, source_target_pairs={{0,1},{1,2},{2,3},{3,4},{4,5},{5,6},{6,7},{8,9},{9,10},{10,11},{11... | collective-permute-start | bytes 294920 | tf_op jit(solution)/shard_map/ppermute | solution.py:389
  75.7 1.3 collective-permute-start.7
  77.0 0.0 copy-done.4
  77.0 0.0 collective-permute-done.4.below_x
  77.1 0.6 collective-permute-done.5.above_x
  77.7 0.0 collective-permute-done.6.below_y
  77.7 19.5 %collective-permute-done.7.above_y = f32[192,128]{1,0:T(8,128)S(1)} collective-permute-done((f32[192,128]{1,0:T(8,128)S(1)}, f32[192,128]{1,0:T(8,128)S(1)}, u32[]{:S(2)}, u32[]{:S(2)}) %collective-permute-start.7) | collective-permute-done | bytes 98336 | tf_op jit(solution)/shard_map/ppermute | solution.py:389
  97.2 0.0 all-to-all-done.1
  97.2 0.0 copy-start.3
  97.2 1.2 shard_map.142
  98.4 23.4 %all_to_all.21 = f32[16,1,128]{2,1,0:T(1,128)S(1)} all-to-all(f32[16,1,128]{2,1,0:T(1,128)S(1)} %get-tuple-element.46), channel_id=1, replica_groups=mesh['zl'=8,'x'=4,'c'=2,'y'=4,'zh'=2] {'zh','zl'}, dimensions={0} | all-to-all | bytes 16384 | tf_op jit(solution)/shard_map/all_to_all | solution.py:383
  121.9 0.6 broadcast_in_dim.15
  122.5 8.6 %all-to-all-start.3 = ((f32[32,1,128]{2,1,0:T(1,128)}), f32[32,1,128]{2,1,0:T(1,128)S(1)}, u32[]{:S(2)}, u32[]{:S(2)}) async-start(f32[32,1,128]{2,1,0:T(1,128)} %broadcast_in_dim.15), calls=%async_computation.3 | async-start | bytes 32768 | tf_op jit(solution)/shard_map/all_to_all | solution.py:383
  131.1 0.0 copy-done.3
  131.2 1.0 shard_map.143
  132.1 0.3 shard_map.144.preconditioned
  132.4 5.6 %all-to-all-done.3 = f32[32,1,128]{2,1,0:T(1,128)S(1)} async-done(((f32[32,1,128]{2,1,0:T(1,128)}), f32[32,1,128]{2,1,0:T(1,128)S(1)}, u32[]{:S(2)}, u32[]{:S(2)}) %all-to-all-start.3) | async-done | bytes 16416 | tf_op jit(solution)/shard_map/all_to_all | solution.py:383
  138.0 0.9 shard_map.145
  (2 shorter events, 0.1 us)
Async XLA Ops:
  0.6 24.4 %copy-start.1 = (f32[4,8,8,3,128]{4,2,3,1,0:T(8,128)S(1)}, f32[4,8,8,3,128]{4,2,3,1,0:T(8,128)}, u32[]{:S(2)}) copy-start(f32[4,8,8,3,128]{4,2,3,1,0:T(8,128)} %param.12) | copy-start | bytes 1179652
  1.8 29.4 %collective-permute-start = (f32[4,3,8,128]{3,2,1,0:T(8,128)S(1)}, f32[4,3,8,128]{3,2,1,0:T(8,128)S(1)}, u32[]{:S(2)}, u32[]{:S(2)}) collective-permute-start(f32[4,3,8,128]{3,2,1,0:T(8,128)S(1)} %get-tuple-element.28), channel_id=1, source_target_pairs={{0,8},{8,16},{16,24},{24,32},{32,40},{40,48},{48,56},{56,64},{64,7... | collective-permute-start | bytes 147464 | tf_op jit(solution)/shard_map/ppermute | solution.py:389
  6.3 24.9 %collective-permute-start.1 = (f32[4,3,8,128]{3,2,1,0:T(8,128)S(1)}, f32[4,3,8,128]{3,2,1,0:T(8,128)S(1)}, u32[]{:S(2)}, u32[]{:S(2)}) collective-permute-start(f32[4,3,8,128]{3,2,1,0:T(8,128)S(1)} %get-tuple-element.29), channel_id=1, source_target_pairs={{8,0},{16,8},{24,16},{32,24},{40,32},{48,40},{56,48},{64,56},{72,6... | collective-permute-start | bytes 147464 | tf_op jit(solution)/shard_map/ppermute | solution.py:389
  11.8 19.4 %collective-permute-start.2 = (f32[96,128]{1,0:T(8,128)S(1)}, f32[96,128]{1,0:T(8,128)S(1)}, u32[]{:S(2)}, u32[]{:S(2)}) collective-permute-start(f32[96,128]{1,0:T(8,128)S(1)} %get-tuple-element.30), channel_id=1, source_target_pairs={{0,1},{1,2},{2,3},{3,4},{4,5},{5,6},{6,7},{8,9},{9,10},{10,11},{11... | collective-permute-start | bytes 147464 | tf_op jit(solution)/shard_map/ppermute | solution.py:389
  23.7 14.1 %collective-permute-start.3 = (f32[96,128]{1,0:T(8,128)S(1)}, f32[96,128]{1,0:T(8,128)S(1)}, u32[]{:S(2)}, u32[]{:S(2)}) collective-permute-start(f32[96,128]{1,0:T(8,128)S(1)} %get-tuple-element.31), channel_id=1, source_target_pairs={{1,0},{2,1},{3,2},{4,3},{5,4},{6,5},{7,6},{9,8},{10,9},{11,10},{12... | collective-permute-start | bytes 147464 | tf_op jit(solution)/shard_map/ppermute | solution.py:389
  25.0 0.7 copy-start.7
  25.6 12.1 %copy-start = (f32[4,8,8,3,128]{4,2,3,1,0:T(8,128)S(1)}, f32[4,8,8,3,128]{4,2,3,1,0:T(8,128)}, u32[]{:S(2)}) copy-start(f32[4,8,8,3,128]{4,2,3,1,0:T(8,128)} %param.13) | copy-start | bytes 1179652
  25.6 12.1 %copy-start.2 = (f32[4,8,8,128]{3,2,1,0:T(8,128)S(1)}, f32[4,8,8,128]{3,2,1,0:T(8,128)}, u32[]{:S(2)}) copy-start(f32[4,8,8,128]{3,2,1,0:T(8,128)} %basis.3) | copy-start | bytes 393220
  25.6 12.1 %copy-start.5 = (f32[8,8,128]{2,1,0:T(8,128)S(1)}, f32[8,8,128]{2,1,0:T(8,128)}, u32[]{:S(2)}) copy-start(f32[8,8,128]{2,1,0:T(8,128)} %stiffness.1) | copy-start | bytes 98308
  25.6 12.1 %copy-start.6 = (f32[8,8,128]{2,1,0:T(8,128)S(1)}, f32[8,8,128]{2,1,0:T(8,128)}, u32[]{:S(2)}) copy-start(f32[8,8,128]{2,1,0:T(8,128)} %coupling.1) | copy-start | bytes 98308
  57.4 19.6 %copy-start.4 = (f32[1,1,12,6144]{3,1,2,0:T(1,128)S(1)}, f32[1,1,12,6144]{3,1,2,0:T(1,128)}, u32[]{:S(2)}) copy-start(f32[1,1,12,6144]{3,1,2,0:T(1,128)} %param.20) | copy-start | bytes 884740
  57.4 39.8 %all-to-all-start.1 = ((f32[32,16,128]{2,1,0:T(8,128)}), f32[32,16,128]{2,1,0:T(8,128)S(1)}, u32[]{:S(2)}, u32[]{:S(2)}) async-start(f32[32,16,128]{2,1,0:T(8,128)} %broadcast_in_dim.14), calls=%async_computation.1 | async-start | bytes 524288 | tf_op jit(solution)/shard_map/all_to_all | solution.py:383
  68.0 9.1 %collective-permute-start.4 = (f32[8,3,8,128]{3,2,1,0:T(8,128)}, f32[8,3,8,128]{3,2,1,0:T(8,128)S(1)}, u32[]{:S(2)}, u32[]{:S(2)}) collective-permute-start(f32[8,3,8,128]{3,2,1,0:T(8,128)} %get-tuple-element.39), channel_id=1, source_target_pairs={{0,8},{8,16},{16,24},{24,32},{32,40},{40,48},{48,56},{56,64},{64,7... | collective-permute-start | bytes 294920 | tf_op jit(solution)/shard_map/ppermute | solution.py:389
  71.5 6.1 %collective-permute-start.5 = (f32[8,3,8,128]{3,2,1,0:T(8,128)}, f32[8,3,8,128]{3,2,1,0:T(8,128)S(1)}, u32[]{:S(2)}, u32[]{:S(2)}) collective-permute-start(f32[8,3,8,128]{3,2,1,0:T(8,128)} %get-tuple-element.40), channel_id=1, source_target_pairs={{8,0},{16,8},{24,16},{32,24},{40,32},{48,40},{56,48},{64,56},{72,6... | collective-permute-start | bytes 294920 | tf_op jit(solution)/shard_map/ppermute | solution.py:389
  73.4 4.2 %collective-permute-start.6 = (f32[192,128]{1,0:T(8,128)}, f32[192,128]{1,0:T(8,128)S(1)}, u32[]{:S(2)}, u32[]{:S(2)}) collective-permute-start(f32[192,128]{1,0:T(8,128)} %get-tuple-element.41), channel_id=1, source_target_pairs={{0,1},{1,2},{2,3},{3,4},{4,5},{5,6},{6,7},{8,9},{9,10},{10,11},{11... | collective-permute-start | bytes 294920 | tf_op jit(solution)/shard_map/ppermute | solution.py:389
  75.7 21.5 %collective-permute-start.7 = (f32[192,128]{1,0:T(8,128)S(1)}, f32[192,128]{1,0:T(8,128)S(1)}, u32[]{:S(2)}, u32[]{:S(2)}) collective-permute-start(f32[192,128]{1,0:T(8,128)S(1)} %get-tuple-element.42), channel_id=1, source_target_pairs={{1,0},{2,1},{3,2},{4,3},{5,4},{6,5},{7,6},{9,8},{10,9},{11,10},{12... | collective-permute-start | bytes 294920 | tf_op jit(solution)/shard_map/ppermute | solution.py:389
  97.2 34.0 %copy-start.3 = (f32[4,8,8,3,128]{4,2,3,1,0:T(8,128)S(1)}, f32[4,8,8,3,128]{4,2,3,1,0:T(8,128)}, u32[]{:S(2)}) copy-start(f32[4,8,8,3,128]{4,2,3,1,0:T(8,128)} %param.11) | copy-start | bytes 1179652
  122.5 15.5 %all-to-all-start.3 = ((f32[32,1,128]{2,1,0:T(1,128)}), f32[32,1,128]{2,1,0:T(1,128)S(1)}, u32[]{:S(2)}, u32[]{:S(2)}) async-start(f32[32,1,128]{2,1,0:T(1,128)} %broadcast_in_dim.15), calls=%async_computation.3 | async-start | bytes 32768 | tf_op jit(solution)/shard_map/all_to_all | solution.py:383

commit v4 on v3

--- a/solution.py
+++ b/solution.py
@@ -23,6 +23,7 @@
 FIELD = (CASES, NX, COMP, NY, NZ)
 f32 = jnp.float32
 bf16 = jnp.bfloat16
+OPERATOR = jax.ShapeDtypeStruct((2 * LINE, LINE), bf16)
 NT = (((1,), (1,)), ((), ()))
 NN = (((1,), (0,)), ((), ()))
 
@@ -43,22 +44,12 @@
     return high, mid, (rest - mid.astype(f32)).astype(bf16)
 
 
-def product(a, b, dims):
-    a0, a1, a2 = thirds(a)
-    b0, b1, b2 = thirds(b)
-    small = mxu(a0, b2, dims) + mxu(a2, b0, dims) + mxu(a1, b1, dims)
-    return (small + (mxu(a0, b1, dims) + mxu(a1, b0, dims))) + mxu(a0, b0, dims)
-
-
-def product_of_halves(a, b, dims):
+def product_of_halves(a, b):
     a0, a1 = halves(a)
     b0, b1 = halves(b)
-    return (mxu(a0, b1, dims) + mxu(a1, b0, dims)) + mxu(a0, b0, dims)
-
-
-def picked(chosen, b, dims):
-    high, low = halves(b)
-    return mxu(chosen, low, dims) + mxu(chosen, high, dims)
+    return mxu(
+        jnp.concatenate([a0, a0, a1], axis=1), jnp.concatenate([b0, b1, b0], axis=0), NN
+    )
 
 
 def lane_sums(a):
@@ -88,22 +79,25 @@
     return jnp.concatenate(rows, axis=0)
 
 
-def local_solve(field, operator_ref, out_ref):
-    total = None
-    for k in range(COMP):
-        rows = field[:, :, k].reshape(CASES * NX * NY, NZ)
-        part = product(rows, operator_ref[k * NZ : (k + 1) * NZ, :], NN)
-        total = part if total is None else total + part
+def local_solve(field, operator, out_ref):
+    rows = [field[:, :, k].reshape(CASES * NX * NY, NZ) for k in range(COMP)]
+    parts = [thirds(row) for row in rows]
+    high, mid, low = (jnp.concatenate([part[i] for part in parts], axis=1) for i in range(3))
+    whole = operator[...]
+    first, second = whole[:LINE], whole[LINE:]
+    total = mxu(
+        jnp.concatenate([low, mid, high, mid, high], axis=1),
+        jnp.concatenate([first, second, second, first, first], axis=0),
+        NN,
+    )
     for k in range(COMP):
         out_ref[:, :, k] = total[:, k * NZ : (k + 1) * NZ].reshape(CASES, NX, NY, NZ)
 
 
 def side_rows(ref, out_ref, y, base):
-    for c in range(CASES):
-        for x in range(NX):
-            for k in range(COMP):
-                row = base + (c * NX + x) * COMP + k
-                out_ref[row : row + 1, :] = ref[c, x, k, y : y + 1, :]
+    flat = ref.reshape(TILES * NY, NZ)
+    for at in range(0, TILES, 8):
+        out_ref[base + at : base + at + 8, :] = flat[pl.ds(at * NY + y, 8, stride=NY), :]
 
 
 def faces_kernel(
@@ -130,29 +124,33 @@
 
 
 def prepare_kernel(
-    prior, residual, lower_hbm, upper_hbm, pivots_hbm, basis_hbm,
+    residual, lower_hbm, upper_hbm, pivots_hbm, basis_hbm, prior_hbm,
     operator, solved, primal, prior_rows,
-    lower, upper, pivots, basis, sems,
-):
-    pairs = ((upper_hbm, upper), (lower_hbm, lower), (pivots_hbm, pivots), (basis_hbm, basis))
+    lower, upper, pivots, basis, prior, sems,
+):
+    pairs = (
+        (upper_hbm, upper), (lower_hbm, lower), (pivots_hbm, pivots), (basis_hbm, basis),
+        (prior_hbm, prior),
+    )
     copies = [
         pltpu.make_async_copy(source, target, sems.at[i])
         for i, (source, target) in enumerate(pairs)
     ]
     for copy in copies:
         copy.start()
-    for c in range(CASES):
-        prior_rows[c : c + 1, :] = jnp.full((1, 128), prior[c], f32)
-    copies[0].wait()
-    copies[1].wait()
-    both = product_of_halves(upper[...], lower[...], NN)
-    copies[2].wait()
+    for copy in copies:
+        copy.wait()
+    for c in range(CASES):
+        prior_rows[c : c + 1, :] = jnp.broadcast_to(prior[0:1, c : c + 1], (1, 128))
+    both = jnp.concatenate(halves(product_of_halves(upper[...], lower[...])), axis=1)
     at = lax.broadcasted_iota(jnp.int32, (LINE, LINE), 0)
     chosen = jnp.where(at == pivots[...], 1.0, 0.0).astype(bf16)
-    rows = picked(chosen, both, NN)
-    operator[...] = picked(chosen, rows, NT)
+    rows = mxu(chosen, both, NN).astype(bf16)
+    rows = jnp.concatenate([rows[:, :LINE], rows[:, LINE:]], axis=0)
+    picked = mxu(chosen, rows, NT).astype(bf16)
+    operator[:LINE, :] = picked[:, :LINE]
+    operator[LINE:, :] = picked[:, LINE:]
     local_solve(residual, operator, solved)
-    copies[3].wait()
     primal[...] = lane_sums(restricted(basis, residual))
 
 
@@ -263,13 +261,13 @@
     primal = everything - weight * pltpu.roll(everything, 80, 1)
     high, low = halves(primal)
     pair = jnp.concatenate([high, low], axis=1)
-    source = lax.broadcasted_iota(jnp.int32, (256, LINE), 0) % 128
-    target = lax.broadcasted_iota(jnp.int32, (256, LINE), 1)
+    source = lax.broadcasted_iota(jnp.int32, (128, LINE), 0)
+    target = lax.broadcasted_iota(jnp.int32, (128, LINE), 1) % PRIMAL
     slot = lax.broadcasted_iota(jnp.int32, (8, LINE), 1) // PRIMAL
     rows = []
     for c in range(CASES):
-        spread = jnp.where(source == c * PRIMAL + target % PRIMAL, 1.0, 0.0).astype(bf16)
-        wide = mxu(pair, spread, NN)
+        spread = jnp.where(source == c * PRIMAL + target, 1.0, 0.0).astype(bf16)
+        wide = mxu(pair, jnp.concatenate([spread, spread], axis=0), NN)
         gathered = []
         for half in range(2):
             total = None
@@ -354,12 +352,11 @@
 
 
 VMEM = pl.BlockSpec(memory_space=pltpu.VMEM)
-SMEM = pl.BlockSpec(memory_space=pltpu.SMEM)
 HBM = pl.BlockSpec(memory_space=pltpu.HBM)
 
 
 def local_call(body, outs, spaces, *args, scratch=()):
-    specs = [{"s": SMEM, "v": VMEM, "h": HBM}[space] for space in spaces]
+    specs = [{"v": VMEM, "h": HBM}[space] for space in spaces]
     specs += [VMEM] * (len(args) - len(specs))
     args = tuple(
         pltpu.with_memory_space_constraint(arg, pltpu.HBM) if spec is HBM else arg
@@ -367,7 +364,10 @@
     )
     return pl.pallas_call(
         body,
-        out_shape=[jax.ShapeDtypeStruct(shape, f32) for shape in outs],
+        out_shape=[
+            shape if hasattr(shape, "dtype") else jax.ShapeDtypeStruct(shape, f32)
+            for shape in outs
+        ],
         in_specs=specs,
         out_specs=[VMEM] * len(outs),
         scratch_shapes=list(scratch),
@@ -408,13 +408,13 @@
     below_x, above_x = neighbours(low_x, high_x, GX_AXES, N_GX)
 
     operator, solved_r, primal_r, prior_rows = local_call(
-        prepare_kernel, [(LINE, LINE), FIELD, (48, 128), (CASES, 128)], "svhhhh",
-        inner_prior, residual, lower_factor[0, 0], upper_factor[0, 0], pivot_order[0],
-        coarse_basis,
+        prepare_kernel, [OPERATOR, FIELD, (48, 128), (CASES, 128)], "vhhhhh",
+        residual, lower_factor[0, 0], upper_factor[0, 0], pivot_order[0], coarse_basis,
+        inner_prior.reshape(1, CASES),
         scratch=[
             pltpu.VMEM((LINE, LINE), f32), pltpu.VMEM((LINE, LINE), f32),
             pltpu.VMEM((1, LINE), jnp.int32), pltpu.VMEM((NP, NX, NY, NZ), f32),
-            pltpu.SemaphoreType.DMA((4,)),
+            pltpu.VMEM((1, CASES), f32), pltpu.SemaphoreType.DMA((5,)),
         ],
     )
 

time: 139 us -> 139 us (level)
  waiting for transfers between devices: 32.3 us -> 34.9 us
  Pallas kernels: 12.2 us -> 9.9 us
    ppermute x8, waiting for transfers between devices: 26.7 us -> 29.2 us  [neighbours(): return (lax.ppermute(high, axes, up), lax.ppermute(low, axes, down))]
    pallas_call x8, Pallas kernels: 12.2 us -> 9.9 us  [local_call(): pl.pallas_call(body, out_shape=[shape if hasattr(shape, 'dtype') else jax...]
  transfers between devices with their start and end apart: 10 -> 10, of which waited for: 4 -> 4; matrix products, arithmetic and copies ran while one was open for 0% -> 0% of each run, Pallas kernels for 5% -> 4%
where the time goes in v4:
time: 139 us
  starting transfers between devices  51.9 us (37%)
  blocking collectives  39.7 us (29%)
  waiting for transfers between devices  34.9 us (25%)
  Pallas kernels  9.9 us (7%)
    all_to_all x2, blocking collectives, exchange(): return lax.all_to_all(rows, axes, 0, 0, tiled=True)  39.7 us
    ppermute x8, starting transfers between devices, neighbours(): return (lax.ppermute(high, axes, up), lax.ppermute(low, axes, down))  32.2 us
    ppermute x8, waiting for transfers between devices, neighbours(): return (lax.ppermute(high, axes, up), lax.ppermute(low, axes, down))  29.2 us
    all_to_all x2, starting transfers between devices, exchange(): return lax.all_to_all(rows, axes, 0, 0, tiled=True)  19.8 us
    pallas_call x8, Pallas kernels, local_call(): pl.pallas_call(body, out_shape=[shape if hasattr(shape, 'dtype') else jax...  9.9 us
    all_to_all x2, waiting for transfers between devices, exchange(): return lax.all_to_all(rows, axes, 0, 0, tiled=True)  5.62 us
  transfers between devices with their start and end apart: 10, of which 4 were waited for; matrix products, arithmetic and copies ran while one was open for 0% of the time, Pallas kernels for 4%

profile of v4, /device:TPU:1, one launch (start us, length us, event | category | flops | bytes accessed | tf_op | source)
XLA Modules:
  0.0 138.6 jit_solution(16272769749990817934)
XLA Ops:
  0.6 0.0 copy-start.1
  0.6 1.1 shard_map.139
  1.8 4.5 %collective-permute-start = (f32[4,3,8,128]{3,2,1,0:T(8,128)S(1)}, f32[4,3,8,128]{3,2,1,0:T(8,128)S(1)}, u32[]{:S(2)}, u32[]{:S(2)}) collective-permute-start(f32[4,3,8,128]{3,2,1,0:T(8,128)S(1)} %get-tuple-element.28), channel_id=1, source_target_pairs={{0,8},{8,16},{16,24},{24,32},{32,40},{40,48},{48,56},{56,64},{64,7... | collective-permute-start | bytes 147464 | tf_op jit(solution)/shard_map/ppermute | solution.py:389
  6.3 5.5 %collective-permute-start.1 = (f32[4,3,8,128]{3,2,1,0:T(8,128)S(1)}, f32[4,3,8,128]{3,2,1,0:T(8,128)S(1)}, u32[]{:S(2)}, u32[]{:S(2)}) collective-permute-start(f32[4,3,8,128]{3,2,1,0:T(8,128)S(1)} %get-tuple-element.29), channel_id=1, source_target_pairs={{8,0},{16,8},{24,16},{32,24},{40,32},{48,40},{56,48},{64,56},{72,6... | collective-permute-start | bytes 147464 | tf_op jit(solution)/shard_map/ppermute | solution.py:389
  11.8 11.8 %collective-permute-start.2 = (f32[96,128]{1,0:T(8,128)S(1)}, f32[96,128]{1,0:T(8,128)S(1)}, u32[]{:S(2)}, u32[]{:S(2)}) collective-permute-start(f32[96,128]{1,0:T(8,128)S(1)} %get-tuple-element.30), channel_id=1, source_target_pairs={{0,1},{1,2},{2,3},{3,4},{4,5},{5,6},{6,7},{8,9},{9,10},{10,11},{11... | collective-permute-start | bytes 147464 | tf_op jit(solution)/shard_map/ppermute | solution.py:389
  23.7 1.3 collective-permute-start.3
  25.0 0.0 copy-done.1
  25.0 0.0 copy-start
  25.0 0.0 copy-start.2
  25.0 0.0 copy-start.5
  25.0 0.0 copy-start.6
  25.0 3.6 %shard_map.138 = (bf16[768,384]{1,0:T(8,128)(2,1)S(1)}, f32[4,8,3,8,128]{4,3,2,1,0:T(8,128)S(1)}, f32[48,128]{1,0:T(8,128)S(1)}, f32[4,128]{1,0:T(4,128)S(1)}) custom-call(f32[4,8,3,8,128]{4,3,2,1,0:T(8,128)S(1)} %bitcast.18, f32[384,384]{1,0:T(8,128)} %bitcast.25, f32[384,384]{1,0:T(8,128)} %bitcast.26, s32[1,384]{1,0:T(1,128)} %bitcast.28, ...), custom_call_target="tpu_custom_call" | custom-call | tf_op jit(solution)/shard_map/pallas_call | solution.py:365
  28.6 0.0 collective-permute-done.below_x
  28.6 0.0 collective-permute-done.1.above_x
  28.6 0.0 collective-permute-done.2.below_y
  28.7 9.1 %collective-permute-done.3.above_y = f32[96,128]{1,0:T(8,128)S(1)} collective-permute-done((f32[96,128]{1,0:T(8,128)S(1)}, f32[96,128]{1,0:T(8,128)S(1)}, u32[]{:S(2)}, u32[]{:S(2)}) %collective-permute-start.3) | collective-permute-done | bytes 49184 | tf_op jit(solution)/shard_map/ppermute | solution.py:389
  37.8 0.0 copy-done
  37.8 0.0 copy-done.2
  37.8 0.0 copy-done.5
  37.8 0.0 copy-done.6
  37.8 1.8 %shard_map.140 = (f32[4,8,3,8,128]{4,3,2,1,0:T(8,128)S(1)}, f32[4,8,3,8,128]{4,3,2,1,0:T(8,128)S(1)}, f32[48,128]{1,0:T(8,128)S(1)}, f32[16,1,128]{2,1,0:T(1,128...) custom-call(f32[4,8,3,8,128]{4,3,2,1,0:T(8,128)S(1)} %bitcast.15, ...), custom_call_target="tpu_custom_call" | custom-call | tf_op jit(solution)/shard_map/pallas_call | solution.py:365
  39.5 16.2 %all_to_all.20 = f32[16,1,128]{2,1,0:T(1,128)S(1)} all-to-all(f32[16,1,128]{2,1,0:T(1,128)S(1)} %get-tuple-element.35), channel_id=1, replica_groups=mesh['zl'=8,'x'=4,'c'=2,'y'=4,'zh'=2] {'zh','zl'}, dimensions={0} | all-to-all | bytes 16384 | tf_op jit(solution)/shard_map/all_to_all | solution.py:383
  55.7 0.7 broadcast_in_dim.14
  56.5 0.0 copy-start.4
  56.5 11.1 %all-to-all-start.1 = ((f32[32,16,128]{2,1,0:T(8,128)}), f32[32,16,128]{2,1,0:T(8,128)S(1)}, u32[]{:S(2)}, u32[]{:S(2)}) async-start(f32[32,16,128]{2,1,0:T(8,128)} %broadcast_in_dim.14), calls=%async_computation.1 | async-start | bytes 524288 | tf_op jit(solution)/shard_map/all_to_all | solution.py:383
  67.6 3.5 %collective-permute-start.4 = (f32[8,3,8,128]{3,2,1,0:T(8,128)}, f32[8,3,8,128]{3,2,1,0:T(8,128)S(1)}, u32[]{:S(2)}, u32[]{:S(2)}) collective-permute-start(f32[8,3,8,128]{3,2,1,0:T(8,128)} %get-tuple-element.39), channel_id=1, source_target_pairs={{0,8},{8,16},{16,24},{24,32},{32,40},{40,48},{48,56},{56,64},{64,7... | collective-permute-start | bytes 294920 | tf_op jit(solution)/shard_map/ppermute | solution.py:389
  71.2 1.9 %collective-permute-start.5 = (f32[8,3,8,128]{3,2,1,0:T(8,128)}, f32[8,3,8,128]{3,2,1,0:T(8,128)S(1)}, u32[]{:S(2)}, u32[]{:S(2)}) collective-permute-start(f32[8,3,8,128]{3,2,1,0:T(8,128)} %get-tuple-element.40), channel_id=1, source_target_pairs={{8,0},{16,8},{24,16},{32,24},{40,32},{48,40},{56,48},{64,56},{72,6... | collective-permute-start | bytes 294920 | tf_op jit(solution)/shard_map/ppermute | solution.py:389
  73.1 2.3 %collective-permute-start.6 = (f32[192,128]{1,0:T(8,128)}, f32[192,128]{1,0:T(8,128)S(1)}, u32[]{:S(2)}, u32[]{:S(2)}) collective-permute-start(f32[192,128]{1,0:T(8,128)} %get-tuple-element.41), channel_id=1, source_target_pairs={{0,1},{1,2},{2,3},{3,4},{4,5},{5,6},{6,7},{8,9},{9,10},{10,11},{11... | collective-permute-start | bytes 294920 | tf_op jit(solution)/shard_map/ppermute | solution.py:389
  75.4 1.3 collective-permute-start.7
  76.7 0.0 copy-done.4
  76.7 0.0 collective-permute-done.4.below_x
  76.7 0.6 collective-permute-done.5.above_x
  77.3 0.0 collective-permute-done.6.below_y
  77.3 19.5 %collective-permute-done.7.above_y = f32[192,128]{1,0:T(8,128)S(1)} collective-permute-done((f32[192,128]{1,0:T(8,128)S(1)}, f32[192,128]{1,0:T(8,128)S(1)}, u32[]{:S(2)}, u32[]{:S(2)}) %collective-permute-start.7) | collective-permute-done | bytes 98336 | tf_op jit(solution)/shard_map/ppermute | solution.py:389
  96.8 0.0 all-to-all-done.1
  96.8 0.0 copy-start.3
  96.8 1.3 shard_map.142
  98.1 23.4 %all_to_all.21 = f32[16,1,128]{2,1,0:T(1,128)S(1)} all-to-all(f32[16,1,128]{2,1,0:T(1,128)S(1)} %get-tuple-element.46), channel_id=1, replica_groups=mesh['zl'=8,'x'=4,'c'=2,'y'=4,'zh'=2] {'zh','zl'}, dimensions={0} | all-to-all | bytes 16384 | tf_op jit(solution)/shard_map/all_to_all | solution.py:383
  121.6 0.6 broadcast_in_dim.15
  122.2 8.6 %all-to-all-start.3 = ((f32[32,1,128]{2,1,0:T(1,128)}), f32[32,1,128]{2,1,0:T(1,128)S(1)}, u32[]{:S(2)}, u32[]{:S(2)}) async-start(f32[32,1,128]{2,1,0:T(1,128)} %broadcast_in_dim.15), calls=%async_computation.3 | async-start | bytes 32768 | tf_op jit(solution)/shard_map/all_to_all | solution.py:383
  130.8 0.0 copy-done.3
  130.8 1.0 shard_map.143
  131.8 0.3 shard_map.144.preconditioned
  132.1 5.6 %all-to-all-done.3 = f32[32,1,128]{2,1,0:T(1,128)S(1)} async-done(((f32[32,1,128]{2,1,0:T(1,128)}), f32[32,1,128]{2,1,0:T(1,128)S(1)}, u32[]{:S(2)}, u32[]{:S(2)}) %all-to-all-start.3) | async-done | bytes 16416 | tf_op jit(solution)/shard_map/all_to_all | solution.py:383
  137.7 0.9 shard_map.145
  (2 shorter events, 0.1 us)
Async XLA Ops:
  0.6 24.3 %copy-start.1 = (f32[4,8,8,3,128]{4,2,3,1,0:T(8,128)S(1)}, f32[4,8,8,3,128]{4,2,3,1,0:T(8,128)}, u32[]{:S(2)}) copy-start(f32[4,8,8,3,128]{4,2,3,1,0:T(8,128)} %param.12) | copy-start | bytes 1179652
  1.8 26.8 %collective-permute-start = (f32[4,3,8,128]{3,2,1,0:T(8,128)S(1)}, f32[4,3,8,128]{3,2,1,0:T(8,128)S(1)}, u32[]{:S(2)}, u32[]{:S(2)}) collective-permute-start(f32[4,3,8,128]{3,2,1,0:T(8,128)S(1)} %get-tuple-element.28), channel_id=1, source_target_pairs={{0,8},{8,16},{16,24},{24,32},{32,40},{40,48},{48,56},{56,64},{64,7... | collective-permute-start | bytes 147464 | tf_op jit(solution)/shard_map/ppermute | solution.py:389
  6.3 22.3 %collective-permute-start.1 = (f32[4,3,8,128]{3,2,1,0:T(8,128)S(1)}, f32[4,3,8,128]{3,2,1,0:T(8,128)S(1)}, u32[]{:S(2)}, u32[]{:S(2)}) collective-permute-start(f32[4,3,8,128]{3,2,1,0:T(8,128)S(1)} %get-tuple-element.29), channel_id=1, source_target_pairs={{8,0},{16,8},{24,16},{32,24},{40,32},{48,40},{56,48},{64,56},{72,6... | collective-permute-start | bytes 147464 | tf_op jit(solution)/shard_map/ppermute | solution.py:389
  11.8 16.8 %collective-permute-start.2 = (f32[96,128]{1,0:T(8,128)S(1)}, f32[96,128]{1,0:T(8,128)S(1)}, u32[]{:S(2)}, u32[]{:S(2)}) collective-permute-start(f32[96,128]{1,0:T(8,128)S(1)} %get-tuple-element.30), channel_id=1, source_target_pairs={{0,1},{1,2},{2,3},{3,4},{4,5},{5,6},{6,7},{8,9},{9,10},{10,11},{11... | collective-permute-start | bytes 147464 | tf_op jit(solution)/shard_map/ppermute | solution.py:389
  23.7 14.1 %collective-permute-start.3 = (f32[96,128]{1,0:T(8,128)S(1)}, f32[96,128]{1,0:T(8,128)S(1)}, u32[]{:S(2)}, u32[]{:S(2)}) collective-permute-start(f32[96,128]{1,0:T(8,128)S(1)} %get-tuple-element.31), channel_id=1, source_target_pairs={{1,0},{2,1},{3,2},{4,3},{5,4},{6,5},{7,6},{9,8},{10,9},{11,10},{12... | collective-permute-start | bytes 147464 | tf_op jit(solution)/shard_map/ppermute | solution.py:389
  25.0 12.8 %copy-start = (f32[4,8,8,3,128]{4,2,3,1,0:T(8,128)S(1)}, f32[4,8,8,3,128]{4,2,3,1,0:T(8,128)}, u32[]{:S(2)}) copy-start(f32[4,8,8,3,128]{4,2,3,1,0:T(8,128)} %param.13) | copy-start | bytes 1179652
  25.0 12.8 %copy-start.2 = (f32[4,8,8,128]{3,2,1,0:T(8,128)S(1)}, f32[4,8,8,128]{3,2,1,0:T(8,128)}, u32[]{:S(2)}) copy-start(f32[4,8,8,128]{3,2,1,0:T(8,128)} %basis.3) | copy-start | bytes 393220
  25.0 12.8 %copy-start.5 = (f32[8,8,128]{2,1,0:T(8,128)S(1)}, f32[8,8,128]{2,1,0:T(8,128)}, u32[]{:S(2)}) copy-start(f32[8,8,128]{2,1,0:T(8,128)} %stiffness.1) | copy-start | bytes 98308
  25.0 12.7 %copy-start.6 = (f32[8,8,128]{2,1,0:T(8,128)S(1)}, f32[8,8,128]{2,1,0:T(8,128)}, u32[]{:S(2)}) copy-start(f32[8,8,128]{2,1,0:T(8,128)} %coupling.1) | copy-start | bytes 98308
  56.5 20.2 %copy-start.4 = (f32[1,1,12,6144]{3,1,2,0:T(1,128)S(1)}, f32[1,1,12,6144]{3,1,2,0:T(1,128)}, u32[]{:S(2)}) copy-start(f32[1,1,12,6144]{3,1,2,0:T(1,128)} %param.20) | copy-start | bytes 884740
  56.5 40.4 %all-to-all-start.1 = ((f32[32,16,128]{2,1,0:T(8,128)}), f32[32,16,128]{2,1,0:T(8,128)S(1)}, u32[]{:S(2)}, u32[]{:S(2)}) async-start(f32[32,16,128]{2,1,0:T(8,128)} %broadcast_in_dim.14), calls=%async_computation.1 | async-start | bytes 524288 | tf_op jit(solution)/shard_map/all_to_all | solution.py:383
  67.6 9.1 %collective-permute-start.4 = (f32[8,3,8,128]{3,2,1,0:T(8,128)}, f32[8,3,8,128]{3,2,1,0:T(8,128)S(1)}, u32[]{:S(2)}, u32[]{:S(2)}) collective-permute-start(f32[8,3,8,128]{3,2,1,0:T(8,128)} %get-tuple-element.39), channel_id=1, source_target_pairs={{0,8},{8,16},{16,24},{24,32},{32,40},{40,48},{48,56},{56,64},{64,7... | collective-permute-start | bytes 294920 | tf_op jit(solution)/shard_map/ppermute | solution.py:389
  71.2 6.1 %collective-permute-start.5 = (f32[8,3,8,128]{3,2,1,0:T(8,128)}, f32[8,3,8,128]{3,2,1,0:T(8,128)S(1)}, u32[]{:S(2)}, u32[]{:S(2)}) collective-permute-start(f32[8,3,8,128]{3,2,1,0:T(8,128)} %get-tuple-element.40), channel_id=1, source_target_pairs={{8,0},{16,8},{24,16},{32,24},{40,32},{48,40},{56,48},{64,56},{72,6... | collective-permute-start | bytes 294920 | tf_op jit(solution)/shard_map/ppermute | solution.py:389
  73.1 4.2 %collective-permute-start.6 = (f32[192,128]{1,0:T(8,128)}, f32[192,128]{1,0:T(8,128)S(1)}, u32[]{:S(2)}, u32[]{:S(2)}) collective-permute-start(f32[192,128]{1,0:T(8,128)} %get-tuple-element.41), channel_id=1, source_target_pairs={{0,1},{1,2},{2,3},{3,4},{4,5},{5,6},{6,7},{8,9},{9,10},{10,11},{11... | collective-permute-start | bytes 294920 | tf_op jit(solution)/shard_map/ppermute | solution.py:389
  75.4 21.5 %collective-permute-start.7 = (f32[192,128]{1,0:T(8,128)S(1)}, f32[192,128]{1,0:T(8,128)S(1)}, u32[]{:S(2)}, u32[]{:S(2)}) collective-permute-start(f32[192,128]{1,0:T(8,128)S(1)} %get-tuple-element.42), channel_id=1, source_target_pairs={{1,0},{2,1},{3,2},{4,3},{5,4},{6,5},{7,6},{9,8},{10,9},{11,10},{12... | collective-permute-start | bytes 294920 | tf_op jit(solution)/shard_map/ppermute | solution.py:389
  96.8 34.0 %copy-start.3 = (f32[4,8,8,3,128]{4,2,3,1,0:T(8,128)S(1)}, f32[4,8,8,3,128]{4,2,3,1,0:T(8,128)}, u32[]{:S(2)}) copy-start(f32[4,8,8,3,128]{4,2,3,1,0:T(8,128)} %param.11) | copy-start | bytes 1179652
  122.2 15.5 %all-to-all-start.3 = ((f32[32,1,128]{2,1,0:T(1,128)}), f32[32,1,128]{2,1,0:T(1,128)S(1)}, u32[]{:S(2)}, u32[]{:S(2)}) async-start(f32[32,1,128]{2,1,0:T(1,128)} %broadcast_in_dim.15), calls=%async_computation.3 | async-start | bytes 32768 | tf_op jit(solution)/shard_map/all_to_all | solution.py:383

commit v5 on v4

--- a/solution.py
+++ b/solution.py
@@ -247,8 +247,7 @@
 
 def coarse_kernel(
     prior, table, inverse, primal_r, primal_w, residual, applied, solved_r, solved_w,
-    below_x, above_x, below_y, above_y,
-    row, steps_out, coarse,
+    partial, steps_out, coarse, edge_x, edge_y,
 ):
     steps = steps_of(table, prior)
     for c in range(CASES):
@@ -287,26 +286,58 @@
     coarse_values = lane_sums(jnp.concatenate(rows, axis=0))
     coarse[...] = coarse_values
 
-    y_at = lax.broadcasted_iota(jnp.int32, (NY, NZ), 0)
-    sums = []
+    flat_r, flat_w = residual.reshape(TILES * NY, NZ), applied.reshape(TILES * NY, NZ)
     for c in range(CASES):
         step = steps[c]
         total = None
         for x in range(NX):
             for k in range(COMP):
-                smooth = smoothed_at(
-                    c, x, k, step, solved_r, solved_w, below_x, above_x, below_y, above_y, y_at
+                rest = residual[c, x, k] - step * applied[c, x, k]
+                part = rest * (solved_r[c, x, k] - step * solved_w[c, x, k])
+                total = part if total is None else total + part
+                if x == 0 or x == NX - 1:
+                    edge_x[x // (NX - 1), c, k] = 0.5 * rest
+        for side, y in ((0, 0), (TILES, NY - 1)):
+            for at in range(c * NX * COMP, (c + 1) * NX * COMP, 8):
+                rows = pl.ds(at * NY + y, 8, stride=NY)
+                edge_y[side + at : side + at + 8, :] = 0.5 * (
+                    flat_r[rows, :] - step * flat_w[rows, :]
                 )
-                part = (residual[c, x, k] - step * applied[c, x, k]) * smooth
+        mine = slice(c * PRIMAL, (c + 1) * PRIMAL)
+        own = primal_r[mine] - step * primal_w[mine]
+        both = jnp.sum(own * coarse_values[mine], axis=0, keepdims=True)
+        partial[c : c + 1, :] = jnp.sum(total, axis=0, keepdims=True) + jnp.where(
+            lane == 0, both, 0.0
+        )
+
+
+def edges_kernel(
+    partial, steps, edge_x, edge_y, below_x, above_x, below_y, above_y, row
+):
+    sums = []
+    for c in range(CASES):
+        step = steps[c : c + 1, :]
+        total = None
+        for side, halo in ((0, below_x), (1, above_x)):
+            for k in range(COMP):
+                part = edge_x[side, c, k] * (halo[c, k] - step * halo[CASES + c, k])
                 total = part if total is None else total + part
-        own = primal_r[c * PRIMAL : (c + 1) * PRIMAL] - step * primal_w[c * PRIMAL : (c + 1) * PRIMAL]
-        both = jnp.sum(own * coarse_values[c * PRIMAL : (c + 1) * PRIMAL], axis=0, keepdims=True)
-        sums.append(
-            jnp.sum(total, axis=0, keepdims=True) + jnp.where(lane == 0, both, 0.0)
-        )
-    row[...] = jnp.broadcast_to(
-        lane_row(jnp.concatenate(sums, axis=0))[None], (N_DEPTH, 1, 128)
-    )
+        for side, halo in ((0, below_y), (TILES, above_y)):
+            for at in range(c * NX * COMP, (c + 1) * NX * COMP, 8):
+                beside = halo[at : at + 8, :] - step * halo[TILES + at : TILES + at + 8, :]
+                total = total + edge_y[side + at : side + at + 8, :] * beside
+        sums.append(jnp.sum(total, axis=0, keepdims=True))
+    whole = jnp.concatenate(sums, axis=0) + partial[...]
+    row[...] = jnp.broadcast_to(lane_row(whole)[None], (N_DEPTH, 1, 128))
+
+
+def spread_kernel(line, out):
+    out[...] = jnp.broadcast_to(line[...][None], (N_PLANE, N_DEPTH, 128))
+
+
+def fold_kernel(line, out):
+    total = jnp.sum(line[...], axis=0, keepdims=True)
+    out[...] = jnp.broadcast_to(total, (N_PLANE, 1, 128))
 
 
 def advance_kernel(
@@ -321,8 +352,10 @@
 
 
 def precondition_kernel(
-    steps, coarse, basis, solved_r, solved_w, below_x, above_x, below_y, above_y, preconditioned
-):
+    steps, coarse, basis, direction, solved_r, solved_w, below_x, above_x, below_y, above_y,
+    preconditioned, held,
+):
+    held[...] = direction[...]
     y_at = lax.broadcasted_iota(jnp.int32, (NY, NZ), 0)
     for c in range(CASES):
         step = steps[c : c + 1, :]
@@ -375,10 +408,6 @@
     )(*args)
 
 
-def spread(block, count):
-    return jnp.broadcast_to(block[None], (count,) + block.shape)
-
-
 def exchange(rows, axes):
     return lax.all_to_all(rows, axes, 0, 0, tiled=True)
 
@@ -435,28 +464,31 @@
         by_depth_kernel, [(PRIMAL, 2, 8, LINE)], "",
         coarse_inverse.reshape(PRIMAL * 48, 128),
     )
-    table = exchange(spread(line.reshape(N_DEPTH, 128), N_PLANE), PLANE)
+    (lines,) = local_call(spread_kernel, [(N_PLANE, N_DEPTH, 128)], "", line.reshape(N_DEPTH, 128))
+    table = exchange(lines, PLANE)
     table = table.reshape(N_PLANE * N_DEPTH, 128)
 
     halo = (below_x, above_x, below_y, above_y)
-    rows, steps, coarse = local_call(
-        coarse_kernel, [rows_z, (CASES, 128), (48, 128)], "",
+    partial, steps, coarse, edge_x, edge_y = local_call(
+        coarse_kernel,
+        [(CASES, 128), (CASES, 128), (48, 128), (2, CASES, COMP, NY, NZ), (2 * TILES, NZ)], "",
         prior_rows, table, inverse, primal_r, primal_w, residual, applied, solved_r, solved_w,
-        *halo,
-    )
+    )
+    (rows,) = local_call(edges_kernel, [rows_z], "", partial, steps, edge_x, edge_y, *halo)
     line = exchange(rows, DEPTH)
     solution_next, residual_next = local_call(
         advance_kernel, [FIELD, FIELD], "",
         steps, solution, residual, direction, applied,
     )
-    parts = exchange(spread(jnp.sum(line, axis=0), N_PLANE), PLANE)
-    (preconditioned,) = local_call(
-        precondition_kernel, [FIELD], "",
-        steps, coarse, coarse_basis, solved_r, solved_w, *halo,
+    (rows,) = local_call(fold_kernel, [(N_PLANE, 1, 128)], "", line)
+    parts = exchange(rows, PLANE)
+    preconditioned, held = local_call(
+        precondition_kernel, [FIELD, FIELD], "",
+        steps, coarse, coarse_basis, direction, solved_r, solved_w, *halo,
     )
     direction_next, inner = local_call(
         final_kernel, [FIELD, (CASES,)], "",
-        prior_rows, parts.reshape(N_PLANE, 128), preconditioned, direction,
+        prior_rows, parts.reshape(N_PLANE, 128), preconditioned, held,
     )
     solution_next, residual_next, direction_next = (
         a.transpose(0, 1, 3, 2, 4) for a in (solution_next, residual_next, direction_next)

time: 139 us -> 138 us (level)
  Pallas kernels: 9.9 us -> 11.4 us
    pallas_call x8 -> x11, Pallas kernels: 9.9 us -> 11.4 us  [local_call(): pl.pallas_call(body, out_shape=[shape if hasattr(shape, 'dtype') else jax...]
  transfers between devices with their start and end apart: 10 -> 10, of which waited for: 4 -> 3; matrix products, arithmetic and copies ran while one was open for 0% -> 0% of each run, Pallas kernels for 4% -> 4%
where the time goes in v5:
time: 138 us
  starting transfers between devices  52.2 us (38%)
  blocking collectives  39.4 us (29%)
  waiting for transfers between devices  33.6 us (24%)
  Pallas kernels  11.4 us (8%)
    all_to_all x2, blocking collectives, exchange(): return lax.all_to_all(rows, axes, 0, 0, tiled=True)  39.4 us
    ppermute x8, starting transfers between devices, neighbours(): return (lax.ppermute(high, axes, up), lax.ppermute(low, axes, down))  32.2 us
    ppermute x8, waiting for transfers between devices, neighbours(): return (lax.ppermute(high, axes, up), lax.ppermute(low, axes, down))  28 us
    all_to_all x2, starting transfers between devices, exchange(): return lax.all_to_all(rows, axes, 0, 0, tiled=True)  20 us
    pallas_call x11, Pallas kernels, local_call(): pl.pallas_call(body, out_shape=[shape if hasattr(shape, 'dtype') else jax...  11.4 us
    all_to_all x2, waiting for transfers between devices, exchange(): return lax.all_to_all(rows, axes, 0, 0, tiled=True)  5.6 us
  transfers between devices with their start and end apart: 10, of which 3 were waited for; matrix products, arithmetic and copies ran while one was open for 0% of the time, Pallas kernels for 4%

profile of v5, /device:TPU:1, one launch (start us, length us, event | category | flops | bytes accessed | tf_op | source)
XLA Modules:
  0.0 137.5 jit_solution(16675161661663800616)
XLA Ops:
  0.6 0.0 copy-start.1
  0.6 1.1 shard_map.139
  1.8 4.5 %collective-permute-start = (f32[4,3,8,128]{3,2,1,0:T(8,128)S(1)}, f32[4,3,8,128]{3,2,1,0:T(8,128)S(1)}, u32[]{:S(2)}, u32[]{:S(2)}) collective-permute-start(f32[4,3,8,128]{3,2,1,0:T(8,128)S(1)} %get-tuple-element.32), channel_id=1, source_target_pairs={{0,8},{8,16},{16,24},{24,32},{32,40},{40,48},{48,56},{56,64},{64,7... | collective-permute-start | bytes 147464 | tf_op jit(solution)/shard_map/ppermute | solution.py:418
  6.3 5.5 %collective-permute-start.1 = (f32[4,3,8,128]{3,2,1,0:T(8,128)S(1)}, f32[4,3,8,128]{3,2,1,0:T(8,128)S(1)}, u32[]{:S(2)}, u32[]{:S(2)}) collective-permute-start(f32[4,3,8,128]{3,2,1,0:T(8,128)S(1)} %get-tuple-element.33), channel_id=1, source_target_pairs={{8,0},{16,8},{24,16},{32,24},{40,32},{48,40},{56,48},{64,56},{72,6... | collective-permute-start | bytes 147464 | tf_op jit(solution)/shard_map/ppermute | solution.py:418
  11.8 11.8 %collective-permute-start.2 = (f32[96,128]{1,0:T(8,128)S(1)}, f32[96,128]{1,0:T(8,128)S(1)}, u32[]{:S(2)}, u32[]{:S(2)}) collective-permute-start(f32[96,128]{1,0:T(8,128)S(1)} %get-tuple-element.34), channel_id=1, source_target_pairs={{0,1},{1,2},{2,3},{3,4},{4,5},{5,6},{6,7},{8,9},{9,10},{10,11},{11... | collective-permute-start | bytes 147464 | tf_op jit(solution)/shard_map/ppermute | solution.py:418
  23.7 1.3 collective-permute-start.3
  25.0 0.0 copy-done.1
  25.0 0.0 copy-start
  25.0 0.0 copy-start.2
  25.0 0.0 copy-start.5
  25.0 0.0 copy-start.6
  25.0 3.6 %shard_map.138 = (bf16[768,384]{1,0:T(8,128)(2,1)S(1)}, f32[4,8,3,8,128]{4,3,2,1,0:T(8,128)S(1)}, f32[48,128]{1,0:T(8,128)S(1)}, f32[4,128]{1,0:T(4,128)S(1)}) custom-call(f32[4,8,3,8,128]{4,3,2,1,0:T(8,128)S(1)} %bitcast.18, f32[384,384]{1,0:T(8,128)} %bitcast.26, f32[384,384]{1,0:T(8,128)} %bitcast.27, s32[1,384]{1,0:T(1,128)} %bitcast.28, ...), custom_call_target="tpu_custom_call" | custom-call | tf_op jit(solution)/shard_map/pallas_call | solution.py:398
  28.6 0.0 collective-permute-done.below_x
  28.6 0.0 collective-permute-done.1.above_x
  28.6 0.0 collective-permute-done.2.below_y
  28.7 9.1 %collective-permute-done.3.above_y = f32[96,128]{1,0:T(8,128)S(1)} collective-permute-done((f32[96,128]{1,0:T(8,128)S(1)}, f32[96,128]{1,0:T(8,128)S(1)}, u32[]{:S(2)}, u32[]{:S(2)}) %collective-permute-start.3) | collective-permute-done | bytes 49184 | tf_op jit(solution)/shard_map/ppermute | solution.py:418
  37.8 0.0 copy-done
  37.8 0.0 copy-done.2
  37.8 0.0 copy-done.5
  37.8 0.0 copy-done.6
  37.8 1.8 %shard_map.140 = (f32[4,8,3,8,128]{4,3,2,1,0:T(8,128)S(1)}, f32[4,8,3,8,128]{4,3,2,1,0:T(8,128)S(1)}, f32[48,128]{1,0:T(8,128)S(1)}, f32[16,1,128]{2,1,0:T(1,128...) custom-call(f32[4,8,3,8,128]{4,3,2,1,0:T(8,128)S(1)} %bitcast.15, ...), custom_call_target="tpu_custom_call" | custom-call | tf_op jit(solution)/shard_map/pallas_call | solution.py:398
  39.6 16.2 %all_to_all.20 = f32[16,1,128]{2,1,0:T(1,128)S(1)} all-to-all(f32[16,1,128]{2,1,0:T(1,128)S(1)} %get-tuple-element.39), channel_id=1, replica_groups=mesh['zl'=8,'x'=4,'c'=2,'y'=4,'zh'=2] {'zh','zl'}, dimensions={0} | all-to-all | bytes 16384 | tf_op jit(solution)/shard_map/all_to_all | solution.py:412
  55.8 0.7 shard_map.141
  56.5 0.0 copy-start.4
  56.5 11.1 %all-to-all-start.1 = ((f32[32,16,128]{2,1,0:T(8,128)}), f32[32,16,128]{2,1,0:T(8,128)S(1)}, u32[]{:S(2)}, u32[]{:S(2)}) async-start(f32[32,16,128]{2,1,0:T(8,128)} %shard_map.141), calls=%async_computation.1 | async-start | bytes 524288 | tf_op jit(solution)/shard_map/all_to_all | solution.py:412
  67.7 3.5 %collective-permute-start.4 = (f32[8,3,8,128]{3,2,1,0:T(8,128)}, f32[8,3,8,128]{3,2,1,0:T(8,128)S(1)}, u32[]{:S(2)}, u32[]{:S(2)}) collective-permute-start(f32[8,3,8,128]{3,2,1,0:T(8,128)} %get-tuple-element.49), channel_id=1, source_target_pairs={{0,8},{8,16},{16,24},{24,32},{32,40},{40,48},{48,56},{56,64},{64,7... | collective-permute-start | bytes 294920 | tf_op jit(solution)/shard_map/ppermute | solution.py:418
  71.2 1.9 %collective-permute-start.5 = (f32[8,3,8,128]{3,2,1,0:T(8,128)}, f32[8,3,8,128]{3,2,1,0:T(8,128)S(1)}, u32[]{:S(2)}, u32[]{:S(2)}) collective-permute-start(f32[8,3,8,128]{3,2,1,0:T(8,128)} %get-tuple-element.50), channel_id=1, source_target_pairs={{8,0},{16,8},{24,16},{32,24},{40,32},{48,40},{56,48},{64,56},{72,6... | collective-permute-start | bytes 294920 | tf_op jit(solution)/shard_map/ppermute | solution.py:418
  73.1 2.3 %collective-permute-start.6 = (f32[192,128]{1,0:T(8,128)}, f32[192,128]{1,0:T(8,128)S(1)}, u32[]{:S(2)}, u32[]{:S(2)}) collective-permute-start(f32[192,128]{1,0:T(8,128)} %get-tuple-element.51), channel_id=1, source_target_pairs={{0,1},{1,2},{2,3},{3,4},{4,5},{5,6},{6,7},{8,9},{9,10},{10,11},{11... | collective-permute-start | bytes 294920 | tf_op jit(solution)/shard_map/ppermute | solution.py:418
  75.4 1.3 collective-permute-start.7
  76.7 0.0 copy-done.4
  76.7 0.0 all-to-all-done.1
  76.7 1.2 shard_map.143
  77.9 0.0 copy-start.3
  77.9 0.0 collective-permute-done.4.below_x
  77.9 0.0 collective-permute-done.5.above_x
  77.9 0.0 collective-permute-done.6.below_y
  78.0 18.9 %collective-permute-done.7.above_y = f32[192,128]{1,0:T(8,128)S(1)} collective-permute-done((f32[192,128]{1,0:T(8,128)}, f32[192,128]{1,0:T(8,128)S(1)}, u32[]{:S(2)}, u32[]{:S(2)}) %collective-permute-start.7) | collective-permute-done | bytes 98336 | tf_op jit(solution)/shard_map/ppermute | solution.py:418
  96.9 0.2 shard_map.145
  97.1 23.2 %all_to_all.21.line = f32[16,1,128]{2,1,0:T(1,128)S(1)} all-to-all(f32[16,1,128]{2,1,0:T(1,128)S(1)} %shard_map.145), channel_id=1, replica_groups=mesh['zl'=8,'x'=4,'c'=2,'y'=4,'zh'=2] {'zh','zl'}, dimensions={0} | all-to-all | bytes 16384 | tf_op jit(solution)/shard_map/all_to_all | solution.py:412
  120.3 0.6 shard_map.146
  120.9 8.9 %all-to-all-start.3 = ((f32[32,1,128]{2,1,0:T(1,128)}), f32[32,1,128]{2,1,0:T(1,128)S(1)}, u32[]{:S(2)}, u32[]{:S(2)}) async-start(f32[32,1,128]{2,1,0:T(1,128)} %shard_map.146), calls=%async_computation.3 | async-start | bytes 32768 | tf_op jit(solution)/shard_map/all_to_all | solution.py:412
  129.8 0.0 copy-done.3
  129.8 1.0 shard_map.144
  130.8 0.3 shard_map.147
  131.1 5.6 %all-to-all-done.3 = f32[32,1,128]{2,1,0:T(1,128)S(1)} async-done(((f32[32,1,128]{2,1,0:T(1,128)}), f32[32,1,128]{2,1,0:T(1,128)S(1)}, u32[]{:S(2)}, u32[]{:S(2)}) %all-to-all-start.3) | async-done | bytes 16416 | tf_op jit(solution)/shard_map/all_to_all | solution.py:412
  136.7 0.9 shard_map.148
  (1 shorter events, 0.0 us)
Async XLA Ops:
  0.6 24.3 %copy-start.1 = (f32[4,8,8,3,128]{4,2,3,1,0:T(8,128)S(1)}, f32[4,8,8,3,128]{4,2,3,1,0:T(8,128)}, u32[]{:S(2)}) copy-start(f32[4,8,8,3,128]{4,2,3,1,0:T(8,128)} %param.12) | copy-start | bytes 1179652
  1.8 26.8 %collective-permute-start = (f32[4,3,8,128]{3,2,1,0:T(8,128)S(1)}, f32[4,3,8,128]{3,2,1,0:T(8,128)S(1)}, u32[]{:S(2)}, u32[]{:S(2)}) collective-permute-start(f32[4,3,8,128]{3,2,1,0:T(8,128)S(1)} %get-tuple-element.32), channel_id=1, source_target_pairs={{0,8},{8,16},{16,24},{24,32},{32,40},{40,48},{48,56},{56,64},{64,7... | collective-permute-start | bytes 147464 | tf_op jit(solution)/shard_map/ppermute | solution.py:418
  6.3 22.3 %collective-permute-start.1 = (f32[4,3,8,128]{3,2,1,0:T(8,128)S(1)}, f32[4,3,8,128]{3,2,1,0:T(8,128)S(1)}, u32[]{:S(2)}, u32[]{:S(2)}) collective-permute-start(f32[4,3,8,128]{3,2,1,0:T(8,128)S(1)} %get-tuple-element.33), channel_id=1, source_target_pairs={{8,0},{16,8},{24,16},{32,24},{40,32},{48,40},{56,48},{64,56},{72,6... | collective-permute-start | bytes 147464 | tf_op jit(solution)/shard_map/ppermute | solution.py:418
  11.8 16.8 %collective-permute-start.2 = (f32[96,128]{1,0:T(8,128)S(1)}, f32[96,128]{1,0:T(8,128)S(1)}, u32[]{:S(2)}, u32[]{:S(2)}) collective-permute-start(f32[96,128]{1,0:T(8,128)S(1)} %get-tuple-element.34), channel_id=1, source_target_pairs={{0,1},{1,2},{2,3},{3,4},{4,5},{5,6},{6,7},{8,9},{9,10},{10,11},{11... | collective-permute-start | bytes 147464 | tf_op jit(solution)/shard_map/ppermute | solution.py:418
  23.7 14.1 %collective-permute-start.3 = (f32[96,128]{1,0:T(8,128)S(1)}, f32[96,128]{1,0:T(8,128)S(1)}, u32[]{:S(2)}, u32[]{:S(2)}) collective-permute-start(f32[96,128]{1,0:T(8,128)S(1)} %get-tuple-element.35), channel_id=1, source_target_pairs={{1,0},{2,1},{3,2},{4,3},{5,4},{6,5},{7,6},{9,8},{10,9},{11,10},{12... | collective-permute-start | bytes 147464 | tf_op jit(solution)/shard_map/ppermute | solution.py:418
  25.0 12.8 %copy-start = (f32[4,8,8,3,128]{4,2,3,1,0:T(8,128)S(1)}, f32[4,8,8,3,128]{4,2,3,1,0:T(8,128)}, u32[]{:S(2)}) copy-start(f32[4,8,8,3,128]{4,2,3,1,0:T(8,128)} %param.13) | copy-start | bytes 1179652
  25.0 12.8 %copy-start.2 = (f32[4,8,8,128]{3,2,1,0:T(8,128)S(1)}, f32[4,8,8,128]{3,2,1,0:T(8,128)}, u32[]{:S(2)}) copy-start(f32[4,8,8,128]{3,2,1,0:T(8,128)} %basis.3) | copy-start | bytes 393220
  25.0 12.8 %copy-start.5 = (f32[8,8,128]{2,1,0:T(8,128)S(1)}, f32[8,8,128]{2,1,0:T(8,128)}, u32[]{:S(2)}) copy-start(f32[8,8,128]{2,1,0:T(8,128)} %stiffness.1) | copy-start | bytes 98308
  25.0 12.7 %copy-start.6 = (f32[8,8,128]{2,1,0:T(8,128)S(1)}, f32[8,8,128]{2,1,0:T(8,128)}, u32[]{:S(2)}) copy-start(f32[8,8,128]{2,1,0:T(8,128)} %coupling.1) | copy-start | bytes 98308
  56.5 20.2 %copy-start.4 = (f32[1,1,12,6144]{3,1,2,0:T(1,128)S(1)}, f32[1,1,12,6144]{3,1,2,0:T(1,128)}, u32[]{:S(2)}) copy-start(f32[1,1,12,6144]{3,1,2,0:T(1,128)} %param.20) | copy-start | bytes 884740
  56.5 20.2 %all-to-all-start.1 = ((f32[32,16,128]{2,1,0:T(8,128)}), f32[32,16,128]{2,1,0:T(8,128)S(1)}, u32[]{:S(2)}, u32[]{:S(2)}) async-start(f32[32,16,128]{2,1,0:T(8,128)} %shard_map.141), calls=%async_computation.1 | async-start | bytes 524288 | tf_op jit(solution)/shard_map/all_to_all | solution.py:412
  67.7 10.3 %collective-permute-start.4 = (f32[8,3,8,128]{3,2,1,0:T(8,128)}, f32[8,3,8,128]{3,2,1,0:T(8,128)S(1)}, u32[]{:S(2)}, u32[]{:S(2)}) collective-permute-start(f32[8,3,8,128]{3,2,1,0:T(8,128)} %get-tuple-element.49), channel_id=1, source_target_pairs={{0,8},{8,16},{16,24},{24,32},{32,40},{40,48},{48,56},{56,64},{64,7... | collective-permute-start | bytes 294920 | tf_op jit(solution)/shard_map/ppermute | solution.py:418
  71.2 6.7 %collective-permute-start.5 = (f32[8,3,8,128]{3,2,1,0:T(8,128)}, f32[8,3,8,128]{3,2,1,0:T(8,128)S(1)}, u32[]{:S(2)}, u32[]{:S(2)}) collective-permute-start(f32[8,3,8,128]{3,2,1,0:T(8,128)} %get-tuple-element.50), channel_id=1, source_target_pairs={{8,0},{16,8},{24,16},{32,24},{40,32},{48,40},{56,48},{64,56},{72,6... | collective-permute-start | bytes 294920 | tf_op jit(solution)/shard_map/ppermute | solution.py:418
  73.1 4.8 %collective-permute-start.6 = (f32[192,128]{1,0:T(8,128)}, f32[192,128]{1,0:T(8,128)S(1)}, u32[]{:S(2)}, u32[]{:S(2)}) collective-permute-start(f32[192,128]{1,0:T(8,128)} %get-tuple-element.51), channel_id=1, source_target_pairs={{0,1},{1,2},{2,3},{3,4},{4,5},{5,6},{6,7},{8,9},{9,10},{10,11},{11... | collective-permute-start | bytes 294920 | tf_op jit(solution)/shard_map/ppermute | solution.py:418
  75.4 21.5 %collective-permute-start.7 = (f32[192,128]{1,0:T(8,128)}, f32[192,128]{1,0:T(8,128)S(1)}, u32[]{:S(2)}, u32[]{:S(2)}) collective-permute-start(f32[192,128]{1,0:T(8,128)} %get-tuple-element.52), channel_id=1, source_target_pairs={{1,0},{2,1},{3,2},{4,3},{5,4},{6,5},{7,6},{9,8},{10,9},{11,10},{12... | collective-permute-start | bytes 294920 | tf_op jit(solution)/shard_map/ppermute | solution.py:418
  77.9 51.9 %copy-start.3 = (f32[4,8,8,3,128]{4,2,3,1,0:T(8,128)S(1)}, f32[4,8,8,3,128]{4,2,3,1,0:T(8,128)}, u32[]{:S(2)}) copy-start(f32[4,8,8,3,128]{4,2,3,1,0:T(8,128)} %param.11) | copy-start | bytes 1179652
  120.9 15.8 %all-to-all-start.3 = ((f32[32,1,128]{2,1,0:T(1,128)}), f32[32,1,128]{2,1,0:T(1,128)S(1)}, u32[]{:S(2)}, u32[]{:S(2)}) async-start(f32[32,1,128]{2,1,0:T(1,128)} %shard_map.146), calls=%async_computation.3 | async-start | bytes 32768 | tf_op jit(solution)/shard_map/all_to_all | solution.py:412

commit v6 on v5

--- a/solution.py
+++ b/solution.py
@@ -352,10 +352,8 @@
 
 
 def precondition_kernel(
-    steps, coarse, basis, direction, solved_r, solved_w, below_x, above_x, below_y, above_y,
-    preconditioned, held,
-):
-    held[...] = direction[...]
+    steps, coarse, basis, solved_r, solved_w, below_x, above_x, below_y, above_y, preconditioned
+):
     y_at = lax.broadcasted_iota(jnp.int32, (NY, NZ), 0)
     for c in range(CASES):
         step = steps[c : c + 1, :]
@@ -370,25 +368,50 @@
                 preconditioned[c, x, k] = out
 
 
-def final_kernel(prior, parts, preconditioned, direction, direction_next, inner):
+def final_kernel(
+    prior, parts, preconditioned_hbm, direction_hbm, direction_next_hbm, inner,
+    preconditioned, direction, direction_next, in_sems, out_sems,
+):
+    copies_in, copies_out = [], []
+    for c in range(CASES):
+        copies_in.append(
+            (
+                pltpu.make_async_copy(
+                    preconditioned_hbm.at[c], preconditioned.at[c], in_sems.at[0, c]
+                ),
+                pltpu.make_async_copy(direction_hbm.at[c], direction.at[c], in_sems.at[1, c]),
+            )
+        )
+        copies_out.append(
+            pltpu.make_async_copy(direction_next.at[c], direction_next_hbm.at[c], out_sems.at[c])
+        )
+        for copy in copies_in[c]:
+            copy.start()
     total = jnp.sum(parts[...], axis=0, keepdims=True)
     inner[...] = total[0, :CASES]
     lane = lax.broadcasted_iota(jnp.int32, (1, 128), 1)
+    growth = []
     for c in range(CASES):
         mine = jnp.sum(jnp.where(lane == c, total, 0.0), axis=1, keepdims=True)
-        growth = jnp.broadcast_to(mine, (1, NZ)) / prior[c : c + 1, :]
+        growth.append(jnp.broadcast_to(mine, (1, NZ)) / prior[c : c + 1, :])
+    for c in range(CASES):
+        for copy in copies_in[c]:
+            copy.wait()
         for x in range(NX):
             for k in range(COMP):
                 direction_next[c, x, k] = (
-                    preconditioned[c, x, k] + growth * direction[c, x, k]
+                    preconditioned[c, x, k] + growth[c] * direction[c, x, k]
                 )
+        copies_out[c].start()
+    for copy in copies_out:
+        copy.wait()
 
 
 VMEM = pl.BlockSpec(memory_space=pltpu.VMEM)
 HBM = pl.BlockSpec(memory_space=pltpu.HBM)
 
 
-def local_call(body, outs, spaces, *args, scratch=()):
+def local_call(body, outs, spaces, *args, scratch=(), results=""):
     specs = [{"v": VMEM, "h": HBM}[space] for space in spaces]
     specs += [VMEM] * (len(args) - len(specs))
     args = tuple(
@@ -402,7 +425,7 @@
             for shape in outs
         ],
         in_specs=specs,
-        out_specs=[VMEM] * len(outs),
+        out_specs=[HBM if space == "h" else VMEM for space in results.ljust(len(outs), "v")],
         scratch_shapes=list(scratch),
         compiler_params=pltpu.CompilerParams(vmem_limit_bytes=20 << 20),
     )(*args)
@@ -482,13 +505,16 @@
     )
     (rows,) = local_call(fold_kernel, [(N_PLANE, 1, 128)], "", line)
     parts = exchange(rows, PLANE)
-    preconditioned, held = local_call(
-        precondition_kernel, [FIELD, FIELD], "",
-        steps, coarse, coarse_basis, direction, solved_r, solved_w, *halo,
+    (preconditioned,) = local_call(
+        precondition_kernel, [FIELD], "",
+        steps, coarse, coarse_basis, solved_r, solved_w, *halo,
     )
     direction_next, inner = local_call(
-        final_kernel, [FIELD, (CASES,)], "",
-        prior_rows, parts.reshape(N_PLANE, 128), preconditioned, held,
+        final_kernel, [FIELD, (CASES,)], "vvhh",
+        prior_rows, parts.reshape(N_PLANE, 128), preconditioned, direction,
+        scratch=[pltpu.VMEM(FIELD, f32)] * 3
+        + [pltpu.SemaphoreType.DMA((2, CASES)), pltpu.SemaphoreType.DMA((CASES,))],
+        results="hv",
     )
     solution_next, residual_next, direction_next = (
         a.transpose(0, 1, 3, 2, 4) for a in (solution_next, residual_next, direction_next)

time: 138 us -> 140 us (1.014)
  Pallas kernels: 11.4 us -> 13 us
    pallas_call x11, Pallas kernels: 11.4 us -> 13 us  [local_call(): pl.pallas_call(body, out_shape=[shape if hasattr(shape, 'dtype') else jax...]
where the time goes in v6:
time: 140 us; the launch traced here: 139 us
  starting transfers between devices  52.2 us (37%)
  blocking collectives  39.4 us (28%)
  waiting for transfers between devices  32.9 us (24%)
  Pallas kernels  13 us (9%)
    all_to_all x2, blocking collectives, exchange(): return lax.all_to_all(rows, axes, 0, 0, tiled=True)  39.4 us
    ppermute x8, starting transfers between devices, neighbours(): return (lax.ppermute(high, axes, up), lax.ppermute(low, axes, down))  32.2 us
    ppermute x8, waiting for transfers between devices, neighbours(): return (lax.ppermute(high, axes, up), lax.ppermute(low, axes, down))  28 us
    all_to_all x2, starting transfers between devices, exchange(): return lax.all_to_all(rows, axes, 0, 0, tiled=True)  20 us
    pallas_call x11, Pallas kernels, local_call(): pl.pallas_call(body, out_shape=[shape if hasattr(shape, 'dtype') else jax...  13 us
    all_to_all x2, waiting for transfers between devices, exchange(): return lax.all_to_all(rows, axes, 0, 0, tiled=True)  4.88 us
  transfers between devices with their start and end apart: 10, of which 3 were waited for; matrix products, arithmetic and copies ran while one was open for 0% of the time, Pallas kernels for 4%

profile of v6, /device:TPU:1, one launch (start us, length us, event | category | flops | bytes accessed | tf_op | source)
XLA Modules:
  0.0 139.1 jit_solution(14717417418150783994)
XLA Ops:
  0.6 0.0 copy-start.1
  0.6 1.1 shard_map.139
  1.8 4.5 %collective-permute-start = (f32[4,3,8,128]{3,2,1,0:T(8,128)S(1)}, f32[4,3,8,128]{3,2,1,0:T(8,128)S(1)}, u32[]{:S(2)}, u32[]{:S(2)}) collective-permute-start(f32[4,3,8,128]{3,2,1,0:T(8,128)S(1)} %get-tuple-element.30), channel_id=1, source_target_pairs={{0,8},{8,16},{16,24},{24,32},{32,40},{40,48},{48,56},{56,64},{64,7... | collective-permute-start | bytes 147464 | tf_op jit(solution)/shard_map/ppermute | solution.py:441
  6.3 5.5 %collective-permute-start.1 = (f32[4,3,8,128]{3,2,1,0:T(8,128)S(1)}, f32[4,3,8,128]{3,2,1,0:T(8,128)S(1)}, u32[]{:S(2)}, u32[]{:S(2)}) collective-permute-start(f32[4,3,8,128]{3,2,1,0:T(8,128)S(1)} %get-tuple-element.31), channel_id=1, source_target_pairs={{8,0},{16,8},{24,16},{32,24},{40,32},{48,40},{56,48},{64,56},{72,6... | collective-permute-start | bytes 147464 | tf_op jit(solution)/shard_map/ppermute | solution.py:441
  11.8 11.8 %collective-permute-start.2 = (f32[96,128]{1,0:T(8,128)S(1)}, f32[96,128]{1,0:T(8,128)S(1)}, u32[]{:S(2)}, u32[]{:S(2)}) collective-permute-start(f32[96,128]{1,0:T(8,128)S(1)} %get-tuple-element.32), channel_id=1, source_target_pairs={{0,1},{1,2},{2,3},{3,4},{4,5},{5,6},{6,7},{8,9},{9,10},{10,11},{11... | collective-permute-start | bytes 147464 | tf_op jit(solution)/shard_map/ppermute | solution.py:441
  23.7 1.3 collective-permute-start.3
  25.0 0.0 copy-done.1
  25.0 0.0 copy-start
  25.0 0.0 copy-start.3
  25.0 0.0 copy-start.6
  25.0 0.0 copy-start.7
  25.0 3.6 %shard_map.138 = (bf16[768,384]{1,0:T(8,128)(2,1)S(1)}, f32[4,8,3,8,128]{4,3,2,1,0:T(8,128)S(1)}, f32[48,128]{1,0:T(8,128)S(1)}, f32[4,128]{1,0:T(4,128)S(1)}) custom-call(f32[4,8,3,8,128]{4,3,2,1,0:T(8,128)S(1)} %bitcast.18, f32[384,384]{1,0:T(8,128)} %bitcast.26, f32[384,384]{1,0:T(8,128)} %bitcast.27, s32[1,384]{1,0:T(1,128)} %bitcast.28, ...), custom_call_target="tpu_custom_call" | custom-call | tf_op jit(solution)/shard_map/pallas_call | solution.py:421
  28.6 0.0 collective-permute-done.below_x
  28.6 0.0 collective-permute-done.1.above_x
  28.6 0.0 collective-permute-done.2.below_y
  28.7 9.1 %collective-permute-done.3.above_y = f32[96,128]{1,0:T(8,128)S(1)} collective-permute-done((f32[96,128]{1,0:T(8,128)S(1)}, f32[96,128]{1,0:T(8,128)S(1)}, u32[]{:S(2)}, u32[]{:S(2)}) %collective-permute-start.3) | collective-permute-done | bytes 49184 | tf_op jit(solution)/shard_map/ppermute | solution.py:441
  37.8 0.0 copy-done
  37.8 0.0 copy-done.3
  37.8 0.0 copy-done.6
  37.8 0.0 copy-done.7
  37.8 1.8 %shard_map.140 = (f32[4,8,3,8,128]{4,3,2,1,0:T(8,128)S(1)}, f32[4,8,3,8,128]{4,3,2,1,0:T(8,128)S(1)}, f32[48,128]{1,0:T(8,128)S(1)}, f32[16,1,128]{2,1,0:T(1,128...) custom-call(f32[4,8,3,8,128]{4,3,2,1,0:T(8,128)S(1)} %bitcast.16, ...), custom_call_target="tpu_custom_call" | custom-call | tf_op jit(solution)/shard_map/pallas_call | solution.py:421
  39.6 16.2 %all_to_all.20 = f32[16,1,128]{2,1,0:T(1,128)S(1)} all-to-all(f32[16,1,128]{2,1,0:T(1,128)S(1)} %get-tuple-element.37), channel_id=1, replica_groups=mesh['zl'=8,'x'=4,'c'=2,'y'=4,'zh'=2] {'zh','zl'}, dimensions={0} | all-to-all | bytes 16384 | tf_op jit(solution)/shard_map/all_to_all | solution.py:435
  55.8 0.7 shard_map.141
  56.5 0.0 copy-start.5
  56.5 11.1 %all-to-all-start.1 = ((f32[32,16,128]{2,1,0:T(8,128)}), f32[32,16,128]{2,1,0:T(8,128)S(1)}, u32[]{:S(2)}, u32[]{:S(2)}) async-start(f32[32,16,128]{2,1,0:T(8,128)} %shard_map.141), calls=%async_computation.1 | async-start | bytes 524288 | tf_op jit(solution)/shard_map/all_to_all | solution.py:435
  67.7 3.5 %collective-permute-start.4 = (f32[8,3,8,128]{3,2,1,0:T(8,128)}, f32[8,3,8,128]{3,2,1,0:T(8,128)S(1)}, u32[]{:S(2)}, u32[]{:S(2)}) collective-permute-start(f32[8,3,8,128]{3,2,1,0:T(8,128)} %get-tuple-element.47), channel_id=1, source_target_pairs={{0,8},{8,16},{16,24},{24,32},{32,40},{40,48},{48,56},{56,64},{64,7... | collective-permute-start | bytes 294920 | tf_op jit(solution)/shard_map/ppermute | solution.py:441
  71.2 1.9 %collective-permute-start.5 = (f32[8,3,8,128]{3,2,1,0:T(8,128)}, f32[8,3,8,128]{3,2,1,0:T(8,128)S(1)}, u32[]{:S(2)}, u32[]{:S(2)}) collective-permute-start(f32[8,3,8,128]{3,2,1,0:T(8,128)} %get-tuple-element.48), channel_id=1, source_target_pairs={{8,0},{16,8},{24,16},{32,24},{40,32},{48,40},{56,48},{64,56},{72,6... | collective-permute-start | bytes 294920 | tf_op jit(solution)/shard_map/ppermute | solution.py:441
  73.1 2.3 %collective-permute-start.6 = (f32[192,128]{1,0:T(8,128)}, f32[192,128]{1,0:T(8,128)S(1)}, u32[]{:S(2)}, u32[]{:S(2)}) collective-permute-start(f32[192,128]{1,0:T(8,128)} %get-tuple-element.49), channel_id=1, source_target_pairs={{0,1},{1,2},{2,3},{3,4},{4,5},{5,6},{6,7},{8,9},{9,10},{10,11},{11... | collective-permute-start | bytes 294920 | tf_op jit(solution)/shard_map/ppermute | solution.py:441
  75.4 1.3 collective-permute-start.7
  76.7 0.0 copy-done.5
  76.7 0.0 all-to-all-done.1
  76.7 1.2 shard_map.143
  77.9 0.0 copy-start.4
  77.9 0.0 collective-permute-done.4.below_x
  77.9 0.0 collective-permute-done.5.above_x
  77.9 0.0 collective-permute-done.6.below_y
  78.0 18.9 %collective-permute-done.7.above_y = f32[192,128]{1,0:T(8,128)S(1)} collective-permute-done((f32[192,128]{1,0:T(8,128)}, f32[192,128]{1,0:T(8,128)S(1)}, u32[]{:S(2)}, u32[]{:S(2)}) %collective-permute-start.7) | collective-permute-done | bytes 98336 | tf_op jit(solution)/shard_map/ppermute | solution.py:441
  96.9 0.2 shard_map.145
  97.1 23.2 %all_to_all.21.line = f32[16,1,128]{2,1,0:T(1,128)S(1)} all-to-all(f32[16,1,128]{2,1,0:T(1,128)S(1)} %shard_map.145), channel_id=1, replica_groups=mesh['zl'=8,'x'=4,'c'=2,'y'=4,'zh'=2] {'zh','zl'}, dimensions={0} | all-to-all | bytes 16384 | tf_op jit(solution)/shard_map/all_to_all | solution.py:435
  120.3 0.6 shard_map.146
  120.9 8.9 %all-to-all-start.3 = ((f32[32,1,128]{2,1,0:T(1,128)}), f32[32,1,128]{2,1,0:T(1,128)S(1)}, u32[]{:S(2)}, u32[]{:S(2)}) async-start(f32[32,1,128]{2,1,0:T(1,128)} %shard_map.146), calls=%async_computation.3 | async-start | bytes 32768 | tf_op jit(solution)/shard_map/all_to_all | solution.py:435
  129.8 0.0 copy-done.4
  129.8 1.0 shard_map.144
  130.8 0.3 shard_map.147.preconditioned_hbm
  131.0 0.0 copy-start.2
  131.0 0.7 copy-done.2
  131.8 4.9 %all-to-all-done.3 = f32[32,1,128]{2,1,0:T(1,128)S(1)} async-done(((f32[32,1,128]{2,1,0:T(1,128)}), f32[32,1,128]{2,1,0:T(1,128)S(1)}, u32[]{:S(2)}, u32[]{:S(2)}) %all-to-all-start.3) | async-done | bytes 16416 | tf_op jit(solution)/shard_map/all_to_all | solution.py:435
  136.7 2.5 %shard_map.148 = (f32[4,8,3,8,128]{4,3,2,1,0:T(8,128)}, f32[4]{0:T(128)}) custom-call(f32[4,128]{1,0:T(4,128)S(1)} %get-tuple-element.29.prior, f32[32,128]{1,0:T(8,128)S(1)} %bitcast.24, f32[4,8,3,8,128]{4,3,2,1,0:T(8,128)} %copy-done.2, f32[4,8,3,8,128]{4,3,2,1,0:T(8,128)} %bitcast.15), custom_call_target="tpu_custom_call" | custom-call | tf_op jit(solution)/shard_map/pallas_call | solution.py:421
  (1 shorter events, 0.0 us)
Async XLA Ops:
  0.6 24.3 %copy-start.1 = (f32[4,8,8,3,128]{4,2,3,1,0:T(8,128)S(1)}, f32[4,8,8,3,128]{4,2,3,1,0:T(8,128)}, u32[]{:S(2)}) copy-start(f32[4,8,8,3,128]{4,2,3,1,0:T(8,128)} %param.12) | copy-start | bytes 1179652
  1.8 26.8 %collective-permute-start = (f32[4,3,8,128]{3,2,1,0:T(8,128)S(1)}, f32[4,3,8,128]{3,2,1,0:T(8,128)S(1)}, u32[]{:S(2)}, u32[]{:S(2)}) collective-permute-start(f32[4,3,8,128]{3,2,1,0:T(8,128)S(1)} %get-tuple-element.30), channel_id=1, source_target_pairs={{0,8},{8,16},{16,24},{24,32},{32,40},{40,48},{48,56},{56,64},{64,7... | collective-permute-start | bytes 147464 | tf_op jit(solution)/shard_map/ppermute | solution.py:441
  6.3 22.3 %collective-permute-start.1 = (f32[4,3,8,128]{3,2,1,0:T(8,128)S(1)}, f32[4,3,8,128]{3,2,1,0:T(8,128)S(1)}, u32[]{:S(2)}, u32[]{:S(2)}) collective-permute-start(f32[4,3,8,128]{3,2,1,0:T(8,128)S(1)} %get-tuple-element.31), channel_id=1, source_target_pairs={{8,0},{16,8},{24,16},{32,24},{40,32},{48,40},{56,48},{64,56},{72,6... | collective-permute-start | bytes 147464 | tf_op jit(solution)/shard_map/ppermute | solution.py:441
  11.8 16.8 %collective-permute-start.2 = (f32[96,128]{1,0:T(8,128)S(1)}, f32[96,128]{1,0:T(8,128)S(1)}, u32[]{:S(2)}, u32[]{:S(2)}) collective-permute-start(f32[96,128]{1,0:T(8,128)S(1)} %get-tuple-element.32), channel_id=1, source_target_pairs={{0,1},{1,2},{2,3},{3,4},{4,5},{5,6},{6,7},{8,9},{9,10},{10,11},{11... | collective-permute-start | bytes 147464 | tf_op jit(solution)/shard_map/ppermute | solution.py:441
  23.7 14.1 %collective-permute-start.3 = (f32[96,128]{1,0:T(8,128)S(1)}, f32[96,128]{1,0:T(8,128)S(1)}, u32[]{:S(2)}, u32[]{:S(2)}) collective-permute-start(f32[96,128]{1,0:T(8,128)S(1)} %get-tuple-element.33), channel_id=1, source_target_pairs={{1,0},{2,1},{3,2},{4,3},{5,4},{6,5},{7,6},{9,8},{10,9},{11,10},{12... | collective-permute-start | bytes 147464 | tf_op jit(solution)/shard_map/ppermute | solution.py:441
  25.0 12.8 %copy-start = (f32[4,8,8,3,128]{4,2,3,1,0:T(8,128)S(1)}, f32[4,8,8,3,128]{4,2,3,1,0:T(8,128)}, u32[]{:S(2)}) copy-start(f32[4,8,8,3,128]{4,2,3,1,0:T(8,128)} %param.13) | copy-start | bytes 1179652
  25.0 12.8 %copy-start.3 = (f32[4,8,8,128]{3,2,1,0:T(8,128)S(1)}, f32[4,8,8,128]{3,2,1,0:T(8,128)}, u32[]{:S(2)}) copy-start(f32[4,8,8,128]{3,2,1,0:T(8,128)} %basis.3) | copy-start | bytes 393220
  25.0 12.8 %copy-start.6 = (f32[8,8,128]{2,1,0:T(8,128)S(1)}, f32[8,8,128]{2,1,0:T(8,128)}, u32[]{:S(2)}) copy-start(f32[8,8,128]{2,1,0:T(8,128)} %stiffness.1) | copy-start | bytes 98308
  25.0 12.7 %copy-start.7 = (f32[8,8,128]{2,1,0:T(8,128)S(1)}, f32[8,8,128]{2,1,0:T(8,128)}, u32[]{:S(2)}) copy-start(f32[8,8,128]{2,1,0:T(8,128)} %coupling.1) | copy-start | bytes 98308
  56.5 20.2 %copy-start.5 = (f32[1,1,12,6144]{3,1,2,0:T(1,128)S(1)}, f32[1,1,12,6144]{3,1,2,0:T(1,128)}, u32[]{:S(2)}) copy-start(f32[1,1,12,6144]{3,1,2,0:T(1,128)} %param.20) | copy-start | bytes 884740
  56.5 20.2 %all-to-all-start.1 = ((f32[32,16,128]{2,1,0:T(8,128)}), f32[32,16,128]{2,1,0:T(8,128)S(1)}, u32[]{:S(2)}, u32[]{:S(2)}) async-start(f32[32,16,128]{2,1,0:T(8,128)} %shard_map.141), calls=%async_computation.1 | async-start | bytes 524288 | tf_op jit(solution)/shard_map/all_to_all | solution.py:435
  67.7 10.3 %collective-permute-start.4 = (f32[8,3,8,128]{3,2,1,0:T(8,128)}, f32[8,3,8,128]{3,2,1,0:T(8,128)S(1)}, u32[]{:S(2)}, u32[]{:S(2)}) collective-permute-start(f32[8,3,8,128]{3,2,1,0:T(8,128)} %get-tuple-element.47), channel_id=1, source_target_pairs={{0,8},{8,16},{16,24},{24,32},{32,40},{40,48},{48,56},{56,64},{64,7... | collective-permute-start | bytes 294920 | tf_op jit(solution)/shard_map/ppermute | solution.py:441
  71.2 6.7 %collective-permute-start.5 = (f32[8,3,8,128]{3,2,1,0:T(8,128)}, f32[8,3,8,128]{3,2,1,0:T(8,128)S(1)}, u32[]{:S(2)}, u32[]{:S(2)}) collective-permute-start(f32[8,3,8,128]{3,2,1,0:T(8,128)} %get-tuple-element.48), channel_id=1, source_target_pairs={{8,0},{16,8},{24,16},{32,24},{40,32},{48,40},{56,48},{64,56},{72,6... | collective-permute-start | bytes 294920 | tf_op jit(solution)/shard_map/ppermute | solution.py:441
  73.1 4.8 %collective-permute-start.6 = (f32[192,128]{1,0:T(8,128)}, f32[192,128]{1,0:T(8,128)S(1)}, u32[]{:S(2)}, u32[]{:S(2)}) collective-permute-start(f32[192,128]{1,0:T(8,128)} %get-tuple-element.49), channel_id=1, source_target_pairs={{0,1},{1,2},{2,3},{3,4},{4,5},{5,6},{6,7},{8,9},{9,10},{10,11},{11... | collective-permute-start | bytes 294920 | tf_op jit(solution)/shard_map/ppermute | solution.py:441
  75.4 21.5 %collective-permute-start.7 = (f32[192,128]{1,0:T(8,128)}, f32[192,128]{1,0:T(8,128)S(1)}, u32[]{:S(2)}, u32[]{:S(2)}) collective-permute-start(f32[192,128]{1,0:T(8,128)} %get-tuple-element.50), channel_id=1, source_target_pairs={{1,0},{2,1},{3,2},{4,3},{5,4},{6,5},{7,6},{9,8},{10,9},{11,10},{12... | collective-permute-start | bytes 294920 | tf_op jit(solution)/shard_map/ppermute | solution.py:441
  77.9 51.9 %copy-start.4 = (f32[4,8,8,3,128]{4,2,3,1,0:T(8,128)S(1)}, f32[4,8,8,3,128]{4,2,3,1,0:T(8,128)}, u32[]{:S(2)}) copy-start(f32[4,8,8,3,128]{4,2,3,1,0:T(8,128)} %param.11) | copy-start | bytes 1179652
  120.9 15.8 %all-to-all-start.3 = ((f32[32,1,128]{2,1,0:T(1,128)}), f32[32,1,128]{2,1,0:T(1,128)S(1)}, u32[]{:S(2)}, u32[]{:S(2)}) async-start(f32[32,1,128]{2,1,0:T(1,128)} %shard_map.146), calls=%async_computation.3 | async-start | bytes 32768 | tf_op jit(solution)/shard_map/all_to_all | solution.py:435
  131.0 0.7 copy-start.2
